TPU v7x, 512 devices: a whole 4x4x16 slice. The times are simulated.
512 devices in a mesh: seq: 64 (over z, y), exp: 8 (over x, core).
Axes of the slice: x: 4, y: 4, z: 16, core: 2. Of those that a mesh axis runs over, the one named last changes fastest.
Arguments:
- queries: bfloat16 [16384, 6144], P('seq', 'exp'), may hold values from -6 to 6
- keys: bfloat16 [16384, 6144], P('seq', 'exp'), may hold values from -6 to 6
- values: bfloat16 [16384, 6144], P('seq', 'exp'), may hold values from -6 to 6
- selections: int32 [64, 8, 5], P('seq'), may hold values from 0 to 255
- router: bfloat16 [6144, 8], P(None, 'exp'), may hold values from -0.0390625 to 0.0390625
- w_up: bfloat16 [8, 9216, 6144], P('exp', 'seq'), may hold values from -0.15625 to 0.15625
- w_down: bfloat16 [8, 6144, 9216], P('exp', 'seq'), may hold values from -0.125 to 0.125
Outputs:
- layer_out: bfloat16 [16384, 6144], P('seq', 'exp')
Inputs may be any that keep to these rules, and one draw needn't show every extreme that they name: `selections`: entries are positions inside the block of 256 tokens; different experts may pick the same token and an expert may pick a token twice.
All inputs are finite; a program needn't handle non-finite values.
Results may differ from a plain program's by a relative error of at most 0.018.
Values may be sent and summed in bfloat16 or wider, within the bound.
No kernel may reach another device: no remote copies, remote signals or barrier semaphores. Data moves between devices by JAX's collectives and lax.ppermute only.
A program may use at most 128 MiB of HBM per device.

v0:
```python
import jax
import jax.numpy as jnp
from jax import lax
from jax.sharding import PartitionSpec as P

HEAD = 96


def entering(array, axis, join, neutral):
    place = lax.axis_index(axis)
    gathered = lax.all_gather(array.astype(jnp.bfloat16), axis)
    state = jnp.zeros_like(array) + jnp.asarray(neutral, array.dtype)

    def one(lap, state):
        return join(state, lax.dynamic_index_in_dim(gathered, lap, 0, False).astype(array.dtype))

    return lax.fori_loop(0, place, one, state)


def body(queries, keys, values, selections, router, w_up, w_down):
    length = queries.shape[0]
    width = queries.shape[1]
    heads_here = width // HEAD
    query_heads = queries.reshape(length, heads_here, HEAD)
    key_heads = keys.reshape(length, heads_here, HEAD)
    value_heads = values.reshape(length, heads_here, HEAD)
    state = jnp.einsum(
        "lhd,lhe->hde", key_heads, value_heads, preferred_element_type=jnp.float32
    ).astype(jnp.bfloat16)
    flat_size = heads_here * HEAD * HEAD
    flat_state = state.reshape(1, flat_size).astype(jnp.float32)
    empty_state = jnp.zeros((1, flat_size), jnp.float32)

    def combine_sum(earlier, later):
        return earlier + later

    before = entering(flat_state, "seq", combine_sum, empty_state)
    before = before.astype(jnp.bfloat16).reshape(heads_here, HEAD, HEAD)
    causal = jnp.arange(length)[:, None] >= jnp.arange(length)[None, :]
    scores = jnp.einsum("qhd,khd->hqk", query_heads, key_heads, preferred_element_type=jnp.float32)
    scores = jnp.where(causal[None], scores, 0.0).astype(jnp.bfloat16)
    inner = jnp.einsum("hqk,khe->qhe", scores, value_heads, preferred_element_type=jnp.float32)
    outer = jnp.einsum("qhd,hde->qhe", query_heads, before, preferred_element_type=jnp.float32)
    mixed = inner + outer
    power = jnp.mean(mixed * mixed, axis=-1, keepdims=True)
    attn = (mixed * lax.rsqrt(power + 1e-06)).astype(jnp.bfloat16).reshape(length, width)
    experts = selections.shape[1]
    capacity = selections.shape[2]
    where = selections[0].reshape(-1)
    picked = attn[where].reshape(experts, capacity, width)
    up_matrix = w_up[0]
    down_matrix = w_down[0]
    arrived = lax.all_to_all(picked, "exp", split_axis=0, concat_axis=2, tiled=True)
    own_rows = arrived.reshape(capacity, -1)
    hidden = jax.nn.silu(
        jnp.einsum(
            "rd,fd->rf",
            lax.all_gather(own_rows, "seq", axis=0, tiled=True),
            up_matrix,
            preferred_element_type=jnp.float32,
        )
    ).astype(jnp.bfloat16)
    gate_value = jax.nn.sigmoid(jnp.dot(own_rows, router, preferred_element_type=jnp.float32))
    columns = jnp.einsum(
        "rf,cf->rc",
        lax.all_gather(hidden, "seq", axis=1, tiled=True),
        down_matrix,
        preferred_element_type=jnp.float32,
    )
    expert_out = lax.all_to_all(columns, "seq", split_axis=0, concat_axis=1, tiled=True)
    weighted = (gate_value * expert_out).astype(jnp.bfloat16).reshape(1, capacity, -1)
    back = lax.all_to_all(weighted, "exp", split_axis=2, concat_axis=0, tiled=True)
    placing = (where[None, :] == jnp.arange(length, dtype=jnp.int32)[:, None]).astype(jnp.bfloat16)
    added = jnp.dot(
        placing, back.reshape(experts * capacity, width), preferred_element_type=jnp.float32
    )
    return (attn.astype(jnp.float32) + added).astype(jnp.bfloat16)


def solution(mesh):
    placed = (
        P("seq", "exp"),
        P("seq", "exp"),
        P("seq", "exp"),
        P("seq", None, None),
        P(None, "exp"),
        P("exp", "seq", None),
        P("exp", "seq", None),
    )
    return jax.shard_map(
        body, mesh=mesh, in_specs=placed, out_specs=P("seq", "exp"), check_vma=False
    )
```

profile of v0, /device:TPU:1, one launch (start us, length us, event | category | flops | bytes accessed | tf_op | source)
XLA Modules:
  0.0 761.9 jit_solution(10522953082573374514)
XLA Ops:
  6.5 1.3 copy.44
  7.9 1.2 copy.45
  9.0 0.3 convolution_convert_fusion
  9.3 1.0 all_gather.12
  10.3 0.0 all-gather.5.cloned.1.call-update
  10.3 0.0 all-gather.9.cloned.1.call-start
  10.4 1.2 copy.43
  11.5 0.1 copy.48
  11.6 0.1 reshape_squeeze.3
  11.8 209.9 %all-gather.5.cloned.1.call-done = bf16[64,1,73728]{2,1,0:T(2,128)(2,1)} async-done(((bf16[1,1,73728]{2,1,0:T(2,128)(2,1)}), bf16[64,1,73728]{2,1,0:T(2,128)(2,1)}) %all-gather.5.cloned.1.call-update) | async-done | bytes 9437200 | tf_op jit(solution)/shard_map/all_gather | solution.py:11
  221.7 0.2 broadcast_in_dim.23
  221.9 0.8 convert_reduce_fusion
  222.6 0.2 reshape.138
  222.8 1.2 convolution_bitcast_fusion
  224.0 2.8 multiply_reduce_fusion
  226.8 1.2 multiply_convert_fusion
  228.0 0.2 copy.47
  228.2 0.6 gather_fusion
  228.9 10.2 %all_to_all.46 = bf16[8,5,768]{2,1,0:T(8,128)(2,1)} all-to-all(bf16[8,5,768]{2,1,0:T(8,128)(2,1)S(1)} %reshape.140), channel_id=1, replica_groups=mesh['seq'=64,'exp'=8] {'exp'}, dimensions={0} | all-to-all | bytes 122880 | tf_op jit(solution)/shard_map/all_to_all | solution.py:53
  239.1 0.0 all-gather.9.cloned.1.call-update
  239.1 0.2 all-gather.7.cloned.1.call-start
  239.4 225.6 %all-gather.9.cloned.1.call-done = bf16[64,5,6144]{2,1,0:T(8,128)(2,1)} async-done(((bf16[1,5,6144]{2,1,0:T(8,128)(2,1)}), bf16[64,5,6144]{2,1,0:T(8,128)(2,1)}) %all-gather.9.cloned.1.call-update) | async-done | bytes 3932176 | tf_op jit(solution)/shard_map/all_gather | solution.py:58
  465.0 7.7 %reshape.154 = bf16[320,6144]{1,0:T(8,128)(2,1)} reshape(bf16[64,5,6144]{2,1,0:T(8,128)(2,1)} %all-gather.9.cloned.1.call-done) | data formatting | bytes 7864320
  472.7 4.3 multiply_convert_fusion.1
  477.0 148.1 %all-gather.7.cloned.1.call-done = bf16[320,9216]{0,1:T(8,128)(2,1)} async-done(((bf16[320,144]{0,1:T(8,128)(2,1)}), bf16[320,9216]{0,1:T(8,128)(2,1)}) %all-gather.7.cloned.1.call-update) | async-done | bytes 5898256 | tf_op jit(solution)/shard_map/all_gather | solution.py:66
  625.1 9.3 %copy.51 = bf16[320,9216]{1,0:T(8,128)(2,1)} copy(bf16[320,9216]{0,1:T(8,128)(2,1)} %all-gather.7.cloned.1.call-done) | data formatting | bytes 11796480 | tf_op jit(solution)/shard_map/all_gather | solution.py:66
  634.4 9.2 %dot_general.32 = bf16[64,5,9216]{2,1,0:T(8,128)(2,1)} reshape(bf16[320,9216]{1,0:T(8,128)(2,1)} %copy.51) | data formatting | bytes 11796480 | tf_op jit(solution)/shard_map/rf,cf->rc/dot_general | solution.py:64
  643.6 10.6 %fusion = f32[64,5,96]{2,0,1:T(8,128)S(1)} fusion(bf16[64,5,9216]{2,1,0:T(8,128)(2,1)} %dot_general.32, bf16[1,96,9216]{2,1,0:T(8,128)(2,1)} %param.15), kind=kOutput, calls=%fused_computation.2 | convolution fusion | flops 566231040 | bytes 7790592 | tf_op jit(solution)/shard_map/rf,cf->rc/dot_general | solution.py:64
  654.2 0.1 copy.53
  654.3 0.9 reshape.161
  655.2 9.4 %all-to-all-start.1 = ((f32[64,1,480]{2,1,0:T(1,128)}), f32[64,1,480]{2,1,0:T(1,128)S(1)}, u32[]{:S(2)}, u32[]{:S(2)}) async-start(f32[64,1,480]{2,1,0:T(1,128)} %reshape.161), calls=%async_computation.1 | async-start | bytes 262144 | tf_op jit(solution)/shard_map/all_to_all | solution.py:70
  664.6 0.2 fusion.12
  664.7 14.7 %all-to-all-done.1 = f32[64,1,480]{2,1,0:T(1,128)S(1)} async-done(((f32[64,1,480]{2,1,0:T(1,128)}), f32[64,1,480]{2,1,0:T(1,128)S(1)}, u32[]{:S(2)}, u32[]{:S(2)}) %all-to-all-start.1) | async-done | bytes 122912 | tf_op jit(solution)/shard_map/all_to_all | solution.py:70
  679.4 0.5 broadcast.59
  680.0 0.9 reduce.2
  680.9 0.1 reshape.162
  681.0 0.1 all_to_all.39
  681.2 0.1 multiply_convert_fusion.2
  681.3 5.2 copy.55
  686.5 0.5 broadcast.60
  687.0 34.2 %reduce.3 = bf16[6144,5]{1,0:T(8,128)(2,1)S(1)} reduce(bf16[6144,1,5]{2,1,0:T(2,128)(2,1)} %bitcast.68, bf16[]{:T(256)} %broadcast.60), dimensions={1}, to_apply=%bitcast.51.reduce_sub_computation | reduce | bytes 122882
  721.2 3.0 reshape.163
  724.3 14.1 %all-to-all-start.2 = ((bf16[8,2,1920]{2,1,0:T(2,128)(2,1)}), bf16[8,2,1920]{2,1,0:T(2,128)(2,1)S(1)}, u32[]{:S(2)}, u32[]{:S(2)}) async-start(bf16[8,2,1920]{2,1,0:T(2,128)(2,1)} %reshape.163), calls=%async_computation.2 | async-start | bytes 122880 | tf_op jit(solution)/shard_map/all_to_all | solution.py:72
  738.4 0.1 eq.15
  738.4 4.8 all-to-all-done.2
  743.2 5.1 reshape.164
  748.3 6.0 copy.56
  754.4 1.0 fusion.8
  (26 shorter events, 0.2 us)
Async XLA Ops:
  6.5 466.1 %copy-start = (bf16[1,144,6144]{2,1,0:T(8,128)(2,1)S(1)}, bf16[1,144,6144]{2,1,0:T(8,128)(2,1)}, u32[]{:S(2)}) copy-start(bf16[1,144,6144]{2,1,0:T(8,128)(2,1)} %param.14) | copy-start | bytes 5308420
  6.5 5.0 copy-start.5
  6.5 215.2 %all-gather.5.cloned.1.call-start = ((), (), s32[]{:S(2)}) async-start(), calls=%async_computation.3 | async-start | bytes 19169280 | tf_op jit(solution)/shard_map/all_gather | solution.py:11
  10.3 454.7 %all-gather.9.cloned.1.call-start = ((), (), s32[]{:S(2)}) async-start(), calls=%async_computation.5 | async-start | bytes 6389760 | tf_op jit(solution)/shard_map/all_gather | solution.py:58
  228.2 244.5 %copy-start.2 = (bf16[256,768]{1,0:T(8,128)(2,1)}, bf16[256,768]{1,0:T(8,128)(2,1)S(1)}, u32[]{:S(2)}) copy-start(bf16[256,768]{1,0:T(8,128)(2,1)S(1)} %copy.47) | copy-start | bytes 1179652
  239.1 386.0 %all-gather.7.cloned.1.call-start = ((), (), s32[]{:S(2)}) async-start(), calls=%async_computation.4 | async-start | bytes 7188480 | tf_op jit(solution)/shard_map/all_gather | solution.py:66
  643.6 21.0 %copy-start.4 = (bf16[8,5,768]{2,1,0:T(8,128)(2,1)S(1)}, bf16[8,5,768]{2,1,0:T(8,128)(2,1)}, u32[]{:S(2)}) copy-start(bf16[8,5,768]{2,1,0:T(8,128)(2,1)} %all_to_all.46) | copy-start | bytes 184324
  643.6 21.0 %copy-start.6 = (bf16[6144,1]{0,1:T(2,128)(2,1)S(1)}, bf16[6144,1]{0,1:T(2,128)(2,1)}, u32[]{:S(2)}) copy-start(bf16[6144,1]{0,1:T(2,128)(2,1)} %param.13) | copy-start | bytes 36868
  655.2 24.2 %all-to-all-start.1 = ((f32[64,1,480]{2,1,0:T(1,128)}), f32[64,1,480]{2,1,0:T(1,128)S(1)}, u32[]{:S(2)}, u32[]{:S(2)}) async-start(f32[64,1,480]{2,1,0:T(1,128)} %reshape.161), calls=%async_computation.1 | async-start | bytes 262144 | tf_op jit(solution)/shard_map/all_to_all | solution.py:70
  721.2 34.1 %copy-start.1 = (bf16[1,144,6144]{2,1,0:T(8,128)(2,1)S(1)}, bf16[1,144,6144]{2,1,0:T(8,128)(2,1)}, u32[]{:S(2)}) copy-start(bf16[1,144,6144]{2,1,0:T(8,128)(2,1)} %param.14) | copy-start | bytes 5308420
  724.3 30.1 %copy-start.3 = (bf16[256,768]{1,0:T(8,128)(2,1)S(1)}, bf16[256,768]{1,0:T(8,128)(2,1)}, u32[]{:S(2)}) copy-start(bf16[256,768]{1,0:T(8,128)(2,1)} %copy-done.2) | copy-start | bytes 1179652
  724.3 18.9 %all-to-all-start.2 = ((bf16[8,2,1920]{2,1,0:T(2,128)(2,1)}), bf16[8,2,1920]{2,1,0:T(2,128)(2,1)S(1)}, u32[]{:S(2)}, u32[]{:S(2)}) async-start(bf16[8,2,1920]{2,1,0:T(2,128)(2,1)} %reshape.163), calls=%async_computation.2 | async-start | bytes 122880 | tf_op jit(solution)/shard_map/all_to_all | solution.py:72
Sparse Core Ops, SparseCore 0:
  10.4 211.2 all-gather.4
  239.3 225.6 all-gather.8
  477.2 147.9 all-gather.6
where the time goes:
time: 765 us; the launch traced here: 762 us
  waiting for transfers between devices  603 us (79%)
  local copies, waits for them, and re-layouts  53.9 us (7%)
  other arithmetic  37.3 us (5%)
  starting transfers between devices  23.7 us (3%)
  matrix products  20.3 us (3%)
  between operations  13.3 us (2%)
  blocking collectives  10.2 us (1%)
    all_gather x1, waiting for transfers between devices, body(): lax.all_gather(own_rows, 'seq', axis=0, tiled=True)  226 us
    all_gather x1, waiting for transfers between devices, entering(): gathered = lax.all_gather(array.astype(jnp.bfloat16), axis)  210 us
    all_gather x1, waiting for transfers between devices, body(): lax.all_gather(hidden, 'seq', axis=1, tiled=True)  148 us
    unnamed x1, other arithmetic  34.2 us
    unnamed x25, local copies, waits for them, and re-layouts  21 us
  transfers between devices with their start and end apart: 5, of which 5 were waited for; matrix products, arithmetic and copies ran while one was open for 0% of the time, Pallas kernels for 0%

commit v1 on v0

v1 whole, which is shorter than its diff:
```python
import jax
import jax.numpy as jnp
from jax import lax
from jax.experimental import pallas as pl
from jax.experimental.pallas import tpu as pltpu
from jax.sharding import Mesh, PartitionSpec as P

HEAD = 96
LANES = 128
SLOTS = 32
INTERPRET = False
BF16 = jnp.bfloat16
F32 = jnp.float32


def call(kernel, out, *args, scratch=(), name=None):
    return pl.pallas_call(
        kernel,
        out_shape=out,
        scratch_shapes=list(scratch),
        compiler_params=pltpu.CompilerParams(vmem_limit_bytes=48 * 2**20),
        interpret=INTERPRET,
        name=name,
    )(*args)


def tile_heads(tile):
    first = tile * LANES // HEAD
    return first, (first + 1) * HEAD - tile * LANES


def head_window(head):
    first, last = head * HEAD // LANES, (head * HEAD + HEAD - 1) // LANES
    return first * LANES, (last + 1) * LANES, head * HEAD - first * LANES


def chunk_rows(tile, third):
    upper, kind = divmod(tile, 3)
    return upper * 32 * 16 + kind * 3 + third


def state_kernel(k_ref, v_ref, out_ref, grand, rows):
    grand[...] = lax.dot_general(
        k_ref[...], v_ref[...], (((0,), (0,)), ((), ())), preferred_element_type=F32
    )
    rows[...] = jnp.zeros_like(rows)
    lane = lax.broadcasted_iota(jnp.int32, (HEAD, LANES), 1)
    for tile in range(6):
        head, split = tile_heads(tile)
        at = slice(tile * LANES, (tile + 1) * LANES)
        one = grand[head * HEAD : (head + 1) * HEAD, at]
        two = grand[(head + 1) * HEAD : (head + 2) * HEAD, at]
        block = jnp.where(lane < split, one, two)
        for third in range(3):
            rows[pl.ds(chunk_rows(tile, third), 32, stride=16), :] = block[third * 32 : third * 32 + 32]
    out_ref[...] = rows[...].reshape(64, 16, LANES).astype(BF16)


def prefix_kernel(in_ref, out_ref):
    total = jnp.zeros((16, LANES), F32)
    for block in range(in_ref.shape[0]):
        out_ref[block] = total.astype(BF16)
        total = total + in_ref[block].astype(F32)


def inner_kernel(q_ref, k_ref, v_ref, out_ref):
    length = q_ref.shape[0]
    out_ref[...] = jnp.zeros_like(out_ref)
    below = lax.broadcasted_iota(jnp.int32, (length, length), 0) >= lax.broadcasted_iota(
        jnp.int32, (length, length), 1
    )
    for head in range(8):
        start, stop, low = head_window(head)
        lane = lax.broadcasted_iota(jnp.int32, (1, stop - start), 1)
        mine = (lane >= low) & (lane < low + HEAD)
        q = q_ref[:, start:stop] * mine.astype(F32).astype(BF16)
        scores = lax.dot_general(
            q, k_ref[:, start:stop], (((1,), (1,)), ((), ())), preferred_element_type=F32
        )
        scores = jnp.where(below, scores, 0.0).astype(BF16)
        mixed = jnp.dot(scores, v_ref[:, start:stop], preferred_element_type=F32)
        out_ref[:, start:stop] = jnp.where(mine, mixed, out_ref[:, start:stop])


def attn_kernel(q_ref, inner_ref, p_ref, sel_ref, attn_ref, pay_ref, rows, wide, normed, picks):
    length = q_ref.shape[0]
    rows[...] = p_ref[...].astype(F32).reshape(64 * 16, LANES)
    wide[...] = jnp.zeros_like(wide)
    lane = lax.broadcasted_iota(jnp.int32, (32, LANES), 1)
    for tile in range(6):
        head, split = tile_heads(tile)
        at = slice(tile * LANES, (tile + 1) * LANES)
        for third in range(3):
            block = rows[pl.ds(chunk_rows(tile, third), 32, stride=16), :]
            low = head * HEAD + third * 32
            wide[low : low + 32, at] = jnp.where(lane < split, block, 0.0).astype(BF16)
            low = low + HEAD
            wide[low : low + 32, at] = jnp.where(lane < split, 0.0, block).astype(BF16)
    normed[...] = inner_ref[...] + jnp.dot(q_ref[...], wide[...], preferred_element_type=F32)
    for head in range(8):
        start, stop, low = head_window(head)
        lane = lax.broadcasted_iota(jnp.int32, (1, stop - start), 1)
        mine = (lane >= low) & (lane < low + HEAD)
        mixed = normed[:, start:stop]
        power = jnp.sum(jnp.where(mine, mixed * mixed, 0.0), axis=-1, keepdims=True) / HEAD
        normed[:, start:stop] = jnp.where(mine, mixed * lax.rsqrt(power + 1e-06), mixed)
    attn = normed[...].astype(BF16)
    attn_ref[...] = attn
    place = lax.broadcasted_iota(jnp.int32, (40, length), 1)
    chosen = jnp.where(place == sel_ref[...], 1.0, 0.0).astype(BF16)
    picked = jnp.dot(chosen, attn, preferred_element_type=F32)
    picks[...] = jnp.zeros_like(picks)
    for i in range(5):
        for tile in range(6):
            picks[pl.ds(i * 6 + tile, 8, stride=SLOTS), :] = picked[
                i * 8 : i * 8 + 8, tile * LANES : (tile + 1) * LANES
            ]
    pay = picks[...].reshape(8, SLOTS, LANES).astype(BF16)
    for copy in range(8):
        pay_ref[copy * 8 : copy * 8 + 8] = pay


def up_kernel(x_ref, w_ref, r_ref, out_ref, rows, picked):
    rows[...] = x_ref[...].astype(F32).reshape(64 * SLOTS, LANES)
    for i in range(5):
        for tile in range(6):
            piece = rows[pl.ds(i * 6 + tile, 64, stride=SLOTS), :]
            picked[i * 64 : i * 64 + 64, tile * LANES : (tile + 1) * LANES] = piece.astype(BF16)
    x = picked[...]
    units = w_ref.shape[0]
    out_ref[:, :units] = lax.dot_general(
        x, w_ref[...], (((1,), (1,)), ((), ())), preferred_element_type=F32
    ).astype(BF16)
    column = jnp.broadcast_to(r_ref[...].astype(F32), (LANES, x.shape[1])).astype(BF16)
    out_ref[:, units:] = lax.dot_general(
        x, column, (((1,), (1,)), ((), ())), preferred_element_type=F32
    ).astype(BF16)


def act_kernel(in_ref, out_ref):
    units = out_ref.shape[1]
    total = in_ref[0].astype(F32)
    for part in range(1, 8):
        total = total + in_ref[part].astype(F32)
    gate = jax.nn.sigmoid(total[:, units : units + 1])
    up = total[:, :units]
    out_ref[...] = (up / (1.0 + jnp.exp(-up)) * gate).astype(BF16)


def down_kernel(h_ref, w_ref, out_ref, rows):
    y = lax.dot_general(
        h_ref[...], w_ref[...], (((1,), (1,)), ((), ())), preferred_element_type=F32
    )
    for slot in (30, 31):
        rows[pl.ds(slot, 64, stride=SLOTS), :] = jnp.zeros((64, LANES), F32)
    for i in range(5):
        for tile in range(6):
            rows[pl.ds(i * 6 + tile, 64, stride=SLOTS), :] = y[
                i * 64 : i * 64 + 64, tile * LANES : (tile + 1) * LANES
            ]
    out_ref[...] = rows[...].reshape(64, SLOTS, LANES).astype(BF16)


def add_kernel(attn_ref, y_ref, sel_ref, out_ref, rows, weighted):
    length = attn_ref.shape[0]
    total = y_ref[0:8].astype(F32)
    for part in range(1, 8):
        total = total + y_ref[part * 8 : part * 8 + 8].astype(F32)
    rows[...] = total.reshape(8 * SLOTS, LANES)
    weighted[...] = jnp.zeros_like(weighted)
    for i in range(5):
        for tile in range(6):
            weighted[i * 8 : i * 8 + 8, tile * LANES : (tile + 1) * LANES] = rows[
                pl.ds(i * 6 + tile, 8, stride=SLOTS), :
            ]
    place = lax.broadcasted_iota(jnp.int32, (length, LANES), 0)
    chosen = jnp.where(place == sel_ref[...], 1.0, 0.0).astype(BF16)
    added = jnp.dot(chosen, weighted[...].astype(BF16), preferred_element_type=F32)
    out_ref[...] = (attn_ref[...].astype(F32) + added).astype(BF16)


def shape(dims, dtype=BF16):
    return jax.ShapeDtypeStruct(dims, dtype)


def body(queries, keys, values, selections, router, w_up, w_down):
    length, width = queries.shape
    parts = lax.axis_size("p")
    seq = ("r", "c")
    swap = [(c * parts + p, p * parts + c) for c in range(parts) for p in range(parts)]
    turn = [
        ((r * parts + c) * parts + p, (c * parts + p) * parts + r)
        for r in range(parts)
        for c in range(parts)
        for p in range(parts)
    ]

    up_here = lax.ppermute(w_up[0], ("c", "p"), swap)
    router_here = lax.ppermute(router.reshape(parts, width), ("c", "p"), swap)
    units, full = up_here.shape
    up_cut = up_here.reshape(units, parts, width).transpose(1, 0, 2)
    up_mine = lax.all_to_all(up_cut, "p", 0, 0, tiled=True).reshape(parts * units, width)
    router_mine = lax.dynamic_slice_in_dim(router_here, lax.axis_index("p"), 1, 0)
    columns, hidden = w_down[0].shape
    group = hidden // parts
    down_cut = w_down[0].reshape(columns, parts, group).transpose(1, 0, 2)
    down_near = lax.all_to_all(down_cut, "c", 0, 0, tiled=True)
    down_mine = lax.ppermute(down_near, ("r", "c", "p"), turn).reshape(parts * columns, group)

    sel = selections[0].T.reshape(-1)
    sel_column = sel[:, None]
    sel_row = jnp.pad(sel, (0, LANES - sel.shape[0]), constant_values=-1)[None]

    state = call(
        state_kernel,
        shape((64, 16, LANES)),
        keys,
        values,
        scratch=[pltpu.VMEM((width, width), F32), pltpu.VMEM((64 * 16, LANES), F32)],
        name="state",
    )
    chunks = lax.all_to_all(state, seq, 0, 0, tiled=True)
    inner = call(inner_kernel, shape((length, width), F32), queries, keys, values, name="inner")
    before = call(prefix_kernel, shape((64, 16, LANES)), chunks, name="prefix")
    before = lax.all_to_all(before, seq, 0, 0, tiled=True)
    attn, pay = call(
        attn_kernel,
        (shape((length, width)), shape((64, SLOTS, LANES))),
        queries,
        inner,
        before,
        sel_column,
        scratch=[
            pltpu.VMEM((64 * 16, LANES), F32),
            pltpu.VMEM((width, width), BF16),
            pltpu.VMEM((length, width), F32),
            pltpu.VMEM((8 * SLOTS, LANES), F32),
        ],
        name="attn",
    )
    arrived = lax.all_to_all(pay, seq, 0, 0, tiled=True)
    partial = call(
        up_kernel,
        shape((320, group + LANES)),
        arrived,
        up_mine,
        router_mine,
        scratch=[pltpu.VMEM((64 * SLOTS, LANES), F32), pltpu.VMEM((320, width), BF16)],
        name="up",
    )
    sums = lax.all_to_all(partial.reshape(parts, 40, group + LANES), "p", 0, 0, tiled=True)
    act = call(act_kernel, shape((40, group)), sums, name="act")
    act = lax.all_gather(act, "p", axis=0, tiled=True)
    out = call(
        down_kernel,
        shape((64, SLOTS, LANES)),
        act,
        down_mine,
        scratch=[pltpu.VMEM((64 * SLOTS, LANES), F32)],
        name="down",
    )
    back = lax.all_to_all(out, seq, 0, 0, tiled=True)
    return call(
        add_kernel,
        shape((length, width)),
        attn,
        back,
        sel_row,
        scratch=[pltpu.VMEM((8 * SLOTS, LANES), F32), pltpu.VMEM((LANES, width), F32)],
        name="add",
    )


def solution(mesh):
    parts = mesh.devices.shape[1]
    split = Mesh(mesh.devices.reshape(-1, parts, parts), ("r", "c", "p"))
    seq = ("r", "c")
    placed = (
        P(seq, "p"),
        P(seq, "p"),
        P(seq, "p"),
        P(seq, None, None),
        P(None, "p"),
        P("p", seq, None),
        P("p", seq, None),
    )
    return jax.shard_map(
        body, mesh=split, in_specs=placed, out_specs=P(seq, "p"), check_vma=False
    )
```

time: 765 us -> 589 us (0.77)
  waiting for transfers between devices: 603 us -> 190 us
  blocking collectives: 10.2 us -> 292 us
  starting transfers between devices: 23.7 us -> 81 us
  local copies, waits for them, and re-layouts: 53.9 us -> 10.4 us
  other arithmetic: 37.3 us -> 0.07 us
  matrix products: 20.3 us -> 0 us
  between operations: 13.3 us -> 0.17 us
  Pallas kernels: 0 us -> 11.3 us
    all_gather x3 -> x0, waiting for transfers between devices: 584 us -> none  [the longest x1 226 us: body(): lax.all_gather(own_rows, 'seq', axis=0, tiled=True)]
    all_to_all x1, blocking collectives: 10.2 us -> 278 us  [body(): lax.all_to_all(partial.reshape(parts, 40, group + LANES), 'p', 0, 0, tile...]
    all_to_all x2 -> x6, waiting for transfers between devices: 19.4 us -> 125 us  [the longest x1 41.8 us: body(): before = lax.all_to_all(before, seq, 0, 0, tiled=True)]
    ppermute x0 -> x3, waiting for transfers between devices: none -> 65.8 us  [the longest x1 39.6 us: body(): router_here = lax.ppermute(router.reshape(parts, width), ('c', 'p'), swap)]
    all_to_all x2 -> x6, starting transfers between devices: 23.4 us -> 68.6 us  [the longest x1 19.3 us: body(): chunks = lax.all_to_all(state, seq, 0, 0, tiled=True)]
    unnamed x1, other arithmetic: 34.2 us -> 0.07 us
    dot_general x7 -> x0, matrix products: 20.3 us -> none  [the longest x1 10.6 us: body(): jnp.einsum('rf,cf->rc', lax.all_gather(hidden, 'seq', axis=1, tiled=True)...]
    all_gather x0 -> x1, blocking collectives: none -> 14.4 us  [body(): act = lax.all_gather(act, 'p', axis=0, tiled=True)]
  transfers between devices with their start and end apart: 5 -> 9, of which waited for: 5 -> 7; matrix products, arithmetic and copies ran while one was open for 0% -> 1% of each run, Pallas kernels for 0% -> 1%
where the time goes in v1:
time: 589 us; the launch traced here: 586 us
  blocking collectives  292 us (50%)
  waiting for transfers between devices  190 us (32%)
  starting transfers between devices  81 us (14%)
  Pallas kernels  11.3 us (2%)
  local copies, waits for them, and re-layouts  10.4 us (2%)
    all_to_all x1, blocking collectives, body(): lax.all_to_all(partial.reshape(parts, 40, group + LANES), 'p', 0, 0, tile...  278 us
    all_to_all x1, waiting for transfers between devices, body(): before = lax.all_to_all(before, seq, 0, 0, tiled=True)  41.8 us
    ppermute x1, waiting for transfers between devices, body(): router_here = lax.ppermute(router.reshape(parts, width), ('c', 'p'), swap)  39.6 us
    all_to_all x1, waiting for transfers between devices, body(): back = lax.all_to_all(out, seq, 0, 0, tiled=True)  31 us
    ppermute x1, waiting for transfers between devices, body(): up_here = lax.ppermute(w_up[0], ('c', 'p'), swap)  26.2 us
    all_to_all x1, waiting for transfers between devices, body(): lax.all_to_all(up_cut, 'p', 0, 0, tiled=True).reshape(parts * units, width)  19.6 us
    all_to_all x1, starting transfers between devices, body(): chunks = lax.all_to_all(state, seq, 0, 0, tiled=True)  19.3 us
    all_to_all x1, starting transfers between devices, body(): back = lax.all_to_all(out, seq, 0, 0, tiled=True)  17.8 us
  transfers between devices with their start and end apart: 9, of which 7 were waited for; matrix products, arithmetic and copies ran while one was open for 1% of the time, Pallas kernels for 1%

profile of v1, /device:TPU:1, one launch (start us, length us, event | category | flops | bytes accessed | tf_op | source)
XLA Modules:
  0.0 585.7 jit_solution(15989532920737854470)
XLA Ops:
  0.0 0.0 copy-start
  0.0 1.0 copy-done
  1.0 0.0 copy-start.2
  1.0 1.0 copy-done.2
  2.0 1.3 state.1
  3.3 19.3 %all-to-all-start = ((bf16[64,16,128]{2,1,0:T(8,128)(2,1)}), bf16[64,16,128]{2,1,0:T(8,128)(2,1)S(1)}, u32[]{:S(2)}, u32[]{:S(2)}) async-start(bf16[64,16,128]{2,1,0:T(8,128)(2,1)} %state.1), calls=%async_computation | async-start | bytes 524288 | tf_op jit(solution)/shard_map/all_to_all | solution.py:222
  22.5 4.0 collective-permute-start
  26.6 15.5 %all-to-all-done.in_ref = bf16[64,16,128]{2,1,0:T(8,128)(2,1)S(1)} async-done(((bf16[64,16,128]{2,1,0:T(8,128)(2,1)}), bf16[64,16,128]{2,1,0:T(8,128)(2,1)S(1)}, u32[]{:S(2)}, u32[]{:S(2)}) %all-to-all-start) | async-done | bytes 262176 | tf_op jit(solution)/shard_map/all_to_all | solution.py:222
  42.0 0.8 prefix.1
  42.8 8.2 %all-to-all-start.1 = ((bf16[64,16,128]{2,1,0:T(8,128)(2,1)}), bf16[64,16,128]{2,1,0:T(8,128)(2,1)S(1)}, u32[]{:S(2)}, u32[]{:S(2)}) async-start(bf16[64,16,128]{2,1,0:T(8,128)(2,1)} %prefix.1), calls=%async_computation.1 | async-start | bytes 524288 | tf_op jit(solution)/shard_map/all_to_all | solution.py:225
  51.1 26.2 %collective-permute-done = bf16[144,6144]{1,0:T(8,128)(2,1)S(1)} collective-permute-done((bf16[144,6144]{1,0:T(8,128)(2,1)}, bf16[144,6144]{1,0:T(8,128)(2,1)S(1)}, u32[]{:S(2)}, u32[]{:S(2)}) %collective-permute-start) | collective-permute-done | bytes 1769504 | tf_op jit(solution)/shard_map/ppermute | solution.py:198
  77.3 1.3 copy.20
  78.6 41.8 %all-to-all-done.1.p_ref = bf16[64,16,128]{2,1,0:T(8,128)(2,1)S(1)} async-done(((bf16[64,16,128]{2,1,0:T(8,128)(2,1)}), bf16[64,16,128]{2,1,0:T(8,128)(2,1)S(1)}, u32[]{:S(2)}, u32[]{:S(2)}) %all-to-all-start.1) | async-done | bytes 262176 | tf_op jit(solution)/shard_map/all_to_all | solution.py:225
  120.4 0.0 copy-start.6
  120.4 0.7 copy-done.6
  121.1 13.2 %all-to-all-start.3 = ((bf16[8,144,768]{2,1,0:T(8,128)(2,1)}), bf16[8,144,768]{2,1,0:T(8,128)(2,1)S(1)}, u32[]{:S(2)}, u32[]{:S(2)}) async-start(bf16[8,144,768]{2,1,0:T(8,128)(2,1)} %bitcast.27), calls=%async_computation.3 | async-start | bytes 3538944 | tf_op jit(solution)/shard_map/all_to_all | solution.py:202
  134.3 1.8 copy.16
  136.0 1.4 copy.21
  137.5 19.6 %all-to-all-done.3 = bf16[8,144,768]{2,1,0:T(8,128)(2,1)S(1)} async-done(((bf16[8,144,768]{2,1,0:T(8,128)(2,1)}), bf16[8,144,768]{2,1,0:T(8,128)(2,1)S(1)}, u32[]{:S(2)}, u32[]{:S(2)}) %all-to-all-start.3) | async-done | bytes 1769504 | tf_op jit(solution)/shard_map/all_to_all | solution.py:202
  157.1 4.4 all-to-all-start.5
  161.6 0.0 copy-done.1
  161.6 0.0 copy-done.3
  161.6 0.0 copy-start.4
  161.6 1.0 copy-done.4
  162.6 0.9 inner.1.inner_ref
  163.5 0.0 copy-done.9
  163.5 0.1 broadcast_in_dim_reshape.4.sel_ref
  163.6 1.0 copy-done.5
  164.6 0.9 copy-done.7
  165.6 1.9 attn.1
  167.5 16.7 %all-to-all-done.5 = bf16[8,96,1152]{2,1,0:T(8,128)(2,1)} async-done(((bf16[8,96,1152]{2,1,0:T(8,128)(2,1)}), bf16[8,96,1152]{2,1,0:T(8,128)(2,1)}, u32[]{:S(2)}, u32[]{:S(2)}) %all-to-all-start.5) | async-done | bytes 1769504 | tf_op jit(solution)/shard_map/all_to_all | solution.py:207
  184.2 5.7 all-to-all-start.2
  189.9 4.1 collective-permute-start.2
  194.0 0.0 copy-done.8
  194.0 0.1 reduce
  194.1 4.3 collective-permute-start.1
  198.4 39.6 %collective-permute-done.1 = bf16[8,768]{1,0:T(8,128)(2,1)S(1)} collective-permute-done((bf16[8,768]{1,0:T(8,128)(2,1)S(1)}, bf16[8,768]{1,0:T(8,128)(2,1)S(1)}, u32[]{:S(2)}, u32[]{:S(2)}) %collective-permute-start.1) | collective-permute-done | bytes 12320 | tf_op jit(solution)/shard_map/ppermute | solution.py:199
  238.0 0.0 all-to-all-done.2.x_ref
  238.0 1.5 up.1
  239.4 278.0 %all_to_all.35.in_ref = bf16[8,40,1280]{2,1,0:T(8,128)(2,1)S(1)} all-to-all(bf16[8,40,1280]{2,1,0:T(8,128)(2,1)S(1)} %bitcast.25), channel_id=1, replica_groups=mesh['r'=8,'c'=8,'p'=8] {'p'}, dimensions={0} | all-to-all | bytes 1638400 | tf_op jit(solution)/shard_map/all_to_all | solution.py:251
  517.4 0.2 act.1
  517.6 14.4 %all_gather.3.h_ref = bf16[320,1152]{1,0:T(8,128)(2,1)S(1)} all-gather(bf16[40,1152]{1,0:T(8,128)(2,1)S(1)} %act.1), channel_id=1, replica_groups=mesh['r'=8,'c'=8,'p'=8] {'p'}, dimensions={0}, use_global_device_ids=true | all-gather | bytes 829440 | tf_op jit(solution)/shard_map/all_gather | solution.py:253
  532.0 0.0 collective-permute-done.2
  532.0 3.7 down.1
  535.7 17.8 %all-to-all-start.6 = ((bf16[64,32,128]{2,1,0:T(8,128)(2,1)}), bf16[64,32,128]{2,1,0:T(8,128)(2,1)S(1)}, u32[]{:S(2)}, u32[]{:S(2)}) async-start(bf16[64,32,128]{2,1,0:T(8,128)(2,1)} %down.1), calls=%async_computation.6 | async-start | bytes 1048576 | tf_op jit(solution)/shard_map/all_to_all | solution.py:262
  553.5 0.1 reshape.23
  553.6 31.0 %all-to-all-done.6.y_ref = bf16[64,32,128]{2,1,0:T(8,128)(2,1)S(1)} async-done(((bf16[64,32,128]{2,1,0:T(8,128)(2,1)}), bf16[64,32,128]{2,1,0:T(8,128)(2,1)S(1)}, u32[]{:S(2)}, u32[]{:S(2)}) %all-to-all-start.6) | async-done | bytes 524320 | tf_op jit(solution)/shard_map/all_to_all | solution.py:262
  584.6 1.1 add.8
  (10 shorter events, 0.1 us)
Async XLA Ops:
  0.0 1.0 copy-start
  1.0 1.0 copy-start.2
  3.3 38.8 %all-to-all-start = ((bf16[64,16,128]{2,1,0:T(8,128)(2,1)}), bf16[64,16,128]{2,1,0:T(8,128)(2,1)S(1)}, u32[]{:S(2)}, u32[]{:S(2)}) async-start(bf16[64,16,128]{2,1,0:T(8,128)(2,1)} %state.1), calls=%async_computation | async-start | bytes 524288 | tf_op jit(solution)/shard_map/all_to_all | solution.py:222
  22.5 54.7 %collective-permute-start = (bf16[144,6144]{1,0:T(8,128)(2,1)}, bf16[144,6144]{1,0:T(8,128)(2,1)S(1)}, u32[]{:S(2)}, u32[]{:S(2)}) collective-permute-start(bf16[144,6144]{1,0:T(8,128)(2,1)} %bitcast.33), channel_id=1, source_target_pairs={{0,0},{1,8},{2,16},{3,24},{4,32},{5,40},{6,48},{7,56},{8,1},{9,9},... | collective-permute-start | bytes 5308424 | tf_op jit(solution)/shard_map/ppermute | solution.py:198
  42.8 77.6 %all-to-all-start.1 = ((bf16[64,16,128]{2,1,0:T(8,128)(2,1)}), bf16[64,16,128]{2,1,0:T(8,128)(2,1)S(1)}, u32[]{:S(2)}, u32[]{:S(2)}) async-start(bf16[64,16,128]{2,1,0:T(8,128)(2,1)} %prefix.1), calls=%async_computation.1 | async-start | bytes 524288 | tf_op jit(solution)/shard_map/all_to_all | solution.py:225
  120.4 0.7 copy-start.6
  121.1 36.0 %all-to-all-start.3 = ((bf16[8,144,768]{2,1,0:T(8,128)(2,1)}), bf16[8,144,768]{2,1,0:T(8,128)(2,1)S(1)}, u32[]{:S(2)}, u32[]{:S(2)}) async-start(bf16[8,144,768]{2,1,0:T(8,128)(2,1)} %bitcast.27), calls=%async_computation.3 | async-start | bytes 3538944 | tf_op jit(solution)/shard_map/all_to_all | solution.py:202
  157.1 4.5 copy-start.1
  157.1 4.5 copy-start.3
  157.1 27.1 %all-to-all-start.5 = ((bf16[8,96,1152]{2,1,0:T(8,128)(2,1)}), bf16[8,96,1152]{2,1,0:T(8,128)(2,1)}, u32[]{:S(2)}, u32[]{:S(2)}) async-start(bf16[8,96,1152]{2,1,0:T(8,128)(2,1)} %bitcast.26), calls=%async_computation.5 | async-start | bytes 3538944 | tf_op jit(solution)/shard_map/all_to_all | solution.py:207
  161.6 1.0 copy-start.4
  162.6 0.9 copy-start.9
  162.6 31.4 %copy-start.8 = (bf16[6144,1]{0,1:T(2,128)(2,1)S(1)}, bf16[6144,1]{0,1:T(2,128)(2,1)}, u32[]{:S(2)}) copy-start(bf16[6144,1]{0,1:T(2,128)(2,1)} %param.11) | copy-start | bytes 36868
  163.6 1.0 copy-start.5
  164.6 0.9 copy-start.7
  184.2 53.8 %all-to-all-start.2 = ((bf16[64,32,128]{2,1,0:T(8,128)(2,1)}), bf16[64,32,128]{2,1,0:T(8,128)(2,1)S(1)}, u32[]{:S(2)}, u32[]{:S(2)}) async-start(bf16[64,32,128]{2,1,0:T(8,128)(2,1)} %get-tuple-element.8), calls=%async_computation.2 | async-start | bytes 1048576 | tf_op jit(solution)/shard_map/all_to_all | solution.py:241
  189.9 342.2 %collective-permute-start.2 = (bf16[8,96,1152]{2,1,0:T(8,128)(2,1)}, bf16[8,96,1152]{2,1,0:T(8,128)(2,1)}, u32[]{:S(2)}, u32[]{:S(2)}) collective-permute-start(bf16[8,96,1152]{2,1,0:T(8,128)(2,1)} %all-to-all-done.5), channel_id=1, source_target_pairs={{0,0},{1,8},{2,16},{3,24},{4,32},{5,40},{6,48},{7,56},{8,64},{9,72... | collective-permute-start | bytes 5308424 | tf_op jit(solution)/shard_map/ppermute | solution.py:208
  194.1 43.9 %collective-permute-start.1 = (bf16[8,768]{1,0:T(8,128)(2,1)S(1)}, bf16[8,768]{1,0:T(8,128)(2,1)S(1)}, u32[]{:S(2)}, u32[]{:S(2)}) collective-permute-start(bf16[8,768]{1,0:T(8,128)(2,1)S(1)} %reshape.20), channel_id=1, source_target_pairs={{0,0},{1,8},{2,16},{3,24},{4,32},{5,40},{6,48},{7,56},{8,1},{9,9},... | collective-permute-start | bytes 36872 | tf_op jit(solution)/shard_map/ppermute | solution.py:199
  535.7 48.9 %all-to-all-start.6 = ((bf16[64,32,128]{2,1,0:T(8,128)(2,1)}), bf16[64,32,128]{2,1,0:T(8,128)(2,1)S(1)}, u32[]{:S(2)}, u32[]{:S(2)}) async-start(bf16[64,32,128]{2,1,0:T(8,128)(2,1)} %down.1), calls=%async_computation.6 | async-start | bytes 1048576 | tf_op jit(solution)/shard_map/all_to_all | solution.py:262

commit v2 on v1

--- a/solution.py
+++ b/solution.py
@@ -13,14 +13,29 @@
 F32 = jnp.float32
 
 
-def call(kernel, out, *args, scratch=(), name=None):
+SMEM = pltpu.SMEM
+VMEM = pltpu.VMEM
+HBM = pltpu.HBM
+
+
+def call(kernel, out, *args, scratch=(), spaces=None, name=None):
+    specs = {}
+    if spaces:
+        ins, outs = spaces
+        specs["in_specs"] = [pl.BlockSpec(memory_space=space) for space in ins]
+        specs["out_specs"] = (
+            [pl.BlockSpec(memory_space=space) for space in outs]
+            if isinstance(outs, list)
+            else pl.BlockSpec(memory_space=outs)
+        )
     return pl.pallas_call(
         kernel,
         out_shape=out,
         scratch_shapes=list(scratch),
-        compiler_params=pltpu.CompilerParams(vmem_limit_bytes=48 * 2**20),
+        compiler_params=pltpu.CompilerParams(vmem_limit_bytes=16 * 2**20),
         interpret=INTERPRET,
         name=name,
+        **specs,
     )(*args)
 
 
@@ -115,44 +130,79 @@
             picks[pl.ds(i * 6 + tile, 8, stride=SLOTS), :] = picked[
                 i * 8 : i * 8 + 8, tile * LANES : (tile + 1) * LANES
             ]
-    pay = picks[...].reshape(8, SLOTS, LANES).astype(BF16)
-    for copy in range(8):
-        pay_ref[copy * 8 : copy * 8 + 8] = pay
-
-
-def up_kernel(x_ref, w_ref, r_ref, out_ref, rows, picked):
+    pay_ref[...] = picks[...].reshape(8, SLOTS, LANES).astype(BF16)
+
+
+def cut_up_kernel(place_ref, w_ref, *refs):
+    outs, sems = refs[:8], refs[8]
+    width = outs[0].shape[1]
+    copies = []
+    for k, out in enumerate(outs):
+        low = pl.multiple_of((place_ref[0] ^ k) * width, LANES)
+        copies.append(pltpu.make_async_copy(w_ref.at[:, pl.ds(low, width)], out, sems.at[k]))
+        copies[-1].start()
+    for copy in copies:
+        copy.wait()
+
+
+def cut_down_kernel(place_ref, w_ref, *refs):
+    outs, cut, sems = refs[:8], refs[8], refs[9]
+    run = w_ref.shape[1] // 64
+    for part in range(8):
+        for group in range(8):
+            low = (group * 8 + part) * run
+            cut[part, :, group * run : (group + 1) * run] = w_ref[:, low : low + run]
+    copies = []
+    for k, out in enumerate(outs):
+        copies.append(pltpu.make_async_copy(cut.at[place_ref[0] ^ k], out, sems.at[k]))
+        copies[-1].start()
+    for copy in copies:
+        copy.wait()
+
+
+def fetch(place_ref, pieces, whole, sems):
+    copies = []
+    for k, piece in enumerate(pieces):
+        rows = piece.shape[0]
+        low = pl.multiple_of((place_ref[0] ^ k) * rows, 16)
+        copies.append(pltpu.make_async_copy(piece, whole.at[pl.ds(low, rows), :], sems.at[k]))
+        copies[-1].start()
+    return copies
+
+
+def up_kernel(place_ref, x_ref, *refs):
+    pieces, out_ref, rows, picked, whole, sems = refs[:8], *refs[8:]
+    copies = fetch(place_ref, pieces, whole, sems)
     rows[...] = x_ref[...].astype(F32).reshape(64 * SLOTS, LANES)
+    picked[320:] = jnp.zeros((64, picked.shape[1]), BF16)
     for i in range(5):
         for tile in range(6):
             piece = rows[pl.ds(i * 6 + tile, 64, stride=SLOTS), :]
             picked[i * 64 : i * 64 + 64, tile * LANES : (tile + 1) * LANES] = piece.astype(BF16)
-    x = picked[...]
-    units = w_ref.shape[0]
-    out_ref[:, :units] = lax.dot_general(
-        x, w_ref[...], (((1,), (1,)), ((), ())), preferred_element_type=F32
+    for copy in copies:
+        copy.wait()
+    out_ref[...] = lax.dot_general(
+        whole[...], picked[...], (((1,), (1,)), ((), ())), preferred_element_type=F32
     ).astype(BF16)
-    column = jnp.broadcast_to(r_ref[...].astype(F32), (LANES, x.shape[1])).astype(BF16)
-    out_ref[:, units:] = lax.dot_general(
-        x, column, (((1,), (1,)), ((), ())), preferred_element_type=F32
-    ).astype(BF16)
 
 
 def act_kernel(in_ref, out_ref):
-    units = out_ref.shape[1]
-    total = in_ref[0].astype(F32)
+    up = in_ref[0].astype(F32)
     for part in range(1, 8):
-        total = total + in_ref[part].astype(F32)
-    gate = jax.nn.sigmoid(total[:, units : units + 1])
-    up = total[:, :units]
-    out_ref[...] = (up / (1.0 + jnp.exp(-up)) * gate).astype(BF16)
-
-
-def down_kernel(h_ref, w_ref, out_ref, rows):
-    y = lax.dot_general(
-        h_ref[...], w_ref[...], (((1,), (1,)), ((), ())), preferred_element_type=F32
-    )
+        up = up + in_ref[part].astype(F32)
+    out_ref[...] = (up / (1.0 + jnp.exp(-up))).astype(BF16)
+
+
+def down_kernel(place_ref, h_ref, *refs):
+    pieces, out_ref, rows, whole, sems = refs[:8], *refs[8:]
+    copies = fetch(place_ref, pieces, whole, sems)
     for slot in (30, 31):
         rows[pl.ds(slot, 64, stride=SLOTS), :] = jnp.zeros((64, LANES), F32)
+    for copy in copies:
+        copy.wait()
+    y = lax.dot_general(
+        h_ref[...], whole[...], (((0,), (1,)), ((), ())), preferred_element_type=F32
+    )
     for i in range(5):
         for tile in range(6):
             rows[pl.ds(i * 6 + tile, 64, stride=SLOTS), :] = y[
@@ -161,12 +211,27 @@
     out_ref[...] = rows[...].reshape(64, SLOTS, LANES).astype(BF16)
 
 
+def weigh_kernel(y_ref, row_ref, router_ref, out_ref):
+    products = jnp.zeros((SLOTS, LANES), F32)
+    for part in range(8):
+        products = products + row_ref[part].astype(F32) * router_ref[part].astype(F32)
+    one = lax.broadcasted_iota(jnp.int32, (SLOTS, SLOTS), 0) // 6
+    two = lax.broadcasted_iota(jnp.int32, (SLOTS, SLOTS), 1) // 6
+    alike = jnp.where(one == two, 1.0, 0.0)
+    sums = jnp.dot(
+        alike, products, preferred_element_type=F32, precision=lax.Precision.HIGHEST
+    )
+    gate = jax.nn.sigmoid(jnp.sum(sums, axis=-1, keepdims=True))
+    for group in range(8):
+        total = y_ref[group * 8].astype(F32)
+        for part in range(1, 8):
+            total = total + y_ref[group * 8 + part].astype(F32)
+        out_ref[group] = (total * gate).astype(BF16)
+
+
 def add_kernel(attn_ref, y_ref, sel_ref, out_ref, rows, weighted):
     length = attn_ref.shape[0]
-    total = y_ref[0:8].astype(F32)
-    for part in range(1, 8):
-        total = total + y_ref[part * 8 : part * 8 + 8].astype(F32)
-    rows[...] = total.reshape(8 * SLOTS, LANES)
+    rows[...] = y_ref[...].astype(F32).reshape(8 * SLOTS, LANES)
     weighted[...] = jnp.zeros_like(weighted)
     for i in range(5):
         for tile in range(6):
@@ -183,33 +248,27 @@
     return jax.ShapeDtypeStruct(dims, dtype)
 
 
+def exchange(pieces, first, last):
+    count = len(pieces)
+    return [
+        lax.ppermute(pieces[k], "c", [(c, c ^ k) for c in range(count)])
+        for k in range(first, last)
+    ]
+
+
 def body(queries, keys, values, selections, router, w_up, w_down):
     length, width = queries.shape
     parts = lax.axis_size("p")
     seq = ("r", "c")
-    swap = [(c * parts + p, p * parts + c) for c in range(parts) for p in range(parts)]
-    turn = [
-        ((r * parts + c) * parts + p, (c * parts + p) * parts + r)
-        for r in range(parts)
-        for c in range(parts)
-        for p in range(parts)
-    ]
-
-    up_here = lax.ppermute(w_up[0], ("c", "p"), swap)
-    router_here = lax.ppermute(router.reshape(parts, width), ("c", "p"), swap)
-    units, full = up_here.shape
-    up_cut = up_here.reshape(units, parts, width).transpose(1, 0, 2)
-    up_mine = lax.all_to_all(up_cut, "p", 0, 0, tiled=True).reshape(parts * units, width)
-    router_mine = lax.dynamic_slice_in_dim(router_here, lax.axis_index("p"), 1, 0)
-    columns, hidden = w_down[0].shape
-    group = hidden // parts
-    down_cut = w_down[0].reshape(columns, parts, group).transpose(1, 0, 2)
-    down_near = lax.all_to_all(down_cut, "c", 0, 0, tiled=True)
-    down_mine = lax.ppermute(down_near, ("r", "c", "p"), turn).reshape(parts * columns, group)
-
+    units = w_up.shape[1]
+    columns = w_down.shape[1]
+    group = w_down.shape[2] // parts
+    place = lax.axis_index("c").astype(jnp.int32).reshape(1)
     sel = selections[0].T.reshape(-1)
     sel_column = sel[:, None]
     sel_row = jnp.pad(sel, (0, LANES - sel.shape[0]), constant_values=-1)[None]
+    router_rows = jnp.tile(router.reshape(parts, 6, LANES), (1, 5, 1))
+    router_rows = jnp.pad(router_rows, ((0, 0), (0, SLOTS - 30), (0, 0)))
 
     state = call(
         state_kernel,
@@ -219,13 +278,38 @@
         scratch=[pltpu.VMEM((width, width), F32), pltpu.VMEM((64 * 16, LANES), F32)],
         name="state",
     )
+    w_up, state = lax.optimization_barrier((w_up, state))
     chunks = lax.all_to_all(state, seq, 0, 0, tiled=True)
+    up_pieces = call(
+        cut_up_kernel,
+        [shape((units, width))] * 8,
+        place,
+        w_up[0],
+        scratch=[pltpu.SemaphoreType.DMA((8,))],
+        spaces=([SMEM, HBM], [HBM] * 8),
+        name="cut_up",
+    )
+    up_first = exchange(up_pieces, 1, 5)
     inner = call(inner_kernel, shape((length, width), F32), queries, keys, values, name="inner")
+    chunks, inner, up_first = lax.optimization_barrier((chunks, inner, up_first))
     before = call(prefix_kernel, shape((64, 16, LANES)), chunks, name="prefix")
+    w_down, up_pieces, before = lax.optimization_barrier((w_down, up_pieces, before))
     before = lax.all_to_all(before, seq, 0, 0, tiled=True)
+    up_last = exchange(up_pieces, 5, 8)
+    down_pieces = call(
+        cut_down_kernel,
+        [shape((columns, group))] * 8,
+        place,
+        w_down[0],
+        scratch=[pltpu.VMEM((8, columns, group), BF16), pltpu.SemaphoreType.DMA((8,))],
+        spaces=([SMEM, VMEM], [HBM] * 8),
+        name="cut_down",
+    )
+    before, up_last, down_pieces = lax.optimization_barrier((before, up_last, down_pieces))
+    down_moved = exchange(down_pieces, 1, 8)
     attn, pay = call(
         attn_kernel,
-        (shape((length, width)), shape((64, SLOTS, LANES))),
+        (shape((length, width)), shape((8, SLOTS, LANES))),
         queries,
         inner,
         before,
@@ -238,33 +322,54 @@
         ],
         name="attn",
     )
-    arrived = lax.all_to_all(pay, seq, 0, 0, tiled=True)
+    whole_rows = lax.all_to_all(pay, "p", 0, 0, tiled=True)
+    arrived = lax.all_to_all(jnp.tile(whole_rows, (8, 1, 1)), seq, 0, 0, tiled=True)
+    arrived, down_moved = lax.optimization_barrier((arrived, down_moved))
     partial = call(
         up_kernel,
-        shape((320, group + LANES)),
+        shape((8 * units, 384)),
+        place,
         arrived,
-        up_mine,
-        router_mine,
-        scratch=[pltpu.VMEM((64 * SLOTS, LANES), F32), pltpu.VMEM((320, width), BF16)],
+        up_pieces[0],
+        *up_first,
+        *up_last,
+        scratch=[
+            pltpu.VMEM((64 * SLOTS, LANES), F32),
+            pltpu.VMEM((384, width), BF16),
+            pltpu.VMEM((8 * units, width), BF16),
+            pltpu.SemaphoreType.DMA((8,)),
+        ],
+        spaces=([SMEM, VMEM] + [HBM] * 8, VMEM),
         name="up",
     )
-    sums = lax.all_to_all(partial.reshape(parts, 40, group + LANES), "p", 0, 0, tiled=True)
-    act = call(act_kernel, shape((40, group)), sums, name="act")
-    act = lax.all_gather(act, "p", axis=0, tiled=True)
+    sums = lax.all_to_all(partial.reshape(8, units, 384), "c", 0, 0, tiled=True)
+    act = call(act_kernel, shape((units, 384)), sums, name="act")
+    act = lax.all_gather(act, "r", axis=0, tiled=True)
     out = call(
         down_kernel,
         shape((64, SLOTS, LANES)),
+        place,
         act,
-        down_mine,
-        scratch=[pltpu.VMEM((64 * SLOTS, LANES), F32)],
+        down_pieces[0],
+        *down_moved,
+        scratch=[
+            pltpu.VMEM((64 * SLOTS, LANES), F32),
+            pltpu.VMEM((8 * columns, group), BF16),
+            pltpu.SemaphoreType.DMA((8,)),
+        ],
+        spaces=([SMEM, VMEM] + [HBM] * 8, VMEM),
         name="down",
     )
     back = lax.all_to_all(out, seq, 0, 0, tiled=True)
+    weighted = call(
+        weigh_kernel, shape((8, SLOTS, LANES)), back, whole_rows, router_rows, name="weigh"
+    )
+    weighted = lax.all_to_all(weighted, "p", 0, 0, tiled=True)
     return call(
         add_kernel,
         shape((length, width)),
         attn,
-        back,
+        weighted,
         sel_row,
         scratch=[pltpu.VMEM((8 * SLOTS, LANES), F32), pltpu.VMEM((LANES, width), F32)],
         name="add",

time: 589 us -> 270 us (0.46)
  blocking collectives: 292 us -> 59.2 us
  waiting for transfers between devices: 190 us -> 69.2 us
  starting transfers between devices: 81 us -> 110 us
  Pallas kernels: 11.3 us -> 18.5 us
    all_to_all x1 -> x2, blocking collectives: 278 us -> 25.1 us  [the longest x1 14.6 us: body(): sums = lax.all_to_all(partial.reshape(8, units, 384), 'c', 0, 0, tiled=True)]
    all_to_all x1, waiting for transfers between devices: 41.8 us -> 0.01 us  [body(): before = lax.all_to_all(before, seq, 0, 0, tiled=True)]
    ppermute x3 -> x14, starting transfers between devices: 12.4 us -> 47.1 us  [exchange(): lax.ppermute(pieces[k], 'c', [(c, c ^ k) for c in range(count)])]
    all_to_all x3 -> x2, waiting for transfers between devices: 36.3 us -> 4.87 us  [the longest x1 4.87 us: body(): weighted = lax.all_to_all(weighted, 'p', 0, 0, tiled=True)]
    ppermute x3 -> x14, waiting for transfers between devices: 65.8 us -> 40.7 us  [exchange(): lax.ppermute(pieces[k], 'c', [(c, c ^ k) for c in range(count)])]
    all_gather x1, blocking collectives: 14.4 us -> 34.1 us  [body(): act = lax.all_gather(act, 'r', axis=0, tiled=True)]
    all_to_all x1, waiting for transfers between devices: 15.5 us -> 0.01 us  [body(): chunks = lax.all_to_all(state, seq, 0, 0, tiled=True)]
    all_to_all x1, starting transfers between devices: 17.8 us -> 6.82 us  [body(): back = lax.all_to_all(out, seq, 0, 0, tiled=True)]
  transfers between devices with their start and end apart: 9 -> 19, of which waited for: 7 -> 11; matrix products, arithmetic and copies ran while one was open for 1% -> 0% of each run, Pallas kernels for 1% -> 1%
where the time goes in v2:
time: 270 us; the launch traced here: 269 us
  starting transfers between devices  110 us (41%)
  waiting for transfers between devices  69.2 us (26%)
  blocking collectives  59.2 us (22%)
  Pallas kernels  18.5 us (7%)
  local copies, waits for them, and re-layouts  10.8 us (4%)
    ppermute x14, starting transfers between devices, exchange(): lax.ppermute(pieces[k], 'c', [(c, c ^ k) for c in range(count)])  47.1 us
    ppermute x14, waiting for transfers between devices, exchange(): lax.ppermute(pieces[k], 'c', [(c, c ^ k) for c in range(count)])  40.7 us
    all_gather x1, blocking collectives, body(): act = lax.all_gather(act, 'r', axis=0, tiled=True)  34.1 us
    all_to_all x1, waiting for transfers between devices, body(): back = lax.all_to_all(out, seq, 0, 0, tiled=True)  23.6 us
    all_to_all x1, starting transfers between devices, body(): chunks = lax.all_to_all(state, seq, 0, 0, tiled=True)  19.5 us
    pallas_call x11, Pallas kernels, call(): pl.pallas_call(kernel, out_shape=out, scratch_shapes=list(scratch), compi...  18.5 us
    all_to_all x1, blocking collectives, body(): sums = lax.all_to_all(partial.reshape(8, units, 384), 'c', 0, 0, tiled=True)  14.6 us
    all_to_all x1, starting transfers between devices, body(): weighted = lax.all_to_all(weighted, 'p', 0, 0, tiled=True)  13.2 us
  transfers between devices with their start and end apart: 19, of which 11 were waited for; matrix products, arithmetic and copies ran while one was open for 0% of the time, Pallas kernels for 1%

profile of v2, /device:TPU:1, one launch (start us, length us, event | category | flops | bytes accessed | tf_op | source)
XLA Modules:
  0.0 268.8 jit_solution(16887459429162097203)
XLA Ops:
  0.0 1.0 copy-done.2
  1.0 1.0 copy-done.4
  2.0 1.3 state.1
  3.3 19.5 %all-to-all-start = ((bf16[64,16,128]{2,1,0:T(8,128)(2,1)}), bf16[64,16,128]{2,1,0:T(8,128)(2,1)}, u32[]{:S(2)}, u32[]{:S(2)}) async-start(bf16[64,16,128]{2,1,0:T(8,128)(2,1)} %state.1), calls=%async_computation | async-start | bytes 524288 | tf_op jit(solution)/shard_map/all_to_all | solution.py:282
  22.8 1.5 copy-done
  24.7 3.1 %collective-permute-start = (bf16[144,768]{1,0:T(8,128)(2,1)S(1)}, bf16[144,768]{1,0:T(8,128)(2,1)S(1)}, u32[]{:S(2)}, u32[]{:S(2)}) collective-permute-start(bf16[144,768]{1,0:T(8,128)(2,1)S(1)} %get-tuple-element.59), channel_id=1, source_target_pairs={{0,8},{8,0},{16,24},{24,16},{32,40},{40,32},{48,56},{56,48},{1,9},... | collective-permute-start | bytes 663560 | tf_op jit(solution)/shard_map/ppermute | solution.py:254
  27.9 4.3 %collective-permute-start.1 = (bf16[144,768]{1,0:T(8,128)(2,1)S(1)}, bf16[144,768]{1,0:T(8,128)(2,1)S(1)}, u32[]{:S(2)}, u32[]{:S(2)}) collective-permute-start(bf16[144,768]{1,0:T(8,128)(2,1)S(1)} %get-tuple-element.60), channel_id=1, source_target_pairs={{0,16},{8,24},{16,0},{24,8},{32,48},{40,56},{48,32},{56,40},{1,17}... | collective-permute-start | bytes 663560 | tf_op jit(solution)/shard_map/ppermute | solution.py:254
  32.2 2.4 collective-permute-start.2
  34.6 2.8 %collective-permute-start.3 = (bf16[144,768]{1,0:T(8,128)(2,1)S(1)}, bf16[144,768]{1,0:T(8,128)(2,1)S(1)}, u32[]{:S(2)}, u32[]{:S(2)}) collective-permute-start(bf16[144,768]{1,0:T(8,128)(2,1)S(1)} %get-tuple-element.62), channel_id=1, source_target_pairs={{0,32},{8,40},{16,48},{24,56},{32,0},{40,8},{48,16},{56,24},{1,33}... | collective-permute-start | bytes 663560 | tf_op jit(solution)/shard_map/ppermute | solution.py:254
  37.5 0.9 inner.1.inner_ref
  39.1 2.5 collective-permute-done.1.refs_2_
  42.3 4.2 %collective-permute-done.2.refs_3_ = bf16[144,768]{1,0:T(8,128)(2,1)S(1)} collective-permute-done((bf16[144,768]{1,0:T(8,128)(2,1)S(1)}, bf16[144,768]{1,0:T(8,128)(2,1)S(1)}, u32[]{:S(2)}, u32[]{:S(2)}) %collective-permute-start.2) | collective-permute-done | bytes 221216 | tf_op jit(solution)/shard_map/ppermute | solution.py:254
  47.2 0.7 copy-done.16
  47.9 1.7 prefix.1
  49.6 11.9 %all-to-all-start.1 = ((bf16[64,16,128]{2,1,0:T(8,128)(2,1)}), bf16[64,16,128]{2,1,0:T(8,128)(2,1)S(1)}, u32[]{:S(2)}, u32[]{:S(2)}) async-start(bf16[64,16,128]{2,1,0:T(8,128)(2,1)} %prefix.1), calls=%async_computation.1 | async-start | bytes 524288 | tf_op jit(solution)/shard_map/all_to_all | solution.py:297
  61.6 3.8 %collective-permute-start.4 = (bf16[144,768]{1,0:T(8,128)(2,1)}, bf16[144,768]{1,0:T(8,128)(2,1)S(1)}, u32[]{:S(2)}, u32[]{:S(2)}) collective-permute-start(bf16[144,768]{1,0:T(8,128)(2,1)} %copy-done.32), channel_id=1, source_target_pairs={{0,40},{8,32},{16,56},{24,48},{32,8},{40,0},{48,24},{56,16},{1,41}... | collective-permute-start | bytes 663560 | tf_op jit(solution)/shard_map/ppermute | solution.py:254
  65.4 4.3 %collective-permute-start.5 = (bf16[144,768]{1,0:T(8,128)(2,1)}, bf16[144,768]{1,0:T(8,128)(2,1)}, u32[]{:S(2)}, u32[]{:S(2)}) collective-permute-start(bf16[144,768]{1,0:T(8,128)(2,1)} %copy-done.31), channel_id=1, source_target_pairs={{0,48},{8,56},{16,32},{24,40},{32,16},{40,24},{48,0},{56,8},{1,49}... | collective-permute-start | bytes 663560 | tf_op jit(solution)/shard_map/ppermute | solution.py:254
  69.7 3.1 %collective-permute-start.6 = (bf16[144,768]{1,0:T(8,128)(2,1)}, bf16[144,768]{1,0:T(8,128)(2,1)}, u32[]{:S(2)}, u32[]{:S(2)}) collective-permute-start(bf16[144,768]{1,0:T(8,128)(2,1)} %copy-done.29), channel_id=1, source_target_pairs={{0,56},{8,48},{16,40},{24,32},{32,24},{40,16},{48,8},{56,0},{1,57}... | collective-permute-start | bytes 663560 | tf_op jit(solution)/shard_map/ppermute | solution.py:254
  72.9 2.3 cut_down.1
  76.6 2.5 collective-permute-done.4.refs_5_
  79.2 6.6 %collective-permute-done.5.refs_6_ = bf16[144,768]{1,0:T(8,128)(2,1)} collective-permute-done((bf16[144,768]{1,0:T(8,128)(2,1)}, bf16[144,768]{1,0:T(8,128)(2,1)}, u32[]{:S(2)}, u32[]{:S(2)}) %collective-permute-start.5) | collective-permute-done | bytes 221216 | tf_op jit(solution)/shard_map/ppermute | solution.py:254
  85.8 4.8 %collective-permute-done.6.refs_7_ = bf16[144,768]{1,0:T(8,128)(2,1)} collective-permute-done((bf16[144,768]{1,0:T(8,128)(2,1)}, bf16[144,768]{1,0:T(8,128)(2,1)}, u32[]{:S(2)}, u32[]{:S(2)}) %collective-permute-start.6) | collective-permute-done | bytes 221216 | tf_op jit(solution)/shard_map/ppermute | solution.py:254
  90.6 1.1 attn.1
  91.7 10.5 %all_to_all.35.row_ref = bf16[8,32,128]{2,1,0:T(8,128)(2,1)S(1)} all-to-all(bf16[8,32,128]{2,1,0:T(8,128)(2,1)S(1)} %get-tuple-element.84), channel_id=1, replica_groups=mesh['r'=8,'c'=8,'p'=8] {'p'}, dimensions={0} | all-to-all | bytes 131072 | tf_op jit(solution)/shard_map/all_to_all | solution.py:325
  102.2 0.9 tile.19
  103.1 11.9 %all-to-all-start.3 = ((bf16[64,32,128]{2,1,0:T(8,128)(2,1)}), bf16[64,32,128]{2,1,0:T(8,128)(2,1)S(1)}, u32[]{:S(2)}, u32[]{:S(2)}) async-start(bf16[64,32,128]{2,1,0:T(8,128)(2,1)} %bitcast.6), calls=%async_computation.3 | async-start | bytes 1048576 | tf_op jit(solution)/shard_map/all_to_all | solution.py:326
  115.0 2.9 %collective-permute-start.7 = (bf16[96,1152]{1,0:T(8,128)(2,1)}, bf16[96,1152]{1,0:T(8,128)(2,1)S(1)}, u32[]{:S(2)}, u32[]{:S(2)}) collective-permute-start(bf16[96,1152]{1,0:T(8,128)(2,1)} %get-tuple-element.85), channel_id=1, source_target_pairs={{0,8},{8,0},{16,24},{24,16},{32,40},{40,32},{48,56},{56,48},{1,9},... | collective-permute-start | bytes 663560 | tf_op jit(solution)/shard_map/ppermute | solution.py:254
  117.9 4.3 %collective-permute-start.8 = (bf16[96,1152]{1,0:T(8,128)(2,1)}, bf16[96,1152]{1,0:T(8,128)(2,1)S(1)}, u32[]{:S(2)}, u32[]{:S(2)}) collective-permute-start(bf16[96,1152]{1,0:T(8,128)(2,1)} %get-tuple-element.86), channel_id=1, source_target_pairs={{0,16},{8,24},{16,0},{24,8},{32,48},{40,56},{48,32},{56,40},{1,17}... | collective-permute-start | bytes 663560 | tf_op jit(solution)/shard_map/ppermute | solution.py:254
  122.3 2.4 collective-permute-start.9
  124.6 2.9 %collective-permute-start.10 = (bf16[96,1152]{1,0:T(8,128)(2,1)}, bf16[96,1152]{1,0:T(8,128)(2,1)S(1)}, u32[]{:S(2)}, u32[]{:S(2)}) collective-permute-start(bf16[96,1152]{1,0:T(8,128)(2,1)} %copy-done.30), channel_id=1, source_target_pairs={{0,32},{8,40},{16,48},{24,56},{32,0},{40,8},{48,16},{56,24},{1,33}... | collective-permute-start | bytes 663560 | tf_op jit(solution)/shard_map/ppermute | solution.py:254
  127.5 1.9 collective-permute-start.11
  129.5 6.4 %collective-permute-start.12 = (bf16[96,1152]{1,0:T(8,128)(2,1)}, bf16[96,1152]{1,0:T(8,128)(2,1)S(1)}, u32[]{:S(2)}, u32[]{:S(2)}) collective-permute-start(bf16[96,1152]{1,0:T(8,128)(2,1)} %copy-done.27), channel_id=1, source_target_pairs={{0,48},{8,56},{16,32},{24,40},{32,16},{40,24},{48,0},{56,8},{1,49}... | collective-permute-start | bytes 663560 | tf_op jit(solution)/shard_map/ppermute | solution.py:254
  135.9 2.4 collective-permute-start.13
  138.3 4.8 %collective-permute-done.10.refs_4_ = bf16[96,1152]{1,0:T(8,128)(2,1)S(1)} collective-permute-done((bf16[96,1152]{1,0:T(8,128)(2,1)}, bf16[96,1152]{1,0:T(8,128)(2,1)S(1)}, u32[]{:S(2)}, u32[]{:S(2)}) %collective-permute-start.10) | collective-permute-done | bytes 221216 | tf_op jit(solution)/shard_map/ppermute | solution.py:254
  143.1 5.7 %collective-permute-done.11.refs_5_ = bf16[96,1152]{1,0:T(8,128)(2,1)S(1)} collective-permute-done((bf16[96,1152]{1,0:T(8,128)(2,1)}, bf16[96,1152]{1,0:T(8,128)(2,1)S(1)}, u32[]{:S(2)}, u32[]{:S(2)}) %collective-permute-start.11) | collective-permute-done | bytes 221216 | tf_op jit(solution)/shard_map/ppermute | solution.py:254
  149.5 5.5 %collective-permute-done.12.refs_6_ = bf16[96,1152]{1,0:T(8,128)(2,1)S(1)} collective-permute-done((bf16[96,1152]{1,0:T(8,128)(2,1)}, bf16[96,1152]{1,0:T(8,128)(2,1)S(1)}, u32[]{:S(2)}, u32[]{:S(2)}) %collective-permute-start.12) | collective-permute-done | bytes 221216 | tf_op jit(solution)/shard_map/ppermute | solution.py:254
  155.0 0.7 copy-done.22
  155.7 4.1 %collective-permute-done.13.refs_7_ = bf16[96,1152]{1,0:T(8,128)(2,1)S(1)} collective-permute-done((bf16[96,1152]{1,0:T(8,128)(2,1)}, bf16[96,1152]{1,0:T(8,128)(2,1)S(1)}, u32[]{:S(2)}, u32[]{:S(2)}) %collective-permute-start.13) | collective-permute-done | bytes 221216 | tf_op jit(solution)/shard_map/ppermute | solution.py:254
  160.5 4.0 %up.1 = bf16[1152,384]{1,0:T(8,128)(2,1)S(1)} custom-call(s32[1]{0:T(128)} %bitcast.place_ref, bf16[64,32,128]{2,1,0:T(8,128)(2,1)S(1)} %all-to-all-done.3.x_ref, bf16[144,768]{1,0:T(8,128)(2,1)S(1)} %copy-done.9, bf16[144,768]{1,0:T(8,128)(2,1)S(1)} %copy-done.11, bf16[144,768]{1,0:T(8,128)(2,1)S(1)} %copy-done.13, bf16[144,768]{1,0:T(8,128)(2,1)S(1)} %copy-done.15, ...), custom_call_target="tpu_custom_call" | custom-call | tf_op jit(solution)/shard_map/up/pallas_call | solution.py:31
  164.5 14.6 %all_to_all.36.in_ref = bf16[8,144,384]{2,1,0:T(8,128)(2,1)S(1)} all-to-all(bf16[8,144,384]{2,1,0:T(8,128)(2,1)S(1)} %bitcast.13), channel_id=1, replica_groups=mesh['r'=8,'c'=8,'p'=8] {'c'}, dimensions={0} | all-to-all | bytes 1769472 | tf_op jit(solution)/shard_map/all_to_all | solution.py:345
  179.3 34.1 %all_gather.3.h_ref = bf16[1152,384]{1,0:T(8,128)(2,1)S(1)} all-gather(bf16[144,384]{1,0:T(8,128)(2,1)S(1)} %act.1), channel_id=1, replica_groups=mesh['r'=8,'c'=8,'p'=8] {'r'}, dimensions={0}, use_global_device_ids=true | all-gather | bytes 995328 | tf_op jit(solution)/shard_map/all_gather | solution.py:347
  213.4 4.8 %down.1 = bf16[64,32,128]{2,1,0:T(8,128)(2,1)} custom-call(s32[1]{0:T(128)} %bitcast.place_ref, bf16[1152,384]{1,0:T(8,128)(2,1)S(1)} %all_gather.3.h_ref, bf16[96,1152]{1,0:T(8,128)(2,1)S(1)} %copy-done.19, bf16[96,1152]{1,0:T(8,128)(2,1)S(1)} %collective-permute-done.7.refs_1_, bf16[96,1152]{1,0:T(8,128)(2,1)S(1)} %collective-permute-done.8.refs_2_, ...), custom_call_target="tpu_custom_call" | custom-call | tf_op jit(solution)/shard_map/down/pallas_call | solution.py:31
  218.2 6.8 %all-to-all-start.5 = ((bf16[64,32,128]{2,1,0:T(8,128)(2,1)}), bf16[64,32,128]{2,1,0:T(8,128)(2,1)S(1)}, u32[]{:S(2)}, u32[]{:S(2)}) async-start(bf16[64,32,128]{2,1,0:T(8,128)(2,1)} %down.1), calls=%async_computation.5 | async-start | bytes 1048576 | tf_op jit(solution)/shard_map/all_to_all | solution.py:363
  225.2 23.6 %all-to-all-done.5.y_ref = bf16[64,32,128]{2,1,0:T(8,128)(2,1)S(1)} async-done(((bf16[64,32,128]{2,1,0:T(8,128)(2,1)}), bf16[64,32,128]{2,1,0:T(8,128)(2,1)S(1)}, u32[]{:S(2)}, u32[]{:S(2)}) %all-to-all-start.5) | async-done | bytes 524320 | tf_op jit(solution)/shard_map/all_to_all | solution.py:363
  248.8 0.9 weigh.1
  249.7 13.2 %all-to-all-start.6 = ((bf16[8,32,128]{2,1,0:T(8,128)(2,1)}), bf16[8,32,128]{2,1,0:T(8,128)(2,1)S(1)}, u32[]{:S(2)}, u32[]{:S(2)}) async-start(bf16[8,32,128]{2,1,0:T(8,128)(2,1)} %weigh.1), calls=%async_computation.6 | async-start | bytes 131072 | tf_op jit(solution)/shard_map/all_to_all | solution.py:367
  262.9 4.9 %all-to-all-done.6.y_ref = bf16[8,32,128]{2,1,0:T(8,128)(2,1)S(1)} async-done(((bf16[8,32,128]{2,1,0:T(8,128)(2,1)}), bf16[8,32,128]{2,1,0:T(8,128)(2,1)S(1)}, u32[]{:S(2)}, u32[]{:S(2)}) %all-to-all-start.6) | async-done | bytes 65568 | tf_op jit(solution)/shard_map/all_to_all | solution.py:367
  267.8 1.0 add.6
  (85 shorter events, 5.7 us)
Async XLA Ops:
  0.0 1.0 copy-start.2
  1.0 1.0 copy-start.4
  2.0 35.5 %copy-start.3 = (bf16[256,768]{1,0:T(8,128)(2,1)S(1)}, bf16[256,768]{1,0:T(8,128)(2,1)}, u32[]{:S(2)}) copy-start(bf16[256,768]{1,0:T(8,128)(2,1)} %k_ref.3) | copy-start | bytes 1179652
  2.0 35.5 %copy-start.5 = (bf16[256,768]{1,0:T(8,128)(2,1)S(1)}, bf16[256,768]{1,0:T(8,128)(2,1)}, u32[]{:S(2)}) copy-start(bf16[256,768]{1,0:T(8,128)(2,1)} %v_ref.3) | copy-start | bytes 1179652
  3.3 44.7 %all-to-all-start = ((bf16[64,16,128]{2,1,0:T(8,128)(2,1)}), bf16[64,16,128]{2,1,0:T(8,128)(2,1)}, u32[]{:S(2)}, u32[]{:S(2)}) async-start(bf16[64,16,128]{2,1,0:T(8,128)(2,1)} %state.1), calls=%async_computation | async-start | bytes 524288 | tf_op jit(solution)/shard_map/all_to_all | solution.py:282
  22.8 1.5 copy-start
  24.3 13.2 %copy-start.6 = (bf16[256,768]{1,0:T(8,128)(2,1)S(1)}, bf16[256,768]{1,0:T(8,128)(2,1)}, u32[]{:S(2)}) copy-start(bf16[256,768]{1,0:T(8,128)(2,1)} %q_ref.3) | copy-start | bytes 1179652
  24.7 13.8 %copy-start.8 = (bf16[144,768]{1,0:T(8,128)(2,1)}, bf16[144,768]{1,0:T(8,128)(2,1)S(1)}, u32[]{:S(2)}) copy-start(bf16[144,768]{1,0:T(8,128)(2,1)S(1)} %get-tuple-element.93.refs_0_) | copy-start | bytes 663556
  24.7 21.8 %copy-start.29 = (bf16[144,768]{1,0:T(8,128)(2,1)}, bf16[144,768]{1,0:T(8,128)(2,1)S(1)}, u32[]{:S(2)}) copy-start(bf16[144,768]{1,0:T(8,128)(2,1)S(1)} %get-tuple-element.72) | copy-start | bytes 663556
  24.7 21.8 %copy-start.31 = (bf16[144,768]{1,0:T(8,128)(2,1)}, bf16[144,768]{1,0:T(8,128)(2,1)S(1)}, u32[]{:S(2)}) copy-start(bf16[144,768]{1,0:T(8,128)(2,1)S(1)} %get-tuple-element.71) | copy-start | bytes 663556
  24.7 21.8 %copy-start.32 = (bf16[144,768]{1,0:T(8,128)(2,1)}, bf16[144,768]{1,0:T(8,128)(2,1)S(1)}, u32[]{:S(2)}) copy-start(bf16[144,768]{1,0:T(8,128)(2,1)S(1)} %get-tuple-element.70) | copy-start | bytes 663556
  24.7 48.1 %copy-start.34 = (s32[1,8,5]{1,0,2:T(1,128)S(1)}, s32[1,8,5]{1,0,2:T(1,128)}, u32[]{:S(2)}) copy-start(s32[1,8,5]{1,0,2:T(1,128)} %param.10) | copy-start | bytes 484
  24.7 48.2 %copy-start.1 = (bf16[1,96,9216]{2,1,0:T(8,128)(2,1)S(1)}, bf16[1,96,9216]{2,1,0:T(8,128)(2,1)}, u32[]{:S(2)}) copy-start(bf16[1,96,9216]{2,1,0:T(8,128)(2,1)} %param.13) | copy-start | bytes 5308420
  24.7 13.7 %collective-permute-start = (bf16[144,768]{1,0:T(8,128)(2,1)S(1)}, bf16[144,768]{1,0:T(8,128)(2,1)S(1)}, u32[]{:S(2)}, u32[]{:S(2)}) collective-permute-start(bf16[144,768]{1,0:T(8,128)(2,1)S(1)} %get-tuple-element.59), channel_id=1, source_target_pairs={{0,8},{8,0},{16,24},{24,16},{32,40},{40,32},{48,56},{56,48},{1,9},... | collective-permute-start | bytes 663560 | tf_op jit(solution)/shard_map/ppermute | solution.py:254
  27.9 13.8 %collective-permute-start.1 = (bf16[144,768]{1,0:T(8,128)(2,1)S(1)}, bf16[144,768]{1,0:T(8,128)(2,1)S(1)}, u32[]{:S(2)}, u32[]{:S(2)}) collective-permute-start(bf16[144,768]{1,0:T(8,128)(2,1)S(1)} %get-tuple-element.60), channel_id=1, source_target_pairs={{0,16},{8,24},{16,0},{24,8},{32,48},{40,56},{48,32},{56,40},{1,17}... | collective-permute-start | bytes 663560 | tf_op jit(solution)/shard_map/ppermute | solution.py:254
  32.2 14.4 %collective-permute-start.2 = (bf16[144,768]{1,0:T(8,128)(2,1)S(1)}, bf16[144,768]{1,0:T(8,128)(2,1)S(1)}, u32[]{:S(2)}, u32[]{:S(2)}) collective-permute-start(bf16[144,768]{1,0:T(8,128)(2,1)S(1)} %get-tuple-element.61), channel_id=1, source_target_pairs={{0,24},{8,16},{16,8},{24,0},{32,56},{40,48},{48,40},{56,32},{1,25}... | collective-permute-start | bytes 663560 | tf_op jit(solution)/shard_map/ppermute | solution.py:254
  34.6 12.6 %collective-permute-start.3 = (bf16[144,768]{1,0:T(8,128)(2,1)S(1)}, bf16[144,768]{1,0:T(8,128)(2,1)S(1)}, u32[]{:S(2)}, u32[]{:S(2)}) collective-permute-start(bf16[144,768]{1,0:T(8,128)(2,1)S(1)} %get-tuple-element.62), channel_id=1, source_target_pairs={{0,32},{8,40},{16,48},{24,56},{32,0},{40,8},{48,16},{56,24},{1,33}... | collective-permute-start | bytes 663560 | tf_op jit(solution)/shard_map/ppermute | solution.py:254
  38.5 52.1 %copy-start.7 = (bf16[256,768]{1,0:T(8,128)(2,1)S(1)}, bf16[256,768]{1,0:T(8,128)(2,1)}, u32[]{:S(2)}) copy-start(bf16[256,768]{1,0:T(8,128)(2,1)} %q_ref.3) | copy-start | bytes 1179652
  46.5 0.7 copy-start.14
  47.2 0.7 copy-start.16
  49.6 40.9 %all-to-all-start.1 = ((bf16[64,16,128]{2,1,0:T(8,128)(2,1)}), bf16[64,16,128]{2,1,0:T(8,128)(2,1)S(1)}, u32[]{:S(2)}, u32[]{:S(2)}) async-start(bf16[64,16,128]{2,1,0:T(8,128)(2,1)} %prefix.1), calls=%async_computation.1 | async-start | bytes 524288 | tf_op jit(solution)/shard_map/all_to_all | solution.py:297
  61.6 17.6 %collective-permute-start.4 = (bf16[144,768]{1,0:T(8,128)(2,1)}, bf16[144,768]{1,0:T(8,128)(2,1)S(1)}, u32[]{:S(2)}, u32[]{:S(2)}) collective-permute-start(bf16[144,768]{1,0:T(8,128)(2,1)} %copy-done.32), channel_id=1, source_target_pairs={{0,40},{8,32},{16,56},{24,48},{32,8},{40,0},{48,24},{56,16},{1,41}... | collective-permute-start | bytes 663560 | tf_op jit(solution)/shard_map/ppermute | solution.py:254
  65.4 20.3 %collective-permute-start.5 = (bf16[144,768]{1,0:T(8,128)(2,1)}, bf16[144,768]{1,0:T(8,128)(2,1)}, u32[]{:S(2)}, u32[]{:S(2)}) collective-permute-start(bf16[144,768]{1,0:T(8,128)(2,1)} %copy-done.31), channel_id=1, source_target_pairs={{0,48},{8,56},{16,32},{24,40},{32,16},{40,24},{48,0},{56,8},{1,49}... | collective-permute-start | bytes 663560 | tf_op jit(solution)/shard_map/ppermute | solution.py:254
  69.7 20.9 %collective-permute-start.6 = (bf16[144,768]{1,0:T(8,128)(2,1)}, bf16[144,768]{1,0:T(8,128)(2,1)}, u32[]{:S(2)}, u32[]{:S(2)}) collective-permute-start(bf16[144,768]{1,0:T(8,128)(2,1)} %copy-done.29), channel_id=1, source_target_pairs={{0,56},{8,48},{16,40},{24,32},{32,24},{40,16},{48,8},{56,0},{1,57}... | collective-permute-start | bytes 663560 | tf_op jit(solution)/shard_map/ppermute | solution.py:254
  76.6 9.2 %copy-start.26 = (bf16[96,1152]{1,0:T(8,128)(2,1)}, bf16[96,1152]{1,0:T(8,128)(2,1)S(1)}, u32[]{:S(2)}) copy-start(bf16[96,1152]{1,0:T(8,128)(2,1)S(1)} %get-tuple-element.91) | copy-start | bytes 663556
  76.6 9.2 %copy-start.27 = (bf16[96,1152]{1,0:T(8,128)(2,1)}, bf16[96,1152]{1,0:T(8,128)(2,1)S(1)}, u32[]{:S(2)}) copy-start(bf16[96,1152]{1,0:T(8,128)(2,1)S(1)} %get-tuple-element.90) | copy-start | bytes 663556
  76.6 9.2 %copy-start.28 = (bf16[96,1152]{1,0:T(8,128)(2,1)}, bf16[96,1152]{1,0:T(8,128)(2,1)S(1)}, u32[]{:S(2)}) copy-start(bf16[96,1152]{1,0:T(8,128)(2,1)S(1)} %get-tuple-element.89) | copy-start | bytes 663556
  76.6 83.8 %copy-start.9 = (bf16[144,768]{1,0:T(8,128)(2,1)S(1)}, bf16[144,768]{1,0:T(8,128)(2,1)}, u32[]{:S(2)}) copy-start(bf16[144,768]{1,0:T(8,128)(2,1)} %copy-done.8) | copy-start | bytes 663556
  76.6 83.8 %copy-start.11 = (bf16[144,768]{1,0:T(8,128)(2,1)S(1)}, bf16[144,768]{1,0:T(8,128)(2,1)}, u32[]{:S(2)}) copy-start(bf16[144,768]{1,0:T(8,128)(2,1)} %copy-done.10) | copy-start | bytes 663556
  76.6 83.8 %copy-start.13 = (bf16[144,768]{1,0:T(8,128)(2,1)S(1)}, bf16[144,768]{1,0:T(8,128)(2,1)}, u32[]{:S(2)}) copy-start(bf16[144,768]{1,0:T(8,128)(2,1)} %copy-done.12) | copy-start | bytes 663556
  76.6 83.8 %copy-start.15 = (bf16[144,768]{1,0:T(8,128)(2,1)S(1)}, bf16[144,768]{1,0:T(8,128)(2,1)}, u32[]{:S(2)}) copy-start(bf16[144,768]{1,0:T(8,128)(2,1)} %copy-done.14) | copy-start | bytes 663556
  76.6 83.8 %copy-start.17 = (bf16[144,768]{1,0:T(8,128)(2,1)S(1)}, bf16[144,768]{1,0:T(8,128)(2,1)}, u32[]{:S(2)}) copy-start(bf16[144,768]{1,0:T(8,128)(2,1)} %copy-done.16) | copy-start | bytes 663556
  103.1 57.4 %all-to-all-start.3 = ((bf16[64,32,128]{2,1,0:T(8,128)(2,1)}), bf16[64,32,128]{2,1,0:T(8,128)(2,1)S(1)}, u32[]{:S(2)}, u32[]{:S(2)}) async-start(bf16[64,32,128]{2,1,0:T(8,128)(2,1)} %bitcast.6), calls=%async_computation.3 | async-start | bytes 1048576 | tf_op jit(solution)/shard_map/all_to_all | solution.py:326
  115.0 14.5 %collective-permute-start.7 = (bf16[96,1152]{1,0:T(8,128)(2,1)}, bf16[96,1152]{1,0:T(8,128)(2,1)S(1)}, u32[]{:S(2)}, u32[]{:S(2)}) collective-permute-start(bf16[96,1152]{1,0:T(8,128)(2,1)} %get-tuple-element.85), channel_id=1, source_target_pairs={{0,8},{8,0},{16,24},{24,16},{32,40},{40,32},{48,56},{56,48},{1,9},... | collective-permute-start | bytes 663560 | tf_op jit(solution)/shard_map/ppermute | solution.py:254
  117.9 17.9 %collective-permute-start.8 = (bf16[96,1152]{1,0:T(8,128)(2,1)}, bf16[96,1152]{1,0:T(8,128)(2,1)S(1)}, u32[]{:S(2)}, u32[]{:S(2)}) collective-permute-start(bf16[96,1152]{1,0:T(8,128)(2,1)} %get-tuple-element.86), channel_id=1, source_target_pairs={{0,16},{8,24},{16,0},{24,8},{32,48},{40,56},{48,32},{56,40},{1,17}... | collective-permute-start | bytes 663560 | tf_op jit(solution)/shard_map/ppermute | solution.py:254
  122.3 16.0 %collective-permute-start.9 = (bf16[96,1152]{1,0:T(8,128)(2,1)}, bf16[96,1152]{1,0:T(8,128)(2,1)S(1)}, u32[]{:S(2)}, u32[]{:S(2)}) collective-permute-start(bf16[96,1152]{1,0:T(8,128)(2,1)} %get-tuple-element.87), channel_id=1, source_target_pairs={{0,24},{8,16},{16,8},{24,0},{32,56},{40,48},{48,40},{56,32},{1,25}... | collective-permute-start | bytes 663560 | tf_op jit(solution)/shard_map/ppermute | solution.py:254
  124.6 18.5 %collective-permute-start.10 = (bf16[96,1152]{1,0:T(8,128)(2,1)}, bf16[96,1152]{1,0:T(8,128)(2,1)S(1)}, u32[]{:S(2)}, u32[]{:S(2)}) collective-permute-start(bf16[96,1152]{1,0:T(8,128)(2,1)} %copy-done.30), channel_id=1, source_target_pairs={{0,32},{8,40},{16,48},{24,56},{32,0},{40,8},{48,16},{56,24},{1,33}... | collective-permute-start | bytes 663560 | tf_op jit(solution)/shard_map/ppermute | solution.py:254
  127.5 21.3 %collective-permute-start.11 = (bf16[96,1152]{1,0:T(8,128)(2,1)}, bf16[96,1152]{1,0:T(8,128)(2,1)S(1)}, u32[]{:S(2)}, u32[]{:S(2)}) collective-permute-start(bf16[96,1152]{1,0:T(8,128)(2,1)} %copy-done.28), channel_id=1, source_target_pairs={{0,40},{8,32},{16,56},{24,48},{32,8},{40,0},{48,24},{56,16},{1,41}... | collective-permute-start | bytes 663560 | tf_op jit(solution)/shard_map/ppermute | solution.py:254
  129.5 25.5 %collective-permute-start.12 = (bf16[96,1152]{1,0:T(8,128)(2,1)}, bf16[96,1152]{1,0:T(8,128)(2,1)S(1)}, u32[]{:S(2)}, u32[]{:S(2)}) collective-permute-start(bf16[96,1152]{1,0:T(8,128)(2,1)} %copy-done.27), channel_id=1, source_target_pairs={{0,48},{8,56},{16,32},{24,40},{32,16},{40,24},{48,0},{56,8},{1,49}... | collective-permute-start | bytes 663560 | tf_op jit(solution)/shard_map/ppermute | solution.py:254
  135.9 23.9 %collective-permute-start.13 = (bf16[96,1152]{1,0:T(8,128)(2,1)}, bf16[96,1152]{1,0:T(8,128)(2,1)S(1)}, u32[]{:S(2)}, u32[]{:S(2)}) collective-permute-start(bf16[96,1152]{1,0:T(8,128)(2,1)} %copy-done.26), channel_id=1, source_target_pairs={{0,56},{8,48},{16,40},{24,32},{32,24},{40,16},{48,8},{56,0},{1,57}... | collective-permute-start | bytes 663560 | tf_op jit(solution)/shard_map/ppermute | solution.py:254
  155.0 0.7 copy-start.22
  164.5 48.9 %copy-start.19 = (bf16[96,1152]{1,0:T(8,128)(2,1)S(1)}, bf16[96,1152]{1,0:T(8,128)(2,1)}, u32[]{:S(2)}) copy-start(bf16[96,1152]{1,0:T(8,128)(2,1)} %copy-done.18) | copy-start | bytes 663556
  164.5 48.9 %copy-start.21 = (bf16[96,1152]{1,0:T(8,128)(2,1)S(1)}, bf16[96,1152]{1,0:T(8,128)(2,1)}, u32[]{:S(2)}) copy-start(bf16[96,1152]{1,0:T(8,128)(2,1)} %copy-done.20) | copy-start | bytes 663556
  164.5 48.9 %copy-start.23 = (bf16[96,1152]{1,0:T(8,128)(2,1)S(1)}, bf16[96,1152]{1,0:T(8,128)(2,1)}, u32[]{:S(2)}) copy-start(bf16[96,1152]{1,0:T(8,128)(2,1)} %copy-done.22) | copy-start | bytes 663556
  164.5 48.9 %copy-start.25 = (bf16[96,1152]{1,0:T(8,128)(2,1)S(1)}, bf16[96,1152]{1,0:T(8,128)(2,1)}, u32[]{:S(2)}) copy-start(bf16[96,1152]{1,0:T(8,128)(2,1)} %copy-done.24) | copy-start | bytes 663556
  213.4 11.7 %copy-start.33 = (bf16[6144,1]{0,1:T(2,128)(2,1)S(1)}, bf16[6144,1]{0,1:T(2,128)(2,1)}, u32[]{:S(2)}) copy-start(bf16[6144,1]{0,1:T(2,128)(2,1)} %param.11) | copy-start | bytes 36868
  218.2 30.7 %all-to-all-start.5 = ((bf16[64,32,128]{2,1,0:T(8,128)(2,1)}), bf16[64,32,128]{2,1,0:T(8,128)(2,1)S(1)}, u32[]{:S(2)}, u32[]{:S(2)}) async-start(bf16[64,32,128]{2,1,0:T(8,128)(2,1)} %down.1), calls=%async_computation.5 | async-start | bytes 1048576 | tf_op jit(solution)/shard_map/all_to_all | solution.py:363
  249.7 18.1 %all-to-all-start.6 = ((bf16[8,32,128]{2,1,0:T(8,128)(2,1)}), bf16[8,32,128]{2,1,0:T(8,128)(2,1)S(1)}, u32[]{:S(2)}, u32[]{:S(2)}) async-start(bf16[8,32,128]{2,1,0:T(8,128)(2,1)} %weigh.1), calls=%async_computation.6 | async-start | bytes 131072 | tf_op jit(solution)/shard_map/all_to_all | solution.py:367
  (6 other events, 4.1 us)

commit v3 on v2

--- a/solution.py
+++ b/solution.py
@@ -289,13 +289,13 @@
         spaces=([SMEM, HBM], [HBM] * 8),
         name="cut_up",
     )
-    up_first = exchange(up_pieces, 1, 5)
+    up_first = exchange(up_pieces, 1, 3)
     inner = call(inner_kernel, shape((length, width), F32), queries, keys, values, name="inner")
     chunks, inner, up_first = lax.optimization_barrier((chunks, inner, up_first))
     before = call(prefix_kernel, shape((64, 16, LANES)), chunks, name="prefix")
     w_down, up_pieces, before = lax.optimization_barrier((w_down, up_pieces, before))
     before = lax.all_to_all(before, seq, 0, 0, tiled=True)
-    up_last = exchange(up_pieces, 5, 8)
+    up_next = exchange(up_pieces, 3, 6)
     down_pieces = call(
         cut_down_kernel,
         [shape((columns, group))] * 8,
@@ -305,8 +305,9 @@
         spaces=([SMEM, VMEM], [HBM] * 8),
         name="cut_down",
     )
-    before, up_last, down_pieces = lax.optimization_barrier((before, up_last, down_pieces))
-    down_moved = exchange(down_pieces, 1, 8)
+    before, up_next, up_pieces, down_pieces = lax.optimization_barrier(
+        (before, up_next, up_pieces, down_pieces)
+    )
     attn, pay = call(
         attn_kernel,
         (shape((length, width)), shape((8, SLOTS, LANES))),
@@ -322,9 +323,16 @@
         ],
         name="attn",
     )
+    up_pieces, down_pieces, pay = lax.optimization_barrier((up_pieces, down_pieces, pay))
+    up_cross = exchange(up_pieces, 6, 7)
     whole_rows = lax.all_to_all(pay, "p", 0, 0, tiled=True)
+    whole_rows, up_cross, up_pieces, down_pieces = lax.optimization_barrier(
+        (whole_rows, up_cross, up_pieces, down_pieces)
+    )
+    up_last = exchange(up_pieces, 7, 8)
+    down_first = exchange(down_pieces, 1, 5)
     arrived = lax.all_to_all(jnp.tile(whole_rows, (8, 1, 1)), seq, 0, 0, tiled=True)
-    arrived, down_moved = lax.optimization_barrier((arrived, down_moved))
+    arrived, up_last, down_first = lax.optimization_barrier((arrived, up_last, down_first))
     partial = call(
         up_kernel,
         shape((8 * units, 384)),
@@ -332,6 +340,8 @@
         arrived,
         up_pieces[0],
         *up_first,
+        *up_next,
+        *up_cross,
         *up_last,
         scratch=[
             pltpu.VMEM((64 * SLOTS, LANES), F32),
@@ -342,7 +352,10 @@
         spaces=([SMEM, VMEM] + [HBM] * 8, VMEM),
         name="up",
     )
+    partial, down_pieces = lax.optimization_barrier((partial, down_pieces))
+    down_last = exchange(down_pieces, 5, 8)
     sums = lax.all_to_all(partial.reshape(8, units, 384), "c", 0, 0, tiled=True)
+    sums, down_last = lax.optimization_barrier((sums, down_last))
     act = call(act_kernel, shape((units, 384)), sums, name="act")
     act = lax.all_gather(act, "r", axis=0, tiled=True)
     out = call(
@@ -351,7 +364,8 @@
         place,
         act,
         down_pieces[0],
-        *down_moved,
+        *down_first,
+        *down_last,
         scratch=[
             pltpu.VMEM((64 * SLOTS, LANES), F32),
             pltpu.VMEM((8 * columns, group), BF16),

time: 270 us -> 269 us (level)
  blocking collectives: 59.2 us -> 46.4 us
  waiting for transfers between devices: 69.2 us -> 81.1 us
  local copies, waits for them, and re-layouts: 10.8 us -> 6.72 us
  starting transfers between devices: 110 us -> 114 us
    all_to_all x1 -> x0, blocking collectives: 14.6 us -> none  [body(): sums = lax.all_to_all(partial.reshape(8, units, 384), 'c', 0, 0, tiled=True)]
    ppermute x14, waiting for transfers between devices: 40.7 us -> 48.7 us  [exchange(): lax.ppermute(pieces[k], 'c', [(c, c ^ k) for c in range(count)])]
    unnamed x70 -> x48, local copies, waits for them, and re-layouts: 9.71 us -> 5.61 us
    all_to_all x1, waiting for transfers between devices: 23.6 us -> 27.5 us  [body(): back = lax.all_to_all(out, seq, 0, 0, tiled=True)]
    all_to_all x1, starting transfers between devices: 13.2 us -> 9.25 us  [body(): weighted = lax.all_to_all(weighted, 'p', 0, 0, tiled=True)]
    all_to_all x0 -> x1, starting transfers between devices: none -> 3.82 us  [body(): sums = lax.all_to_all(partial.reshape(8, units, 384), 'c', 0, 0, tiled=True)]
    ppermute x14, starting transfers between devices: 47.1 us -> 50.3 us  [exchange(): lax.ppermute(pieces[k], 'c', [(c, c ^ k) for c in range(count)])]
  transfers between devices with their start and end apart: 19 -> 20, of which waited for: 11 -> 12; matrix products, arithmetic and copies ran while one was open for 0% -> 0% of each run, Pallas kernels for 1% -> 2%
where the time goes in v3:
time: 269 us; the launch traced here: 268 us
  starting transfers between devices  114 us (42%)
  waiting for transfers between devices  81.1 us (30%)
  blocking collectives  46.4 us (17%)
  Pallas kernels  19.4 us (7%)
  local copies, waits for them, and re-layouts  6.72 us (2%)
    ppermute x14, starting transfers between devices, exchange(): lax.ppermute(pieces[k], 'c', [(c, c ^ k) for c in range(count)])  50.3 us
    ppermute x14, waiting for transfers between devices, exchange(): lax.ppermute(pieces[k], 'c', [(c, c ^ k) for c in range(count)])  48.7 us
    all_gather x1, blocking collectives, body(): act = lax.all_gather(act, 'r', axis=0, tiled=True)  35.9 us
    all_to_all x1, waiting for transfers between devices, body(): back = lax.all_to_all(out, seq, 0, 0, tiled=True)  27.5 us
    all_to_all x1, starting transfers between devices, body(): chunks = lax.all_to_all(state, seq, 0, 0, tiled=True)  19.5 us
    pallas_call x11, Pallas kernels, call(): pl.pallas_call(kernel, out_shape=out, scratch_shapes=list(scratch), compi...  19.4 us
    all_to_all x1, starting transfers between devices, body(): before = lax.all_to_all(before, seq, 0, 0, tiled=True)  12.3 us
    all_to_all x1, starting transfers between devices, body(): lax.all_to_all(jnp.tile(whole_rows, (8, 1, 1)), seq, 0, 0, tiled=True)  11.6 us
  transfers between devices with their start and end apart: 20, of which 12 were waited for; matrix products, arithmetic and copies ran while one was open for 0% of the time, Pallas kernels for 2%

profile of v3, /device:TPU:1, one launch (start us, length us, event | category | flops | bytes accessed | tf_op | source)
XLA Modules:
  0.0 268.3 jit_solution(16212026376403517209)
XLA Ops:
  0.0 1.0 copy-done.2
  1.0 1.0 copy-done.4
  2.0 1.3 state.1
  3.3 19.5 %all-to-all-start = ((bf16[64,16,128]{2,1,0:T(8,128)(2,1)}), bf16[64,16,128]{2,1,0:T(8,128)(2,1)}, u32[]{:S(2)}, u32[]{:S(2)}) async-start(bf16[64,16,128]{2,1,0:T(8,128)(2,1)} %state.1), calls=%async_computation | async-start | bytes 524288 | tf_op jit(solution)/shard_map/all_to_all | solution.py:282
  22.8 1.5 copy-done
  24.3 1.0 cut_up.1
  25.4 3.1 %collective-permute-start = (bf16[144,768]{1,0:T(8,128)(2,1)S(1)}, bf16[144,768]{1,0:T(8,128)(2,1)S(1)}, u32[]{:S(2)}, u32[]{:S(2)}) collective-permute-start(bf16[144,768]{1,0:T(8,128)(2,1)S(1)} %get-tuple-element.93), channel_id=1, source_target_pairs={{0,8},{8,0},{16,24},{24,16},{32,40},{40,32},{48,56},{56,48},{1,9},... | collective-permute-start | bytes 663560 | tf_op jit(solution)/shard_map/ppermute | solution.py:254
  28.5 4.3 %collective-permute-start.1 = (bf16[144,768]{1,0:T(8,128)(2,1)S(1)}, bf16[144,768]{1,0:T(8,128)(2,1)S(1)}, u32[]{:S(2)}, u32[]{:S(2)}) collective-permute-start(bf16[144,768]{1,0:T(8,128)(2,1)S(1)} %get-tuple-element.94), channel_id=1, source_target_pairs={{0,16},{8,24},{16,0},{24,8},{32,48},{40,56},{48,32},{56,40},{1,17}... | collective-permute-start | bytes 663560 | tf_op jit(solution)/shard_map/ppermute | solution.py:254
  32.8 0.9 inner.1.inner_ref
  33.8 1.1 collective-permute-done.refs_1_
  35.7 6.4 %collective-permute-done.1.refs_2_ = bf16[144,768]{1,0:T(8,128)(2,1)S(1)} collective-permute-done((bf16[144,768]{1,0:T(8,128)(2,1)S(1)}, bf16[144,768]{1,0:T(8,128)(2,1)S(1)}, u32[]{:S(2)}, u32[]{:S(2)}) %collective-permute-start.1) | collective-permute-done | bytes 221216 | tf_op jit(solution)/shard_map/ppermute | solution.py:254
  42.1 0.7 copy-done.12
  42.8 1.7 prefix.1
  44.5 12.3 %all-to-all-start.1 = ((bf16[64,16,128]{2,1,0:T(8,128)(2,1)}), bf16[64,16,128]{2,1,0:T(8,128)(2,1)S(1)}, u32[]{:S(2)}, u32[]{:S(2)}) async-start(bf16[64,16,128]{2,1,0:T(8,128)(2,1)} %prefix.1), calls=%async_computation.1 | async-start | bytes 524288 | tf_op jit(solution)/shard_map/all_to_all | solution.py:297
  56.8 4.1 %collective-permute-start.2 = (bf16[144,768]{1,0:T(8,128)(2,1)}, bf16[144,768]{1,0:T(8,128)(2,1)}, u32[]{:S(2)}, u32[]{:S(2)}) collective-permute-start(bf16[144,768]{1,0:T(8,128)(2,1)} %copy-done.21), channel_id=1, source_target_pairs={{0,24},{8,16},{16,8},{24,0},{32,56},{40,48},{48,40},{56,32},{1,25}... | collective-permute-start | bytes 663560 | tf_op jit(solution)/shard_map/ppermute | solution.py:254
  60.9 3.1 %collective-permute-start.3 = (bf16[144,768]{1,0:T(8,128)(2,1)}, bf16[144,768]{1,0:T(8,128)(2,1)}, u32[]{:S(2)}, u32[]{:S(2)}) collective-permute-start(bf16[144,768]{1,0:T(8,128)(2,1)} %copy-done.20), channel_id=1, source_target_pairs={{0,32},{8,40},{16,48},{24,56},{32,0},{40,8},{48,16},{56,24},{1,33}... | collective-permute-start | bytes 663560 | tf_op jit(solution)/shard_map/ppermute | solution.py:254
  64.0 1.9 collective-permute-start.4
  66.0 2.3 cut_down.1
  69.1 5.1 %collective-permute-done.3.refs_4_ = bf16[144,768]{1,0:T(8,128)(2,1)} collective-permute-done((bf16[144,768]{1,0:T(8,128)(2,1)}, bf16[144,768]{1,0:T(8,128)(2,1)}, u32[]{:S(2)}, u32[]{:S(2)}) %collective-permute-start.3) | collective-permute-done | bytes 221216 | tf_op jit(solution)/shard_map/ppermute | solution.py:254
  74.2 5.5 %collective-permute-done.4.refs_5_ = bf16[144,768]{1,0:T(8,128)(2,1)} collective-permute-done((bf16[144,768]{1,0:T(8,128)(2,1)}, bf16[144,768]{1,0:T(8,128)(2,1)}, u32[]{:S(2)}, u32[]{:S(2)}) %collective-permute-start.4) | collective-permute-done | bytes 221216 | tf_op jit(solution)/shard_map/ppermute | solution.py:254
  79.7 1.1 attn.1
  80.8 5.3 %collective-permute-start.5 = (bf16[144,768]{1,0:T(8,128)(2,1)}, bf16[144,768]{1,0:T(8,128)(2,1)S(1)}, u32[]{:S(2)}, u32[]{:S(2)}) collective-permute-start(bf16[144,768]{1,0:T(8,128)(2,1)} %copy-done.17), channel_id=1, source_target_pairs={{0,48},{8,56},{16,32},{24,40},{32,16},{40,24},{48,0},{56,8},{1,49}... | collective-permute-start | bytes 663560 | tf_op jit(solution)/shard_map/ppermute | solution.py:254
  86.1 10.5 %all_to_all.35.row_ref = bf16[8,32,128]{2,1,0:T(8,128)(2,1)S(1)} all-to-all(bf16[8,32,128]{2,1,0:T(8,128)(2,1)S(1)} %get-tuple-element.133), channel_id=1, replica_groups=mesh['r'=8,'c'=8,'p'=8] {'p'}, dimensions={0} | all-to-all | bytes 131072 | tf_op jit(solution)/shard_map/all_to_all | solution.py:328
  96.6 0.9 tile.19
  97.5 11.6 %all-to-all-start.3 = ((bf16[64,32,128]{2,1,0:T(8,128)(2,1)}), bf16[64,32,128]{2,1,0:T(8,128)(2,1)S(1)}, u32[]{:S(2)}, u32[]{:S(2)}) async-start(bf16[64,32,128]{2,1,0:T(8,128)(2,1)} %bitcast.6), calls=%async_computation.3 | async-start | bytes 1048576 | tf_op jit(solution)/shard_map/all_to_all | solution.py:334
  109.1 5.0 %collective-permute-start.6 = (bf16[144,768]{1,0:T(8,128)(2,1)}, bf16[144,768]{1,0:T(8,128)(2,1)S(1)}, u32[]{:S(2)}, u32[]{:S(2)}) collective-permute-start(bf16[144,768]{1,0:T(8,128)(2,1)} %get-tuple-element.146), channel_id=1, source_target_pairs={{0,56},{8,48},{16,40},{24,32},{32,24},{40,16},{48,8},{56,0},{1,57}... | collective-permute-start | bytes 663560 | tf_op jit(solution)/shard_map/ppermute | solution.py:254
  114.2 1.9 collective-permute-start.7
  116.1 3.4 %collective-permute-start.8 = (bf16[96,1152]{1,0:T(8,128)(2,1)}, bf16[96,1152]{1,0:T(8,128)(2,1)S(1)}, u32[]{:S(2)}, u32[]{:S(2)}) collective-permute-start(bf16[96,1152]{1,0:T(8,128)(2,1)} %get-tuple-element.148), channel_id=1, source_target_pairs={{0,16},{8,24},{16,0},{24,8},{32,48},{40,56},{48,32},{56,40},{1,17}... | collective-permute-start | bytes 663560 | tf_op jit(solution)/shard_map/ppermute | solution.py:254
  119.5 4.3 %collective-permute-start.9 = (bf16[96,1152]{1,0:T(8,128)(2,1)}, bf16[96,1152]{1,0:T(8,128)(2,1)S(1)}, u32[]{:S(2)}, u32[]{:S(2)}) collective-permute-start(bf16[96,1152]{1,0:T(8,128)(2,1)} %get-tuple-element.149), channel_id=1, source_target_pairs={{0,24},{8,16},{16,8},{24,0},{32,56},{40,48},{48,40},{56,32},{1,25}... | collective-permute-start | bytes 663560 | tf_op jit(solution)/shard_map/ppermute | solution.py:254
  123.8 2.2 collective-permute-start.10
  126.0 13.1 %collective-permute-done.6.refs_7_ = bf16[144,768]{1,0:T(8,128)(2,1)S(1)} collective-permute-done((bf16[144,768]{1,0:T(8,128)(2,1)}, bf16[144,768]{1,0:T(8,128)(2,1)S(1)}, u32[]{:S(2)}, u32[]{:S(2)}) %collective-permute-start.6) | collective-permute-done | bytes 221216 | tf_op jit(solution)/shard_map/ppermute | solution.py:254
  139.4 2.7 %collective-permute-done.10.refs_4_ = bf16[96,1152]{1,0:T(8,128)(2,1)S(1)} collective-permute-done((bf16[96,1152]{1,0:T(8,128)(2,1)}, bf16[96,1152]{1,0:T(8,128)(2,1)S(1)}, u32[]{:S(2)}, u32[]{:S(2)}) %collective-permute-start.10) | collective-permute-done | bytes 221216 | tf_op jit(solution)/shard_map/ppermute | solution.py:254
  142.1 4.2 %up.1 = bf16[1152,384]{1,0:T(8,128)(2,1)} custom-call(s32[1]{0:T(128)} %bitcast.place_ref, bf16[64,32,128]{2,1,0:T(8,128)(2,1)S(1)} %all-to-all-done.3.x_ref, bf16[144,768]{1,0:T(8,128)(2,1)S(1)} %copy-done.9, bf16[144,768]{1,0:T(8,128)(2,1)S(1)} %copy-done.11, bf16[144,768]{1,0:T(8,128)(2,1)S(1)} %copy-done.13, ...), custom_call_target="tpu_custom_call" | custom-call | tf_op jit(solution)/shard_map/up/pallas_call | solution.py:31
  146.4 3.8 %all-to-all-start.4 = ((bf16[8,144,384]{2,1,0:T(8,128)(2,1)}), bf16[8,144,384]{2,1,0:T(8,128)(2,1)S(1)}, u32[]{:S(2)}, u32[]{:S(2)}) async-start(bf16[8,144,384]{2,1,0:T(8,128)(2,1)} %bitcast.7), calls=%async_computation.4 | async-start | bytes 1769472 | tf_op jit(solution)/shard_map/all_to_all | solution.py:357
  150.2 4.3 %collective-permute-start.11 = (bf16[96,1152]{1,0:T(8,128)(2,1)}, bf16[96,1152]{1,0:T(8,128)(2,1)S(1)}, u32[]{:S(2)}, u32[]{:S(2)}) collective-permute-start(bf16[96,1152]{1,0:T(8,128)(2,1)} %copy-done.16), channel_id=1, source_target_pairs={{0,40},{8,32},{16,56},{24,48},{32,8},{40,0},{48,24},{56,16},{1,41}... | collective-permute-start | bytes 663560 | tf_op jit(solution)/shard_map/ppermute | solution.py:254
  154.5 4.3 %collective-permute-start.12 = (bf16[96,1152]{1,0:T(8,128)(2,1)}, bf16[96,1152]{1,0:T(8,128)(2,1)S(1)}, u32[]{:S(2)}, u32[]{:S(2)}) collective-permute-start(bf16[96,1152]{1,0:T(8,128)(2,1)} %copy-done.15), channel_id=1, source_target_pairs={{0,48},{8,56},{16,32},{24,40},{32,16},{40,24},{48,0},{56,8},{1,49}... | collective-permute-start | bytes 663560 | tf_op jit(solution)/shard_map/ppermute | solution.py:254
  158.8 3.1 %collective-permute-start.13 = (bf16[96,1152]{1,0:T(8,128)(2,1)}, bf16[96,1152]{1,0:T(8,128)(2,1)S(1)}, u32[]{:S(2)}, u32[]{:S(2)}) collective-permute-start(bf16[96,1152]{1,0:T(8,128)(2,1)} %copy-done.14), channel_id=1, source_target_pairs={{0,56},{8,48},{16,40},{24,32},{32,24},{40,16},{48,8},{56,0},{1,57}... | collective-permute-start | bytes 663560 | tf_op jit(solution)/shard_map/ppermute | solution.py:254
  161.9 3.5 %collective-permute-done.11.refs_5_ = bf16[96,1152]{1,0:T(8,128)(2,1)S(1)} collective-permute-done((bf16[96,1152]{1,0:T(8,128)(2,1)}, bf16[96,1152]{1,0:T(8,128)(2,1)S(1)}, u32[]{:S(2)}, u32[]{:S(2)}) %collective-permute-start.11) | collective-permute-done | bytes 221216 | tf_op jit(solution)/shard_map/ppermute | solution.py:254
  165.3 6.3 %collective-permute-done.12.refs_6_ = bf16[96,1152]{1,0:T(8,128)(2,1)S(1)} collective-permute-done((bf16[96,1152]{1,0:T(8,128)(2,1)}, bf16[96,1152]{1,0:T(8,128)(2,1)S(1)}, u32[]{:S(2)}, u32[]{:S(2)}) %collective-permute-start.12) | collective-permute-done | bytes 221216 | tf_op jit(solution)/shard_map/ppermute | solution.py:254
  171.7 4.6 %collective-permute-done.13.refs_7_ = bf16[96,1152]{1,0:T(8,128)(2,1)S(1)} collective-permute-done((bf16[96,1152]{1,0:T(8,128)(2,1)}, bf16[96,1152]{1,0:T(8,128)(2,1)S(1)}, u32[]{:S(2)}, u32[]{:S(2)}) %collective-permute-start.13) | collective-permute-done | bytes 221216 | tf_op jit(solution)/shard_map/ppermute | solution.py:254
  176.5 35.9 %all_gather.3.h_ref = bf16[1152,384]{1,0:T(8,128)(2,1)S(1)} all-gather(bf16[144,384]{1,0:T(8,128)(2,1)S(1)} %act.1), channel_id=1, replica_groups=mesh['r'=8,'c'=8,'p'=8] {'r'}, dimensions={0}, use_global_device_ids=true | all-gather | bytes 995328 | tf_op jit(solution)/shard_map/all_gather | solution.py:360
  212.4 4.7 %down.1 = bf16[64,32,128]{2,1,0:T(8,128)(2,1)} custom-call(s32[1]{0:T(128)} %bitcast.place_ref, bf16[1152,384]{1,0:T(8,128)(2,1)S(1)} %all_gather.3.h_ref, bf16[96,1152]{1,0:T(8,128)(2,1)S(1)} %get-tuple-element.169.refs_0_, bf16[96,1152]{1,0:T(8,128)(2,1)S(1)} %collective-permute-done.7.refs_1_, bf16[96,1152]{1,0:T(8,128)(2,1)S(1)} %collective-permute-done.8.refs_2_, ...), custom_call_target="tpu_custom_call" | custom-call | tf_op jit(solution)/shard_map/down/pallas_call | solution.py:31
  217.1 7.3 %all-to-all-start.5 = ((bf16[64,32,128]{2,1,0:T(8,128)(2,1)}), bf16[64,32,128]{2,1,0:T(8,128)(2,1)S(1)}, u32[]{:S(2)}, u32[]{:S(2)}) async-start(bf16[64,32,128]{2,1,0:T(8,128)(2,1)} %down.1), calls=%async_computation.5 | async-start | bytes 1048576 | tf_op jit(solution)/shard_map/all_to_all | solution.py:377
  224.7 27.5 %all-to-all-done.5.y_ref = bf16[64,32,128]{2,1,0:T(8,128)(2,1)S(1)} async-done(((bf16[64,32,128]{2,1,0:T(8,128)(2,1)}), bf16[64,32,128]{2,1,0:T(8,128)(2,1)S(1)}, u32[]{:S(2)}, u32[]{:S(2)}) %all-to-all-start.5) | async-done | bytes 524320 | tf_op jit(solution)/shard_map/all_to_all | solution.py:377
  252.2 0.9 weigh.1
  253.1 9.2 %all-to-all-start.6 = ((bf16[8,32,128]{2,1,0:T(8,128)(2,1)}), bf16[8,32,128]{2,1,0:T(8,128)(2,1)S(1)}, u32[]{:S(2)}, u32[]{:S(2)}) async-start(bf16[8,32,128]{2,1,0:T(8,128)(2,1)} %weigh.1), calls=%async_computation.6 | async-start | bytes 131072 | tf_op jit(solution)/shard_map/all_to_all | solution.py:381
  262.4 4.9 %all-to-all-done.6.y_ref = bf16[8,32,128]{2,1,0:T(8,128)(2,1)S(1)} async-done(((bf16[8,32,128]{2,1,0:T(8,128)(2,1)}), bf16[8,32,128]{2,1,0:T(8,128)(2,1)S(1)}, u32[]{:S(2)}, u32[]{:S(2)}) %all-to-all-start.6) | async-done | bytes 65568 | tf_op jit(solution)/shard_map/all_to_all | solution.py:381
  267.2 1.0 add.6
  (64 shorter events, 2.2 us)
Async XLA Ops:
  0.0 1.0 copy-start.2
  1.0 1.0 copy-start.4
  2.0 30.8 %copy-start.3 = (bf16[256,768]{1,0:T(8,128)(2,1)S(1)}, bf16[256,768]{1,0:T(8,128)(2,1)}, u32[]{:S(2)}) copy-start(bf16[256,768]{1,0:T(8,128)(2,1)} %k_ref.3) | copy-start | bytes 1179652
  2.0 30.8 %copy-start.5 = (bf16[256,768]{1,0:T(8,128)(2,1)S(1)}, bf16[256,768]{1,0:T(8,128)(2,1)}, u32[]{:S(2)}) copy-start(bf16[256,768]{1,0:T(8,128)(2,1)} %v_ref.3) | copy-start | bytes 1179652
  3.3 39.5 %all-to-all-start = ((bf16[64,16,128]{2,1,0:T(8,128)(2,1)}), bf16[64,16,128]{2,1,0:T(8,128)(2,1)}, u32[]{:S(2)}, u32[]{:S(2)}) async-start(bf16[64,16,128]{2,1,0:T(8,128)(2,1)} %state.1), calls=%async_computation | async-start | bytes 524288 | tf_op jit(solution)/shard_map/all_to_all | solution.py:282
  22.8 1.5 copy-start
  24.3 8.5 %copy-start.6 = (bf16[256,768]{1,0:T(8,128)(2,1)S(1)}, bf16[256,768]{1,0:T(8,128)(2,1)}, u32[]{:S(2)}) copy-start(bf16[256,768]{1,0:T(8,128)(2,1)} %q_ref.3) | copy-start | bytes 1179652
  25.3 8.5 %copy-start.8 = (bf16[144,768]{1,0:T(8,128)(2,1)}, bf16[144,768]{1,0:T(8,128)(2,1)S(1)}, u32[]{:S(2)}) copy-start(bf16[144,768]{1,0:T(8,128)(2,1)S(1)} %get-tuple-element.152.refs_0_) | copy-start | bytes 663556
  25.3 9.6 %copy-start.17 = (bf16[144,768]{1,0:T(8,128)(2,1)}, bf16[144,768]{1,0:T(8,128)(2,1)S(1)}, u32[]{:S(2)}) copy-start(bf16[144,768]{1,0:T(8,128)(2,1)S(1)} %get-tuple-element.134) | copy-start | bytes 663556
  25.3 9.6 %copy-start.19 = (bf16[144,768]{1,0:T(8,128)(2,1)}, bf16[144,768]{1,0:T(8,128)(2,1)S(1)}, u32[]{:S(2)}) copy-start(bf16[144,768]{1,0:T(8,128)(2,1)S(1)} %get-tuple-element.106) | copy-start | bytes 663556
  25.3 9.6 %copy-start.20 = (bf16[144,768]{1,0:T(8,128)(2,1)}, bf16[144,768]{1,0:T(8,128)(2,1)S(1)}, u32[]{:S(2)}) copy-start(bf16[144,768]{1,0:T(8,128)(2,1)S(1)} %get-tuple-element.105) | copy-start | bytes 663556
  25.3 9.6 %copy-start.21 = (bf16[144,768]{1,0:T(8,128)(2,1)}, bf16[144,768]{1,0:T(8,128)(2,1)S(1)}, u32[]{:S(2)}) copy-start(bf16[144,768]{1,0:T(8,128)(2,1)S(1)} %get-tuple-element.104) | copy-start | bytes 663556
  25.4 40.6 %copy-start.23 = (s32[1,8,5]{1,0,2:T(1,128)S(1)}, s32[1,8,5]{1,0,2:T(1,128)}, u32[]{:S(2)}) copy-start(s32[1,8,5]{1,0,2:T(1,128)} %param.10) | copy-start | bytes 484
  25.4 40.7 %copy-start.1 = (bf16[1,96,9216]{2,1,0:T(8,128)(2,1)S(1)}, bf16[1,96,9216]{2,1,0:T(8,128)(2,1)}, u32[]{:S(2)}) copy-start(bf16[1,96,9216]{2,1,0:T(8,128)(2,1)} %param.13) | copy-start | bytes 5308420
  25.4 9.6 %collective-permute-start = (bf16[144,768]{1,0:T(8,128)(2,1)S(1)}, bf16[144,768]{1,0:T(8,128)(2,1)S(1)}, u32[]{:S(2)}, u32[]{:S(2)}) collective-permute-start(bf16[144,768]{1,0:T(8,128)(2,1)S(1)} %get-tuple-element.93), channel_id=1, source_target_pairs={{0,8},{8,0},{16,24},{24,16},{32,40},{40,32},{48,56},{56,48},{1,9},... | collective-permute-start | bytes 663560 | tf_op jit(solution)/shard_map/ppermute | solution.py:254
  28.5 13.6 %collective-permute-start.1 = (bf16[144,768]{1,0:T(8,128)(2,1)S(1)}, bf16[144,768]{1,0:T(8,128)(2,1)S(1)}, u32[]{:S(2)}, u32[]{:S(2)}) collective-permute-start(bf16[144,768]{1,0:T(8,128)(2,1)S(1)} %get-tuple-element.94), channel_id=1, source_target_pairs={{0,16},{8,24},{16,0},{24,8},{32,48},{40,56},{48,32},{56,40},{1,17}... | collective-permute-start | bytes 663560 | tf_op jit(solution)/shard_map/ppermute | solution.py:254
  33.8 45.9 %copy-start.7 = (bf16[256,768]{1,0:T(8,128)(2,1)S(1)}, bf16[256,768]{1,0:T(8,128)(2,1)}, u32[]{:S(2)}) copy-start(bf16[256,768]{1,0:T(8,128)(2,1)} %q_ref.3) | copy-start | bytes 1179652
  35.0 0.7 copy-start.10
  42.1 0.7 copy-start.12
  44.5 35.2 %all-to-all-start.1 = ((bf16[64,16,128]{2,1,0:T(8,128)(2,1)}), bf16[64,16,128]{2,1,0:T(8,128)(2,1)S(1)}, u32[]{:S(2)}, u32[]{:S(2)}) async-start(bf16[64,16,128]{2,1,0:T(8,128)(2,1)} %prefix.1), calls=%async_computation.1 | async-start | bytes 524288 | tf_op jit(solution)/shard_map/all_to_all | solution.py:297
  56.8 12.3 %collective-permute-start.2 = (bf16[144,768]{1,0:T(8,128)(2,1)}, bf16[144,768]{1,0:T(8,128)(2,1)}, u32[]{:S(2)}, u32[]{:S(2)}) collective-permute-start(bf16[144,768]{1,0:T(8,128)(2,1)} %copy-done.21), channel_id=1, source_target_pairs={{0,24},{8,16},{16,8},{24,0},{32,56},{40,48},{48,40},{56,32},{1,25}... | collective-permute-start | bytes 663560 | tf_op jit(solution)/shard_map/ppermute | solution.py:254
  60.9 13.3 %collective-permute-start.3 = (bf16[144,768]{1,0:T(8,128)(2,1)}, bf16[144,768]{1,0:T(8,128)(2,1)}, u32[]{:S(2)}, u32[]{:S(2)}) collective-permute-start(bf16[144,768]{1,0:T(8,128)(2,1)} %copy-done.20), channel_id=1, source_target_pairs={{0,32},{8,40},{16,48},{24,56},{32,0},{40,8},{48,16},{56,24},{1,33}... | collective-permute-start | bytes 663560 | tf_op jit(solution)/shard_map/ppermute | solution.py:254
  64.0 15.7 %collective-permute-start.4 = (bf16[144,768]{1,0:T(8,128)(2,1)}, bf16[144,768]{1,0:T(8,128)(2,1)}, u32[]{:S(2)}, u32[]{:S(2)}) collective-permute-start(bf16[144,768]{1,0:T(8,128)(2,1)} %copy-done.19), channel_id=1, source_target_pairs={{0,40},{8,32},{16,56},{24,48},{32,8},{40,0},{48,24},{56,16},{1,41}... | collective-permute-start | bytes 663560 | tf_op jit(solution)/shard_map/ppermute | solution.py:254
  68.4 0.7 copy-start.18
  69.0 5.2 %copy-start.14 = (bf16[96,1152]{1,0:T(8,128)(2,1)}, bf16[96,1152]{1,0:T(8,128)(2,1)S(1)}, u32[]{:S(2)}) copy-start(bf16[96,1152]{1,0:T(8,128)(2,1)S(1)} %get-tuple-element.167) | copy-start | bytes 663556
  69.1 5.2 %copy-start.15 = (bf16[96,1152]{1,0:T(8,128)(2,1)}, bf16[96,1152]{1,0:T(8,128)(2,1)S(1)}, u32[]{:S(2)}) copy-start(bf16[96,1152]{1,0:T(8,128)(2,1)S(1)} %get-tuple-element.166) | copy-start | bytes 663556
  69.1 5.2 %copy-start.16 = (bf16[96,1152]{1,0:T(8,128)(2,1)}, bf16[96,1152]{1,0:T(8,128)(2,1)S(1)}, u32[]{:S(2)}) copy-start(bf16[96,1152]{1,0:T(8,128)(2,1)S(1)} %get-tuple-element.165) | copy-start | bytes 663556
  69.1 73.1 %copy-start.9 = (bf16[144,768]{1,0:T(8,128)(2,1)S(1)}, bf16[144,768]{1,0:T(8,128)(2,1)}, u32[]{:S(2)}) copy-start(bf16[144,768]{1,0:T(8,128)(2,1)} %copy-done.8) | copy-start | bytes 663556
  69.1 73.1 %copy-start.11 = (bf16[144,768]{1,0:T(8,128)(2,1)S(1)}, bf16[144,768]{1,0:T(8,128)(2,1)}, u32[]{:S(2)}) copy-start(bf16[144,768]{1,0:T(8,128)(2,1)} %copy-done.10) | copy-start | bytes 663556
  69.1 73.0 %copy-start.13 = (bf16[144,768]{1,0:T(8,128)(2,1)S(1)}, bf16[144,768]{1,0:T(8,128)(2,1)}, u32[]{:S(2)}) copy-start(bf16[144,768]{1,0:T(8,128)(2,1)} %copy-done.12) | copy-start | bytes 663556
  80.8 15.8 %collective-permute-start.5 = (bf16[144,768]{1,0:T(8,128)(2,1)}, bf16[144,768]{1,0:T(8,128)(2,1)S(1)}, u32[]{:S(2)}, u32[]{:S(2)}) collective-permute-start(bf16[144,768]{1,0:T(8,128)(2,1)} %copy-done.17), channel_id=1, source_target_pairs={{0,48},{8,56},{16,32},{24,40},{32,16},{40,24},{48,0},{56,8},{1,49}... | collective-permute-start | bytes 663560 | tf_op jit(solution)/shard_map/ppermute | solution.py:254
  97.5 44.6 %all-to-all-start.3 = ((bf16[64,32,128]{2,1,0:T(8,128)(2,1)}), bf16[64,32,128]{2,1,0:T(8,128)(2,1)S(1)}, u32[]{:S(2)}, u32[]{:S(2)}) async-start(bf16[64,32,128]{2,1,0:T(8,128)(2,1)} %bitcast.6), calls=%async_computation.3 | async-start | bytes 1048576 | tf_op jit(solution)/shard_map/all_to_all | solution.py:334
  109.1 30.0 %collective-permute-start.6 = (bf16[144,768]{1,0:T(8,128)(2,1)}, bf16[144,768]{1,0:T(8,128)(2,1)S(1)}, u32[]{:S(2)}, u32[]{:S(2)}) collective-permute-start(bf16[144,768]{1,0:T(8,128)(2,1)} %get-tuple-element.146), channel_id=1, source_target_pairs={{0,56},{8,48},{16,40},{24,32},{32,24},{40,16},{48,8},{56,0},{1,57}... | collective-permute-start | bytes 663560 | tf_op jit(solution)/shard_map/ppermute | solution.py:254
  114.2 24.9 %collective-permute-start.7 = (bf16[96,1152]{1,0:T(8,128)(2,1)}, bf16[96,1152]{1,0:T(8,128)(2,1)S(1)}, u32[]{:S(2)}, u32[]{:S(2)}) collective-permute-start(bf16[96,1152]{1,0:T(8,128)(2,1)} %get-tuple-element.147), channel_id=1, source_target_pairs={{0,8},{8,0},{16,24},{24,16},{32,40},{40,32},{48,56},{56,48},{1,9},... | collective-permute-start | bytes 663560 | tf_op jit(solution)/shard_map/ppermute | solution.py:254
  116.1 23.0 %collective-permute-start.8 = (bf16[96,1152]{1,0:T(8,128)(2,1)}, bf16[96,1152]{1,0:T(8,128)(2,1)S(1)}, u32[]{:S(2)}, u32[]{:S(2)}) collective-permute-start(bf16[96,1152]{1,0:T(8,128)(2,1)} %get-tuple-element.148), channel_id=1, source_target_pairs={{0,16},{8,24},{16,0},{24,8},{32,48},{40,56},{48,32},{56,40},{1,17}... | collective-permute-start | bytes 663560 | tf_op jit(solution)/shard_map/ppermute | solution.py:254
  119.5 19.9 %collective-permute-start.9 = (bf16[96,1152]{1,0:T(8,128)(2,1)}, bf16[96,1152]{1,0:T(8,128)(2,1)S(1)}, u32[]{:S(2)}, u32[]{:S(2)}) collective-permute-start(bf16[96,1152]{1,0:T(8,128)(2,1)} %get-tuple-element.149), channel_id=1, source_target_pairs={{0,24},{8,16},{16,8},{24,0},{32,56},{40,48},{48,40},{56,32},{1,25}... | collective-permute-start | bytes 663560 | tf_op jit(solution)/shard_map/ppermute | solution.py:254
  123.8 18.3 %collective-permute-start.10 = (bf16[96,1152]{1,0:T(8,128)(2,1)}, bf16[96,1152]{1,0:T(8,128)(2,1)S(1)}, u32[]{:S(2)}, u32[]{:S(2)}) collective-permute-start(bf16[96,1152]{1,0:T(8,128)(2,1)} %copy-done.18), channel_id=1, source_target_pairs={{0,32},{8,40},{16,48},{24,56},{32,0},{40,8},{48,16},{56,24},{1,33}... | collective-permute-start | bytes 663560 | tf_op jit(solution)/shard_map/ppermute | solution.py:254
  146.4 30.0 %all-to-all-start.4 = ((bf16[8,144,384]{2,1,0:T(8,128)(2,1)}), bf16[8,144,384]{2,1,0:T(8,128)(2,1)S(1)}, u32[]{:S(2)}, u32[]{:S(2)}) async-start(bf16[8,144,384]{2,1,0:T(8,128)(2,1)} %bitcast.7), calls=%async_computation.4 | async-start | bytes 1769472 | tf_op jit(solution)/shard_map/all_to_all | solution.py:357
  150.2 15.2 %collective-permute-start.11 = (bf16[96,1152]{1,0:T(8,128)(2,1)}, bf16[96,1152]{1,0:T(8,128)(2,1)S(1)}, u32[]{:S(2)}, u32[]{:S(2)}) collective-permute-start(bf16[96,1152]{1,0:T(8,128)(2,1)} %copy-done.16), channel_id=1, source_target_pairs={{0,40},{8,32},{16,56},{24,48},{32,8},{40,0},{48,24},{56,16},{1,41}... | collective-permute-start | bytes 663560 | tf_op jit(solution)/shard_map/ppermute | solution.py:254
  154.5 17.2 %collective-permute-start.12 = (bf16[96,1152]{1,0:T(8,128)(2,1)}, bf16[96,1152]{1,0:T(8,128)(2,1)S(1)}, u32[]{:S(2)}, u32[]{:S(2)}) collective-permute-start(bf16[96,1152]{1,0:T(8,128)(2,1)} %copy-done.15), channel_id=1, source_target_pairs={{0,48},{8,56},{16,32},{24,40},{32,16},{40,24},{48,0},{56,8},{1,49}... | collective-permute-start | bytes 663560 | tf_op jit(solution)/shard_map/ppermute | solution.py:254
  158.8 17.6 %collective-permute-start.13 = (bf16[96,1152]{1,0:T(8,128)(2,1)}, bf16[96,1152]{1,0:T(8,128)(2,1)S(1)}, u32[]{:S(2)}, u32[]{:S(2)}) collective-permute-start(bf16[96,1152]{1,0:T(8,128)(2,1)} %copy-done.14), channel_id=1, source_target_pairs={{0,56},{8,48},{16,40},{24,32},{32,24},{40,16},{48,8},{56,0},{1,57}... | collective-permute-start | bytes 663560 | tf_op jit(solution)/shard_map/ppermute | solution.py:254
  212.4 12.1 %copy-start.22 = (bf16[6144,1]{0,1:T(2,128)(2,1)S(1)}, bf16[6144,1]{0,1:T(2,128)(2,1)}, u32[]{:S(2)}) copy-start(bf16[6144,1]{0,1:T(2,128)(2,1)} %param.11) | copy-start | bytes 36868
  217.1 35.1 %all-to-all-start.5 = ((bf16[64,32,128]{2,1,0:T(8,128)(2,1)}), bf16[64,32,128]{2,1,0:T(8,128)(2,1)S(1)}, u32[]{:S(2)}, u32[]{:S(2)}) async-start(bf16[64,32,128]{2,1,0:T(8,128)(2,1)} %down.1), calls=%async_computation.5 | async-start | bytes 1048576 | tf_op jit(solution)/shard_map/all_to_all | solution.py:377
  253.1 14.1 %all-to-all-start.6 = ((bf16[8,32,128]{2,1,0:T(8,128)(2,1)}), bf16[8,32,128]{2,1,0:T(8,128)(2,1)S(1)}, u32[]{:S(2)}, u32[]{:S(2)}) async-start(bf16[8,32,128]{2,1,0:T(8,128)(2,1)} %weigh.1), calls=%async_computation.6 | async-start | bytes 131072 | tf_op jit(solution)/shard_map/all_to_all | solution.py:381

commit v4 on v2

--- a/solution.py
+++ b/solution.py
@@ -13,8 +13,6 @@
 F32 = jnp.float32
 
 
-SMEM = pltpu.SMEM
-VMEM = pltpu.VMEM
 HBM = pltpu.HBM
 
 
@@ -133,56 +131,34 @@
     pay_ref[...] = picks[...].reshape(8, SLOTS, LANES).astype(BF16)
 
 
-def cut_up_kernel(place_ref, w_ref, *refs):
-    outs, sems = refs[:8], refs[8]
-    width = outs[0].shape[1]
+def cut_up_kernel(w_ref, out_ref, sems):
+    width = out_ref.shape[2]
     copies = []
-    for k, out in enumerate(outs):
-        low = pl.multiple_of((place_ref[0] ^ k) * width, LANES)
-        copies.append(pltpu.make_async_copy(w_ref.at[:, pl.ds(low, width)], out, sems.at[k]))
+    for part in range(8):
+        source = w_ref.at[:, part * width : (part + 1) * width]
+        copies.append(pltpu.make_async_copy(source, out_ref.at[part], sems.at[part]))
         copies[-1].start()
     for copy in copies:
         copy.wait()
 
 
-def cut_down_kernel(place_ref, w_ref, *refs):
-    outs, cut, sems = refs[:8], refs[8], refs[9]
+def cut_down_kernel(w_ref, out_ref):
     run = w_ref.shape[1] // 64
     for part in range(8):
         for group in range(8):
             low = (group * 8 + part) * run
-            cut[part, :, group * run : (group + 1) * run] = w_ref[:, low : low + run]
-    copies = []
-    for k, out in enumerate(outs):
-        copies.append(pltpu.make_async_copy(cut.at[place_ref[0] ^ k], out, sems.at[k]))
-        copies[-1].start()
-    for copy in copies:
-        copy.wait()
-
-
-def fetch(place_ref, pieces, whole, sems):
-    copies = []
-    for k, piece in enumerate(pieces):
-        rows = piece.shape[0]
-        low = pl.multiple_of((place_ref[0] ^ k) * rows, 16)
-        copies.append(pltpu.make_async_copy(piece, whole.at[pl.ds(low, rows), :], sems.at[k]))
-        copies[-1].start()
-    return copies
-
-
-def up_kernel(place_ref, x_ref, *refs):
-    pieces, out_ref, rows, picked, whole, sems = refs[:8], *refs[8:]
-    copies = fetch(place_ref, pieces, whole, sems)
+            out_ref[part, :, group * run : (group + 1) * run] = w_ref[:, low : low + run]
+
+
+def up_kernel(x_ref, w_ref, out_ref, rows, picked):
     rows[...] = x_ref[...].astype(F32).reshape(64 * SLOTS, LANES)
     picked[320:] = jnp.zeros((64, picked.shape[1]), BF16)
     for i in range(5):
         for tile in range(6):
             piece = rows[pl.ds(i * 6 + tile, 64, stride=SLOTS), :]
             picked[i * 64 : i * 64 + 64, tile * LANES : (tile + 1) * LANES] = piece.astype(BF16)
-    for copy in copies:
-        copy.wait()
     out_ref[...] = lax.dot_general(
-        whole[...], picked[...], (((1,), (1,)), ((), ())), preferred_element_type=F32
+        w_ref[...], picked[...], (((1,), (1,)), ((), ())), preferred_element_type=F32
     ).astype(BF16)
 
 
@@ -193,15 +169,11 @@
     out_ref[...] = (up / (1.0 + jnp.exp(-up))).astype(BF16)
 
 
-def down_kernel(place_ref, h_ref, *refs):
-    pieces, out_ref, rows, whole, sems = refs[:8], *refs[8:]
-    copies = fetch(place_ref, pieces, whole, sems)
+def down_kernel(h_ref, w_ref, out_ref, rows):
     for slot in (30, 31):
         rows[pl.ds(slot, 64, stride=SLOTS), :] = jnp.zeros((64, LANES), F32)
-    for copy in copies:
-        copy.wait()
     y = lax.dot_general(
-        h_ref[...], whole[...], (((0,), (1,)), ((), ())), preferred_element_type=F32
+        h_ref[...], w_ref[...], (((0,), (1,)), ((), ())), preferred_element_type=F32
     )
     for i in range(5):
         for tile in range(6):
@@ -248,14 +220,6 @@
     return jax.ShapeDtypeStruct(dims, dtype)
 
 
-def exchange(pieces, first, last):
-    count = len(pieces)
-    return [
-        lax.ppermute(pieces[k], "c", [(c, c ^ k) for c in range(count)])
-        for k in range(first, last)
-    ]
-
-
 def body(queries, keys, values, selections, router, w_up, w_down):
     length, width = queries.shape
     parts = lax.axis_size("p")
@@ -263,7 +227,6 @@
     units = w_up.shape[1]
     columns = w_down.shape[1]
     group = w_down.shape[2] // parts
-    place = lax.axis_index("c").astype(jnp.int32).reshape(1)
     sel = selections[0].T.reshape(-1)
     sel_column = sel[:, None]
     sel_row = jnp.pad(sel, (0, LANES - sel.shape[0]), constant_values=-1)[None]
@@ -278,35 +241,23 @@
         scratch=[pltpu.VMEM((width, width), F32), pltpu.VMEM((64 * 16, LANES), F32)],
         name="state",
     )
-    w_up, state = lax.optimization_barrier((w_up, state))
+    w_up, w_down, state = lax.optimization_barrier((w_up, w_down, state))
     chunks = lax.all_to_all(state, seq, 0, 0, tiled=True)
-    up_pieces = call(
+    inner = call(inner_kernel, shape((length, width), F32), queries, keys, values, name="inner")
+    up_cut = call(
         cut_up_kernel,
-        [shape((units, width))] * 8,
-        place,
+        shape((8, units, width)),
         w_up[0],
         scratch=[pltpu.SemaphoreType.DMA((8,))],
-        spaces=([SMEM, HBM], [HBM] * 8),
+        spaces=([HBM], HBM),
         name="cut_up",
     )
-    up_first = exchange(up_pieces, 1, 5)
-    inner = call(inner_kernel, shape((length, width), F32), queries, keys, values, name="inner")
-    chunks, inner, up_first = lax.optimization_barrier((chunks, inner, up_first))
+    chunks, inner, up_cut = lax.optimization_barrier((chunks, inner, up_cut))
     before = call(prefix_kernel, shape((64, 16, LANES)), chunks, name="prefix")
-    w_down, up_pieces, before = lax.optimization_barrier((w_down, up_pieces, before))
+    before, w_down = lax.optimization_barrier((before, w_down))
     before = lax.all_to_all(before, seq, 0, 0, tiled=True)
-    up_last = exchange(up_pieces, 5, 8)
-    down_pieces = call(
-        cut_down_kernel,
-        [shape((columns, group))] * 8,
-        place,
-        w_down[0],
-        scratch=[pltpu.VMEM((8, columns, group), BF16), pltpu.SemaphoreType.DMA((8,))],
-        spaces=([SMEM, VMEM], [HBM] * 8),
-        name="cut_down",
-    )
-    before, up_last, down_pieces = lax.optimization_barrier((before, up_last, down_pieces))
-    down_moved = exchange(down_pieces, 1, 8)
+    down_cut = call(cut_down_kernel, shape((8, columns, group)), w_down[0], name="cut_down")
+    before, down_cut = lax.optimization_barrier((before, down_cut))
     attn, pay = call(
         attn_kernel,
         (shape((length, width)), shape((8, SLOTS, LANES))),
@@ -323,41 +274,29 @@
         name="attn",
     )
     whole_rows = lax.all_to_all(pay, "p", 0, 0, tiled=True)
-    arrived = lax.all_to_all(jnp.tile(whole_rows, (8, 1, 1)), seq, 0, 0, tiled=True)
-    arrived, down_moved = lax.optimization_barrier((arrived, down_moved))
+    near_rows = lax.all_to_all(whole_rows, "c", 0, 0, tiled=True)
+    near_rows, up_cut = lax.optimization_barrier((near_rows, up_cut))
+    up_mine = lax.all_to_all(up_cut, "c", 0, 0, tiled=True).reshape(8 * units, width)
+    arrived = lax.all_gather(near_rows, "r", axis=0, tiled=True)
     partial = call(
         up_kernel,
         shape((8 * units, 384)),
-        place,
         arrived,
-        up_pieces[0],
-        *up_first,
-        *up_last,
-        scratch=[
-            pltpu.VMEM((64 * SLOTS, LANES), F32),
-            pltpu.VMEM((384, width), BF16),
-            pltpu.VMEM((8 * units, width), BF16),
-            pltpu.SemaphoreType.DMA((8,)),
-        ],
-        spaces=([SMEM, VMEM] + [HBM] * 8, VMEM),
+        up_mine,
+        scratch=[pltpu.VMEM((64 * SLOTS, LANES), F32), pltpu.VMEM((384, width), BF16)],
         name="up",
     )
     sums = lax.all_to_all(partial.reshape(8, units, 384), "c", 0, 0, tiled=True)
     act = call(act_kernel, shape((units, 384)), sums, name="act")
+    act, down_cut = lax.optimization_barrier((act, down_cut))
+    down_mine = lax.all_to_all(down_cut, "c", 0, 0, tiled=True).reshape(8 * columns, group)
     act = lax.all_gather(act, "r", axis=0, tiled=True)
     out = call(
         down_kernel,
         shape((64, SLOTS, LANES)),
-        place,
         act,
-        down_pieces[0],
-        *down_moved,
-        scratch=[
-            pltpu.VMEM((64 * SLOTS, LANES), F32),
-            pltpu.VMEM((8 * columns, group), BF16),
-            pltpu.SemaphoreType.DMA((8,)),
-        ],
-        spaces=([SMEM, VMEM] + [HBM] * 8, VMEM),
+        down_mine,
+        scratch=[pltpu.VMEM((64 * SLOTS, LANES), F32)],
         name="down",
     )
     back = lax.all_to_all(out, seq, 0, 0, tiled=True)

time: 270 us -> 259 us (0.959)
  blocking collectives: 59.2 us -> 112 us
  starting transfers between devices: 110 us -> 71.3 us
  waiting for transfers between devices: 69.2 us -> 55.2 us
  Pallas kernels: 18.5 us -> 13.2 us
  local copies, waits for them, and re-layouts: 10.8 us -> 6.81 us
    ppermute x14 -> x0, starting transfers between devices: 47.1 us -> none  [exchange(): lax.ppermute(pieces[k], 'c', [(c, c ^ k) for c in range(count)])]
    ppermute x14 -> x0, waiting for transfers between devices: 40.7 us -> none  [exchange(): lax.ppermute(pieces[k], 'c', [(c, c ^ k) for c in range(count)])]
    all_gather x0 -> x1, blocking collectives: none -> 38 us  [body(): arrived = lax.all_gather(near_rows, 'r', axis=0, tiled=True)]
    all_to_all x1, waiting for transfers between devices: 0.01 us -> 14.8 us  [body(): before = lax.all_to_all(before, seq, 0, 0, tiled=True)]
    all_to_all x1, waiting for transfers between devices: 0.01 us -> 13.9 us  [body(): chunks = lax.all_to_all(state, seq, 0, 0, tiled=True)]
    all_to_all x1, starting transfers between devices: 13.2 us -> 27.1 us  [body(): weighted = lax.all_to_all(weighted, 'p', 0, 0, tiled=True)]
    all_to_all x0 -> x1, blocking collectives: none -> 7.98 us  [body(): near_rows = lax.all_to_all(whole_rows, 'c', 0, 0, tiled=True)]
    pallas_call x11, Pallas kernels: 18.5 us -> 13.2 us  [call(): pl.pallas_call(kernel, out_shape=out, scratch_shapes=list(scratch), compi...]
  transfers between devices with their start and end apart: 19 -> 6, of which waited for: 11 -> 4; matrix products, arithmetic and copies ran while one was open for 0% -> 0% of each run, Pallas kernels for 1% -> 2%
where the time goes in v4:
time: 259 us; the launch traced here: 258 us
  blocking collectives  112 us (43%)
  starting transfers between devices  71.3 us (28%)
  waiting for transfers between devices  55.2 us (21%)
  Pallas kernels  13.2 us (5%)
  local copies, waits for them, and re-layouts  6.81 us (3%)
    all_gather x1, blocking collectives, body(): arrived = lax.all_gather(near_rows, 'r', axis=0, tiled=True)  38 us
    all_gather x1, blocking collectives, body(): act = lax.all_gather(act, 'r', axis=0, tiled=True)  36.9 us
    all_to_all x1, starting transfers between devices, body(): weighted = lax.all_to_all(weighted, 'p', 0, 0, tiled=True)  27.1 us
    all_to_all x1, waiting for transfers between devices, body(): back = lax.all_to_all(out, seq, 0, 0, tiled=True)  21.6 us
    all_to_all x1, starting transfers between devices, body(): chunks = lax.all_to_all(state, seq, 0, 0, tiled=True)  19.3 us
    all_to_all x1, waiting for transfers between devices, body(): before = lax.all_to_all(before, seq, 0, 0, tiled=True)  14.8 us
    all_to_all x1, blocking collectives, body(): sums = lax.all_to_all(partial.reshape(8, units, 384), 'c', 0, 0, tiled=True)  14.6 us
    all_to_all x1, blocking collectives, body(): whole_rows = lax.all_to_all(pay, 'p', 0, 0, tiled=True)  14.2 us
  transfers between devices with their start and end apart: 6, of which 4 were waited for; matrix products, arithmetic and copies ran while one was open for 0% of the time, Pallas kernels for 2%

profile of v4, /device:TPU:1, one launch (start us, length us, event | category | flops | bytes accessed | tf_op | source)
XLA Modules:
  0.0 258.5 jit_solution(13415946755768010208)
XLA Ops:
  0.0 0.0 copy-start
  0.0 0.0 copy-start.2
  0.0 1.1 copy-done.2
  1.1 0.0 copy-start.4
  1.1 1.0 copy-done.4
  2.1 1.3 state.1
  3.4 19.3 %all-to-all-start = ((bf16[64,16,128]{2,1,0:T(8,128)(2,1)}), bf16[64,16,128]{2,1,0:T(8,128)(2,1)S(1)}, u32[]{:S(2)}, u32[]{:S(2)}) async-start(bf16[64,16,128]{2,1,0:T(8,128)(2,1)} %state.1), calls=%async_computation | async-start | bytes 524288 | tf_op jit(solution)/shard_map/all_to_all | solution.py:245
  22.7 0.0 copy-start.3
  22.7 1.0 copy-done.3
  23.7 1.0 copy-done.5
  24.7 0.0 copy-start.6
  24.7 1.0 copy-done.6
  25.7 0.9 inner.1.inner_ref
  26.6 0.0 copy-done
  26.6 0.0 copy-start.9
  26.6 1.3 cut_up.1
  28.0 13.9 %all-to-all-done.in_ref = bf16[64,16,128]{2,1,0:T(8,128)(2,1)S(1)} async-done(((bf16[64,16,128]{2,1,0:T(8,128)(2,1)}), bf16[64,16,128]{2,1,0:T(8,128)(2,1)S(1)}, u32[]{:S(2)}, u32[]{:S(2)}) %all-to-all-start) | async-done | bytes 262176 | tf_op jit(solution)/shard_map/all_to_all | solution.py:245
  41.9 0.8 prefix.1
  42.7 7.4 %all-to-all-start.1 = ((bf16[64,16,128]{2,1,0:T(8,128)(2,1)}), bf16[64,16,128]{2,1,0:T(8,128)(2,1)S(1)}, u32[]{:S(2)}, u32[]{:S(2)}) async-start(bf16[64,16,128]{2,1,0:T(8,128)(2,1)} %prefix.1), calls=%async_computation.1 | async-start | bytes 524288 | tf_op jit(solution)/shard_map/all_to_all | solution.py:258
  50.0 0.0 copy-done.9
  50.0 0.1 broadcast_in_dim_reshape.4.sel_ref
  50.1 0.0 copy-start.1
  50.1 1.5 copy-done.1
  51.6 2.0 cut_down.1
  53.6 14.8 %all-to-all-done.1.p_ref = bf16[64,16,128]{2,1,0:T(8,128)(2,1)S(1)} async-done(((bf16[64,16,128]{2,1,0:T(8,128)(2,1)}), bf16[64,16,128]{2,1,0:T(8,128)(2,1)S(1)}, u32[]{:S(2)}, u32[]{:S(2)}) %all-to-all-start.1) | async-done | bytes 262176 | tf_op jit(solution)/shard_map/all_to_all | solution.py:258
  68.4 0.0 copy-done.7
  68.4 1.1 attn.1
  69.5 14.2 %all_to_all.45.row_ref = bf16[8,32,128]{2,1,0:T(8,128)(2,1)S(1)} all-to-all(bf16[8,32,128]{2,1,0:T(8,128)(2,1)S(1)} %get-tuple-element.30), channel_id=1, replica_groups=mesh['r'=8,'c'=8,'p'=8] {'p'}, dimensions={0} | all-to-all | bytes 131072 | tf_op jit(solution)/shard_map/all_to_all | solution.py:276
  83.7 8.0 %all_to_all.46 = bf16[8,32,128]{2,1,0:T(8,128)(2,1)S(1)} all-to-all(bf16[8,32,128]{2,1,0:T(8,128)(2,1)S(1)} %all_to_all.45.row_ref), channel_id=1, replica_groups=mesh['r'=8,'c'=8,'p'=8] {'c'}, dimensions={0} | all-to-all | bytes 131072 | tf_op jit(solution)/shard_map/all_to_all | solution.py:277
  91.7 3.6 %all-to-all-start.4 = ((bf16[8,144,768]{2,1,0:T(8,128)(2,1)}), bf16[8,144,768]{2,1,0:T(8,128)(2,1)S(1)}, u32[]{:S(2)}, u32[]{:S(2)}) async-start(bf16[8,144,768]{2,1,0:T(8,128)(2,1)} %cut_up.1), calls=%async_computation.4 | async-start | bytes 3538944 | tf_op jit(solution)/shard_map/all_to_all | solution.py:279
  95.3 38.0 %all_gather.6.x_ref = bf16[64,32,128]{2,1,0:T(8,128)(2,1)S(1)} all-gather(bf16[8,32,128]{2,1,0:T(8,128)(2,1)S(1)} %all_to_all.46), channel_id=1, replica_groups=mesh['r'=8,'c'=8,'p'=8] {'r'}, dimensions={0}, use_global_device_ids=true | all-gather | bytes 589824 | tf_op jit(solution)/shard_map/all_gather | solution.py:280
  133.3 0.0 all-to-all-done.4
  133.3 1.4 up.1
  134.7 14.6 %all_to_all.47.in_ref = bf16[8,144,384]{2,1,0:T(8,128)(2,1)S(1)} all-to-all(bf16[8,144,384]{2,1,0:T(8,128)(2,1)S(1)} %bitcast.15), channel_id=1, replica_groups=mesh['r'=8,'c'=8,'p'=8] {'c'}, dimensions={0} | all-to-all | bytes 1769472 | tf_op jit(solution)/shard_map/all_to_all | solution.py:289
  149.3 0.2 act.1
  149.5 3.6 %all-to-all-start.6 = ((bf16[8,96,1152]{2,1,0:T(8,128)(2,1)}), bf16[8,96,1152]{2,1,0:T(8,128)(2,1)S(1)}, u32[]{:S(2)}, u32[]{:S(2)}) async-start(bf16[8,96,1152]{2,1,0:T(8,128)(2,1)} %cut_down.1), calls=%async_computation.6 | async-start | bytes 3538944 | tf_op jit(solution)/shard_map/all_to_all | solution.py:292
  153.1 36.9 %all_gather.7.h_ref = bf16[1152,384]{1,0:T(8,128)(2,1)S(1)} all-gather(bf16[144,384]{1,0:T(8,128)(2,1)S(1)} %act.1), channel_id=1, replica_groups=mesh['r'=8,'c'=8,'p'=8] {'r'}, dimensions={0}, use_global_device_ids=true | all-gather | bytes 995328 | tf_op jit(solution)/shard_map/all_gather | solution.py:293
  190.0 0.0 all-to-all-done.6
  190.0 2.3 down.1
  192.4 10.3 %all-to-all-start.7 = ((bf16[64,32,128]{2,1,0:T(8,128)(2,1)}), bf16[64,32,128]{2,1,0:T(8,128)(2,1)S(1)}, u32[]{:S(2)}, u32[]{:S(2)}) async-start(bf16[64,32,128]{2,1,0:T(8,128)(2,1)} %down.1), calls=%async_computation.7 | async-start | bytes 1048576 | tf_op jit(solution)/shard_map/all_to_all | solution.py:302
  202.7 0.1 reshape.19
  202.8 0.0 copy-done.8
  202.8 0.1 reduce
  203.0 21.6 %all-to-all-done.7.y_ref = bf16[64,32,128]{2,1,0:T(8,128)(2,1)S(1)} async-done(((bf16[64,32,128]{2,1,0:T(8,128)(2,1)}), bf16[64,32,128]{2,1,0:T(8,128)(2,1)S(1)}, u32[]{:S(2)}, u32[]{:S(2)}) %all-to-all-start.7) | async-done | bytes 524320 | tf_op jit(solution)/shard_map/all_to_all | solution.py:302
  224.6 0.9 weigh.1
  225.5 27.1 %all-to-all-start.8 = ((bf16[8,32,128]{2,1,0:T(8,128)(2,1)}), bf16[8,32,128]{2,1,0:T(8,128)(2,1)S(1)}, u32[]{:S(2)}, u32[]{:S(2)}) async-start(bf16[8,32,128]{2,1,0:T(8,128)(2,1)} %weigh.1), calls=%async_computation.8 | async-start | bytes 131072 | tf_op jit(solution)/shard_map/all_to_all | solution.py:306
  252.6 4.9 %all-to-all-done.8.y_ref = bf16[8,32,128]{2,1,0:T(8,128)(2,1)S(1)} async-done(((bf16[8,32,128]{2,1,0:T(8,128)(2,1)}), bf16[8,32,128]{2,1,0:T(8,128)(2,1)S(1)}, u32[]{:S(2)}, u32[]{:S(2)}) %all-to-all-start.8) | async-done | bytes 65568 | tf_op jit(solution)/shard_map/all_to_all | solution.py:306
  257.4 1.0 add.6
  (10 shorter events, 0.1 us)
Async XLA Ops:
  0.0 26.6 %copy-start = (bf16[1,144,6144]{2,1,0:T(8,128)(2,1)S(1)}, bf16[1,144,6144]{2,1,0:T(8,128)(2,1)}, u32[]{:S(2)}) copy-start(bf16[1,144,6144]{2,1,0:T(8,128)(2,1)} %param.12) | copy-start | bytes 5308420
  0.0 1.1 copy-start.2
  1.1 1.0 copy-start.4
  3.4 38.5 %all-to-all-start = ((bf16[64,16,128]{2,1,0:T(8,128)(2,1)}), bf16[64,16,128]{2,1,0:T(8,128)(2,1)S(1)}, u32[]{:S(2)}, u32[]{:S(2)}) async-start(bf16[64,16,128]{2,1,0:T(8,128)(2,1)} %state.1), calls=%async_computation | async-start | bytes 524288 | tf_op jit(solution)/shard_map/all_to_all | solution.py:245
  22.7 1.0 copy-start.3
  23.7 1.0 copy-start.5
  24.7 1.0 copy-start.6
  26.6 23.4 %copy-start.9 = (s32[1,8,5]{1,0,2:T(1,128)S(1)}, s32[1,8,5]{1,0,2:T(1,128)}, u32[]{:S(2)}) copy-start(s32[1,8,5]{1,0,2:T(1,128)} %param.10) | copy-start | bytes 484
  42.7 25.7 %all-to-all-start.1 = ((bf16[64,16,128]{2,1,0:T(8,128)(2,1)}), bf16[64,16,128]{2,1,0:T(8,128)(2,1)S(1)}, u32[]{:S(2)}, u32[]{:S(2)}) async-start(bf16[64,16,128]{2,1,0:T(8,128)(2,1)} %prefix.1), calls=%async_computation.1 | async-start | bytes 524288 | tf_op jit(solution)/shard_map/all_to_all | solution.py:258
  50.1 1.5 copy-start.1
  51.6 16.8 %copy-start.7 = (bf16[256,768]{1,0:T(8,128)(2,1)S(1)}, bf16[256,768]{1,0:T(8,128)(2,1)}, u32[]{:S(2)}) copy-start(bf16[256,768]{1,0:T(8,128)(2,1)} %q_ref.3) | copy-start | bytes 1179652
  91.7 41.6 %all-to-all-start.4 = ((bf16[8,144,768]{2,1,0:T(8,128)(2,1)}), bf16[8,144,768]{2,1,0:T(8,128)(2,1)S(1)}, u32[]{:S(2)}, u32[]{:S(2)}) async-start(bf16[8,144,768]{2,1,0:T(8,128)(2,1)} %cut_up.1), calls=%async_computation.4 | async-start | bytes 3538944 | tf_op jit(solution)/shard_map/all_to_all | solution.py:279
  149.5 40.5 %all-to-all-start.6 = ((bf16[8,96,1152]{2,1,0:T(8,128)(2,1)}), bf16[8,96,1152]{2,1,0:T(8,128)(2,1)S(1)}, u32[]{:S(2)}, u32[]{:S(2)}) async-start(bf16[8,96,1152]{2,1,0:T(8,128)(2,1)} %cut_down.1), calls=%async_computation.6 | async-start | bytes 3538944 | tf_op jit(solution)/shard_map/all_to_all | solution.py:292
  190.0 12.8 %copy-start.8 = (bf16[6144,1]{0,1:T(2,128)(2,1)S(1)}, bf16[6144,1]{0,1:T(2,128)(2,1)}, u32[]{:S(2)}) copy-start(bf16[6144,1]{0,1:T(2,128)(2,1)} %param.11) | copy-start | bytes 36868
  192.4 32.2 %all-to-all-start.7 = ((bf16[64,32,128]{2,1,0:T(8,128)(2,1)}), bf16[64,32,128]{2,1,0:T(8,128)(2,1)S(1)}, u32[]{:S(2)}, u32[]{:S(2)}) async-start(bf16[64,32,128]{2,1,0:T(8,128)(2,1)} %down.1), calls=%async_computation.7 | async-start | bytes 1048576 | tf_op jit(solution)/shard_map/all_to_all | solution.py:302
  225.5 32.0 %all-to-all-start.8 = ((bf16[8,32,128]{2,1,0:T(8,128)(2,1)}), bf16[8,32,128]{2,1,0:T(8,128)(2,1)S(1)}, u32[]{:S(2)}, u32[]{:S(2)}) async-start(bf16[8,32,128]{2,1,0:T(8,128)(2,1)} %weigh.1), calls=%async_computation.8 | async-start | bytes 131072 | tf_op jit(solution)/shard_map/all_to_all | solution.py:306

commit v5 on v4

--- a/solution.py
+++ b/solution.py
@@ -1,3 +1,5 @@
+import functools
+
 import jax
 import jax.numpy as jnp
 from jax import lax
@@ -14,6 +16,8 @@
 
 
 HBM = pltpu.HBM
+SMEM = pltpu.SMEM
+VMEM = pltpu.VMEM
 
 
 def call(kernel, out, *args, scratch=(), spaces=None, name=None):
@@ -131,34 +135,82 @@
     pay_ref[...] = picks[...].reshape(8, SLOTS, LANES).astype(BF16)
 
 
-def cut_up_kernel(w_ref, out_ref, sems):
-    width = out_ref.shape[2]
+def piece_of(k, outs):
+    for first, out in zip((4, 2, 1, 0), outs):
+        if k >= first:
+            return out.at[k - first]
+
+
+def cut_up_kernel(order_ref, w_ref, *refs):
+    outs, sems = refs[:4], refs[4]
+    width = outs[0].shape[2]
     copies = []
-    for part in range(8):
-        source = w_ref.at[:, part * width : (part + 1) * width]
-        copies.append(pltpu.make_async_copy(source, out_ref.at[part], sems.at[part]))
+    for k in range(8):
+        low = pl.multiple_of(order_ref[k] * width, LANES)
+        source = w_ref.at[:, pl.ds(low, width)]
+        copies.append(pltpu.make_async_copy(source, piece_of(k, outs), sems.at[k]))
         copies[-1].start()
     for copy in copies:
         copy.wait()
 
 
-def cut_down_kernel(w_ref, out_ref):
+def cut_down_kernel(order_ref, w_ref, *refs):
+    outs, cut, sems = refs[:4], refs[4], refs[5]
     run = w_ref.shape[1] // 64
     for part in range(8):
         for group in range(8):
             low = (group * 8 + part) * run
-            out_ref[part, :, group * run : (group + 1) * run] = w_ref[:, low : low + run]
-
-
-def up_kernel(x_ref, w_ref, out_ref, rows, picked):
+            cut[part, :, group * run : (group + 1) * run] = w_ref[:, low : low + run]
+    copies = []
+    for k in range(8):
+        source = cut.at[order_ref[k]]
+        copies.append(pltpu.make_async_copy(source, piece_of(k, outs), sems.at[k]))
+        copies[-1].start()
+    for copy in copies:
+        copy.wait()
+
+
+def join_kernel(plan, *refs):
+    out, sems = refs[-2:]
+    copies = []
+    for n, (which, row) in enumerate(plan):
+        copies.append(pltpu.make_async_copy(refs[which].at[row], out.at[n], sems.at[n]))
+        copies[-1].start()
+    for copy in copies:
+        copy.wait()
+
+
+def fetch(order_ref, held, first, second, third, whole, sems):
+    rows = held.shape[1]
+    copies = []
+    for k in range(8):
+        one, two, three = k >> 2, k >> 1 & 1, k & 1
+        if three:
+            source = third.at[one * 2 + two]
+        elif two:
+            source = second.at[one * 2]
+        elif one:
+            source = first.at[0]
+        else:
+            source = held.at[0]
+        low = pl.multiple_of(order_ref[k] * rows, 16)
+        copies.append(pltpu.make_async_copy(source, whole.at[pl.ds(low, rows), :], sems.at[k]))
+        copies[-1].start()
+    return copies
+
+
+def up_kernel(order_ref, x_ref, w0, w1, w2, w3, out_ref, rows, picked, whole, sems):
+    copies = fetch(order_ref, w0, w1, w2, w3, whole, sems)
     rows[...] = x_ref[...].astype(F32).reshape(64 * SLOTS, LANES)
     picked[320:] = jnp.zeros((64, picked.shape[1]), BF16)
     for i in range(5):
         for tile in range(6):
             piece = rows[pl.ds(i * 6 + tile, 64, stride=SLOTS), :]
             picked[i * 64 : i * 64 + 64, tile * LANES : (tile + 1) * LANES] = piece.astype(BF16)
+    for copy in copies:
+        copy.wait()
     out_ref[...] = lax.dot_general(
-        w_ref[...], picked[...], (((1,), (1,)), ((), ())), preferred_element_type=F32
+        whole[...], picked[...], (((1,), (1,)), ((), ())), preferred_element_type=F32
     ).astype(BF16)
 
 
@@ -169,11 +221,14 @@
     out_ref[...] = (up / (1.0 + jnp.exp(-up))).astype(BF16)
 
 
-def down_kernel(h_ref, w_ref, out_ref, rows):
+def down_kernel(order_ref, h_ref, w0, w1, w2, w3, out_ref, rows, whole, sems):
+    copies = fetch(order_ref, w0, w1, w2, w3, whole, sems)
     for slot in (30, 31):
         rows[pl.ds(slot, 64, stride=SLOTS), :] = jnp.zeros((64, LANES), F32)
+    for copy in copies:
+        copy.wait()
     y = lax.dot_general(
-        h_ref[...], w_ref[...], (((0,), (1,)), ((), ())), preferred_element_type=F32
+        h_ref[...], whole[...], (((0,), (1,)), ((), ())), preferred_element_type=F32
     )
     for i in range(5):
         for tile in range(6):
@@ -220,6 +275,47 @@
     return jax.ShapeDtypeStruct(dims, dtype)
 
 
+def neighbour(place, mask):
+    code = place ^ (place >> 1 & 1)
+    code = code ^ mask
+    return code ^ (code >> 1 & 1)
+
+
+def swap_with(array, mask):
+    return lax.ppermute(array, "c", [(c, neighbour(c, mask)) for c in range(8)])
+
+
+def order_of(masks):
+    place = lax.axis_index("c").astype(jnp.int32)
+    masks = [
+        (k >> 2) * masks[0] + (k >> 1 & 1) * masks[1] + (k & 1) * masks[2] for k in range(8)
+    ]
+    return neighbour(place, jnp.asarray(masks, jnp.int32))
+
+
+UP_MASKS = (1, 2, 4)
+DOWN_MASKS = (4, 1, 2)
+
+
+def join(plan, *arrays):
+    return call(
+        functools.partial(join_kernel, plan),
+        shape((len(plan), *arrays[0].shape[1:])),
+        *arrays,
+        scratch=[pltpu.SemaphoreType.DMA((len(plan),))],
+        spaces=([HBM] * len(arrays), HBM),
+        name="join",
+    )
+
+
+def second_half(held, first):
+    return join([(0, 0), (0, 1), (1, 2), (1, 3)], held, first)
+
+
+def third_half(held, first, second):
+    return join([(0, 0), (2, 1), (1, 1), (2, 3)], held, first, second)
+
+
 def body(queries, keys, values, selections, router, w_up, w_down):
     length, width = queries.shape
     parts = lax.axis_size("p")
@@ -241,23 +337,40 @@
         scratch=[pltpu.VMEM((width, width), F32), pltpu.VMEM((64 * 16, LANES), F32)],
         name="state",
     )
+    up_order, down_order = order_of(UP_MASKS), order_of(DOWN_MASKS)
     w_up, w_down, state = lax.optimization_barrier((w_up, w_down, state))
     chunks = lax.all_to_all(state, seq, 0, 0, tiled=True)
     inner = call(inner_kernel, shape((length, width), F32), queries, keys, values, name="inner")
-    up_cut = call(
+    up_0 = call(
         cut_up_kernel,
-        shape((8, units, width)),
+        [shape((n, units, width)) for n in (4, 2, 1, 1)],
+        up_order,
         w_up[0],
         scratch=[pltpu.SemaphoreType.DMA((8,))],
-        spaces=([HBM], HBM),
+        spaces=([SMEM, HBM], [HBM] * 4),
         name="cut_up",
     )
-    chunks, inner, up_cut = lax.optimization_barrier((chunks, inner, up_cut))
+    up_1 = swap_with(up_0[0], UP_MASKS[0])
+    down_0 = call(
+        cut_down_kernel,
+        [shape((n, columns, group)) for n in (4, 2, 1, 1)],
+        down_order,
+        w_down[0],
+        scratch=[pltpu.VMEM((8, columns, group), BF16), pltpu.SemaphoreType.DMA((8,))],
+        spaces=([SMEM, VMEM], [HBM] * 4),
+        name="cut_down",
+    )
+    chunks, inner, up_0, up_1, down_0 = lax.optimization_barrier(
+        (chunks, inner, up_0, up_1, down_0)
+    )
     before = call(prefix_kernel, shape((64, 16, LANES)), chunks, name="prefix")
-    before, w_down = lax.optimization_barrier((before, w_down))
+    before, up_0, up_1, down_0 = lax.optimization_barrier((before, up_0, up_1, down_0))
     before = lax.all_to_all(before, seq, 0, 0, tiled=True)
-    down_cut = call(cut_down_kernel, shape((8, columns, group)), w_down[0], name="cut_down")
-    before, down_cut = lax.optimization_barrier((before, down_cut))
+    up_2 = swap_with(second_half(up_0[1], up_1), UP_MASKS[1])
+    down_1 = swap_with(down_0[0], DOWN_MASKS[0])
+    before, up_0, up_1, up_2, down_0, down_1 = lax.optimization_barrier(
+        (before, up_0, up_1, up_2, down_0, down_1)
+    )
     attn, pay = call(
         attn_kernel,
         (shape((length, width)), shape((8, SLOTS, LANES))),
@@ -273,30 +386,55 @@
         ],
         name="attn",
     )
+    pay, up_0, up_1, up_2, down_0, down_1 = lax.optimization_barrier(
+        (pay, up_0, up_1, up_2, down_0, down_1)
+    )
     whole_rows = lax.all_to_all(pay, "p", 0, 0, tiled=True)
+    up_3 = swap_with(third_half(up_0[2], up_1, up_2), UP_MASKS[2])
+    down_2 = swap_with(second_half(down_0[1], down_1), DOWN_MASKS[1])
     near_rows = lax.all_to_all(whole_rows, "c", 0, 0, tiled=True)
-    near_rows, up_cut = lax.optimization_barrier((near_rows, up_cut))
-    up_mine = lax.all_to_all(up_cut, "c", 0, 0, tiled=True).reshape(8 * units, width)
+    near_rows, up_3, down_0, down_1, down_2 = lax.optimization_barrier(
+        (near_rows, up_3, down_0, down_1, down_2)
+    )
+    down_3 = swap_with(third_half(down_0[2], down_1, down_2), DOWN_MASKS[2])
     arrived = lax.all_gather(near_rows, "r", axis=0, tiled=True)
+    arrived, down_3 = lax.optimization_barrier((arrived, down_3))
     partial = call(
         up_kernel,
         shape((8 * units, 384)),
+        up_order,
         arrived,
-        up_mine,
-        scratch=[pltpu.VMEM((64 * SLOTS, LANES), F32), pltpu.VMEM((384, width), BF16)],
+        up_0[3],
+        up_1,
+        up_2,
+        up_3,
+        scratch=[
+            pltpu.VMEM((64 * SLOTS, LANES), F32),
+            pltpu.VMEM((384, width), BF16),
+            pltpu.VMEM((8 * units, width), BF16),
+            pltpu.SemaphoreType.DMA((8,)),
+        ],
+        spaces=([SMEM, VMEM] + [HBM] * 4, VMEM),
         name="up",
     )
     sums = lax.all_to_all(partial.reshape(8, units, 384), "c", 0, 0, tiled=True)
     act = call(act_kernel, shape((units, 384)), sums, name="act")
-    act, down_cut = lax.optimization_barrier((act, down_cut))
-    down_mine = lax.all_to_all(down_cut, "c", 0, 0, tiled=True).reshape(8 * columns, group)
     act = lax.all_gather(act, "r", axis=0, tiled=True)
     out = call(
         down_kernel,
         shape((64, SLOTS, LANES)),
+        down_order,
         act,
-        down_mine,
-        scratch=[pltpu.VMEM((64 * SLOTS, LANES), F32)],
+        down_0[3],
+        down_1,
+        down_2,
+        down_3,
+        scratch=[
+            pltpu.VMEM((64 * SLOTS, LANES), F32),
+            pltpu.VMEM((8 * columns, group), BF16),
+            pltpu.SemaphoreType.DMA((8,)),
+        ],
+        spaces=([SMEM, VMEM] + [HBM] * 4, VMEM),
         name="down",
     )
     back = lax.all_to_all(out, seq, 0, 0, tiled=True)

time: 259 us -> 273 us (1.054)
  blocking collectives: 112 us -> 89.5 us
  Pallas kernels: 13.2 us -> 26.9 us
  starting transfers between devices: 71.3 us -> 82.3 us
  local copies, waits for them, and re-layouts: 6.81 us -> 12 us
  waiting for transfers between devices: 55.2 us -> 59.7 us
    ppermute x0 -> x6, waiting for transfers between devices: none -> 33.2 us  [swap_with(): return lax.ppermute(array, 'c', [(c, neighbour(c, mask)) for c in range(8)])]
    ppermute x0 -> x6, starting transfers between devices: none -> 19.6 us  [swap_with(): return lax.ppermute(array, 'c', [(c, neighbour(c, mask)) for c in range(8)])]
    all_to_all x1, waiting for transfers between devices: 14.8 us -> 0.01 us  [body(): before = lax.all_to_all(before, seq, 0, 0, tiled=True)]
    all_to_all x1, waiting for transfers between devices: 13.9 us -> 0.01 us  [body(): chunks = lax.all_to_all(state, seq, 0, 0, tiled=True)]
    pallas_call x11 -> x15, Pallas kernels: 13.2 us -> 26.9 us  [call(): pl.pallas_call(kernel, out_shape=out, scratch_shapes=list(scratch), compi...]
    all_gather x1, blocking collectives: 38 us -> 27 us  [body(): arrived = lax.all_gather(near_rows, 'r', axis=0, tiled=True)]
    all_gather x1, blocking collectives: 36.9 us -> 27.1 us  [body(): act = lax.all_gather(act, 'r', axis=0, tiled=True)]
    all_to_all x2 -> x0, starting transfers between devices: 7.19 us -> none  [the longest x1 3.6 us: body(): lax.all_to_all(down_cut, 'c', 0, 0, tiled=True).reshape(8 * columns, group)]
  transfers between devices with their start and end apart: 6 -> 10, of which waited for: 4 -> 5; matrix products, arithmetic and copies ran while one was open for 0% -> 0% of each run, Pallas kernels for 2% -> 3%
where the time goes in v5:
time: 273 us; the launch traced here: 271 us
  blocking collectives  89.5 us (33%)
  starting transfers between devices  82.3 us (30%)
  waiting for transfers between devices  59.7 us (22%)
  Pallas kernels  26.9 us (10%)
  local copies, waits for them, and re-layouts  12 us (4%)
    ppermute x6, waiting for transfers between devices, swap_with(): return lax.ppermute(array, 'c', [(c, neighbour(c, mask)) for c in range(8)])  33.2 us
    all_gather x1, blocking collectives, body(): act = lax.all_gather(act, 'r', axis=0, tiled=True)  27.1 us
    all_gather x1, blocking collectives, body(): arrived = lax.all_gather(near_rows, 'r', axis=0, tiled=True)  27 us
    pallas_call x15, Pallas kernels, call(): pl.pallas_call(kernel, out_shape=out, scratch_shapes=list(scratch), compi...  26.9 us
    all_to_all x1, starting transfers between devices, body(): weighted = lax.all_to_all(weighted, 'p', 0, 0, tiled=True)  22.2 us
    all_to_all x1, waiting for transfers between devices, body(): back = lax.all_to_all(out, seq, 0, 0, tiled=True)  21.6 us
    ppermute x6, starting transfers between devices, swap_with(): return lax.ppermute(array, 'c', [(c, neighbour(c, mask)) for c in range(8)])  19.6 us
    all_to_all x1, starting transfers between devices, body(): chunks = lax.all_to_all(state, seq, 0, 0, tiled=True)  19.5 us
  transfers between devices with their start and end apart: 10, of which 5 were waited for; matrix products, arithmetic and copies ran while one was open for 0% of the time, Pallas kernels for 3%

profile of v5, /device:TPU:1, one launch (start us, length us, event | category | flops | bytes accessed | tf_op | source)
XLA Modules:
  0.0 271.5 jit_solution(13249838885026873860)
XLA Ops:
  0.0 1.0 copy-done.2
  1.0 1.0 copy-done.4
  2.0 1.3 state.1
  3.3 19.5 %all-to-all-start = ((bf16[64,16,128]{2,1,0:T(8,128)(2,1)}), bf16[64,16,128]{2,1,0:T(8,128)(2,1)}, u32[]{:S(2)}, u32[]{:S(2)}) async-start(bf16[64,16,128]{2,1,0:T(8,128)(2,1)} %state.1), calls=%async_computation | async-start | bytes 524288 | tf_op jit(solution)/shard_map/all_to_all | solution.py:342
  22.8 0.7 xor_xor_fusion
  23.5 1.5 copy-done
  25.0 0.9 cut_up.1
  25.9 2.8 %collective-permute-start = (bf16[4,144,768]{2,1,0:T(8,128)(2,1)S(1)}, bf16[4,144,768]{2,1,0:T(8,128)(2,1)S(1)}, u32[]{:S(2)}, u32[]{:S(2)}) collective-permute-start(bf16[4,144,768]{2,1,0:T(8,128)(2,1)S(1)} %get-tuple-element.65), channel_id=1, source_target_pairs={{0,8},{8,0},{16,24},{24,16},{32,40},{40,32},{48,56},{56,48},{1,9},... | collective-permute-start | bytes 2654216 | tf_op jit(solution)/shard_map/ppermute | solution.py:285
  28.8 1.0 copy-done.3
  29.8 1.0 copy-done.5
  30.8 1.0 copy-done.6
  31.8 0.9 inner.1.inner_ref
  32.7 3.5 %cut_down.1 = (bf16[4,96,1152]{2,1,0:T(8,128)(2,1)}, bf16[2,96,1152]{2,1,0:T(8,128)(2,1)S(1)}, bf16[1,96,1152]{2,1,0:T(8,128)(2,1)S(1)}, bf16[1,96,1152]{2,1,0:T(8,128)(2,1)S(1)}) custom-call(s32[8]{0:T(128)S(1)} %get-tuple-element.121.order_ref, bf16[96,9216]{1,0:T(8,128)(2,1)S(1)} %bitcast.13), custom_call_target="tpu_custom_call" | custom-call | tf_op jit(solution)/shard_map/cut_down/pallas_call | solution.py:33
  36.2 0.8 copy-done.8
  37.0 0.7 copy-done.14
  37.7 0.7 copy-done.18
  38.3 11.8 %collective-permute-done.refs_1_.w1 = bf16[4,144,768]{2,1,0:T(8,128)(2,1)S(1)} collective-permute-done((bf16[4,144,768]{2,1,0:T(8,128)(2,1)S(1)}, bf16[4,144,768]{2,1,0:T(8,128)(2,1)S(1)}, u32[]{:S(2)}, u32[]{:S(2)}) %collective-permute-start) | collective-permute-done | bytes 884768 | tf_op jit(solution)/shard_map/ppermute | solution.py:285
  50.1 1.7 prefix.1
  51.8 13.7 %all-to-all-start.1 = ((bf16[64,16,128]{2,1,0:T(8,128)(2,1)}), bf16[64,16,128]{2,1,0:T(8,128)(2,1)}, u32[]{:S(2)}, u32[]{:S(2)}) async-start(bf16[64,16,128]{2,1,0:T(8,128)(2,1)} %prefix.1), calls=%async_computation.1 | async-start | bytes 524288 | tf_op jit(solution)/shard_map/all_to_all | solution.py:368
  65.5 1.0 copy-done.11
  66.5 1.0 join.4
  67.5 4.1 %collective-permute-start.1 = (bf16[4,144,768]{2,1,0:T(8,128)(2,1)}, bf16[4,144,768]{2,1,0:T(8,128)(2,1)S(1)}, u32[]{:S(2)}, u32[]{:S(2)}) collective-permute-start(bf16[4,144,768]{2,1,0:T(8,128)(2,1)} %join.4), channel_id=1, source_target_pairs={{0,24},{8,16},{16,8},{24,0},{32,56},{40,48},{48,40},{56,32},{1,25}... | collective-permute-start | bytes 2654216 | tf_op jit(solution)/shard_map/ppermute | solution.py:285
  71.6 3.1 %collective-permute-start.2 = (bf16[4,96,1152]{2,1,0:T(8,128)(2,1)}, bf16[4,96,1152]{2,1,0:T(8,128)(2,1)S(1)}, u32[]{:S(2)}, u32[]{:S(2)}) collective-permute-start(bf16[4,96,1152]{2,1,0:T(8,128)(2,1)} %get-tuple-element.89), channel_id=1, source_target_pairs={{0,32},{8,40},{16,48},{24,56},{32,0},{40,8},{48,16},{56,24},{1,33}... | collective-permute-start | bytes 2654216 | tf_op jit(solution)/shard_map/ppermute | solution.py:285
  74.8 17.8 %collective-permute-done.1.refs_2_.w2 = bf16[4,144,768]{2,1,0:T(8,128)(2,1)S(1)} collective-permute-done((bf16[4,144,768]{2,1,0:T(8,128)(2,1)}, bf16[4,144,768]{2,1,0:T(8,128)(2,1)S(1)}, u32[]{:S(2)}, u32[]{:S(2)}) %collective-permute-start.1) | collective-permute-done | bytes 884768 | tf_op jit(solution)/shard_map/ppermute | solution.py:285
  92.6 3.7 %collective-permute-done.2.refs_1_.w1 = bf16[4,96,1152]{2,1,0:T(8,128)(2,1)S(1)} collective-permute-done((bf16[4,96,1152]{2,1,0:T(8,128)(2,1)}, bf16[4,96,1152]{2,1,0:T(8,128)(2,1)S(1)}, u32[]{:S(2)}, u32[]{:S(2)}) %collective-permute-start.2) | collective-permute-done | bytes 884768 | tf_op jit(solution)/shard_map/ppermute | solution.py:285
  96.3 1.0 copy-done.7
  97.3 2.1 attn.1
  99.4 1.1 copy-done.9
  100.5 1.1 join.6
  101.7 3.6 %collective-permute-start.4 = (bf16[4,96,1152]{2,1,0:T(8,128)(2,1)S(1)}, bf16[4,96,1152]{2,1,0:T(8,128)(2,1)S(1)}, u32[]{:S(2)}, u32[]{:S(2)}) collective-permute-start(bf16[4,96,1152]{2,1,0:T(8,128)(2,1)S(1)} %join.6), channel_id=1, source_target_pairs={{0,8},{8,0},{16,24},{24,16},{32,40},{40,32},{48,56},{56,48},{1,9},... | collective-permute-start | bytes 2654216 | tf_op jit(solution)/shard_map/ppermute | solution.py:285
  105.4 1.2 join.5
  106.5 3.3 %collective-permute-start.3 = (bf16[4,144,768]{2,1,0:T(8,128)(2,1)S(1)}, bf16[4,144,768]{2,1,0:T(8,128)(2,1)S(1)}, u32[]{:S(2)}, u32[]{:S(2)}) collective-permute-start(bf16[4,144,768]{2,1,0:T(8,128)(2,1)S(1)} %join.5), channel_id=1, source_target_pairs={{0,32},{8,40},{16,48},{24,56},{32,0},{40,8},{48,16},{56,24},{1,33}... | collective-permute-start | bytes 2654216 | tf_op jit(solution)/shard_map/ppermute | solution.py:285
  109.8 10.7 %all_to_all.35.row_ref = bf16[8,32,128]{2,1,0:T(8,128)(2,1)S(1)} all-to-all(bf16[8,32,128]{2,1,0:T(8,128)(2,1)S(1)} %get-tuple-element.104), channel_id=1, replica_groups=mesh['r'=8,'c'=8,'p'=8] {'p'}, dimensions={0} | all-to-all | bytes 131072 | tf_op jit(solution)/shard_map/all_to_all | solution.py:392
  120.5 10.5 %all_to_all.36 = bf16[8,32,128]{2,1,0:T(8,128)(2,1)S(1)} all-to-all(bf16[8,32,128]{2,1,0:T(8,128)(2,1)S(1)} %all_to_all.35.row_ref), channel_id=1, replica_groups=mesh['r'=8,'c'=8,'p'=8] {'c'}, dimensions={0} | all-to-all | bytes 131072 | tf_op jit(solution)/shard_map/all_to_all | solution.py:395
  131.0 1.2 join.7
  132.2 2.7 collective-permute-start.5
  134.8 27.0 %all_gather.6.x_ref = bf16[64,32,128]{2,1,0:T(8,128)(2,1)S(1)} all-gather(bf16[8,32,128]{2,1,0:T(8,128)(2,1)S(1)} %all_to_all.36), channel_id=1, replica_groups=mesh['r'=8,'c'=8,'p'=8] {'r'}, dimensions={0}, use_global_device_ids=true | all-gather | bytes 589824 | tf_op jit(solution)/shard_map/all_gather | solution.py:400
  161.8 4.7 %up.1 = bf16[1152,384]{1,0:T(8,128)(2,1)S(1)} custom-call(s32[8]{0:T(128)S(1)} %get-tuple-element.122.order_ref, bf16[64,32,128]{2,1,0:T(8,128)(2,1)S(1)} %all_gather.6.x_ref, bf16[1,144,768]{2,1,0:T(8,128)(2,1)S(1)} %copy-done.21, bf16[4,144,768]{2,1,0:T(8,128)(2,1)S(1)} %collective-permute-done.refs_1_.w1, ...), custom_call_target="tpu_custom_call" | custom-call | tf_op jit(solution)/shard_map/up/pallas_call | solution.py:33
  166.5 14.3 %all_to_all.37.in_ref = bf16[8,144,384]{2,1,0:T(8,128)(2,1)S(1)} all-to-all(bf16[8,144,384]{2,1,0:T(8,128)(2,1)S(1)} %bitcast.11), channel_id=1, replica_groups=mesh['r'=8,'c'=8,'p'=8] {'c'}, dimensions={0} | all-to-all | bytes 1769472 | tf_op jit(solution)/shard_map/all_to_all | solution.py:420
  180.8 0.2 act.1
  181.0 27.1 %all_gather.7.h_ref = bf16[1152,384]{1,0:T(8,128)(2,1)S(1)} all-gather(bf16[144,384]{1,0:T(8,128)(2,1)S(1)} %act.1), channel_id=1, replica_groups=mesh['r'=8,'c'=8,'p'=8] {'r'}, dimensions={0}, use_global_device_ids=true | all-gather | bytes 995328 | tf_op jit(solution)/shard_map/all_gather | solution.py:422
  208.1 5.3 %down.1 = bf16[64,32,128]{2,1,0:T(8,128)(2,1)} custom-call(s32[8]{0:T(128)S(1)} %get-tuple-element.121.order_ref, bf16[1152,384]{1,0:T(8,128)(2,1)S(1)} %all_gather.7.h_ref, bf16[1,96,1152]{2,1,0:T(8,128)(2,1)S(1)} %copy-done.19, bf16[4,96,1152]{2,1,0:T(8,128)(2,1)S(1)} %collective-permute-done.2.refs_1_.w1, ...), custom_call_target="tpu_custom_call" | custom-call | tf_op jit(solution)/shard_map/down/pallas_call | solution.py:33
  213.4 7.3 %all-to-all-start.5 = ((bf16[64,32,128]{2,1,0:T(8,128)(2,1)}), bf16[64,32,128]{2,1,0:T(8,128)(2,1)S(1)}, u32[]{:S(2)}, u32[]{:S(2)}) async-start(bf16[64,32,128]{2,1,0:T(8,128)(2,1)} %down.1), calls=%async_computation.5 | async-start | bytes 1048576 | tf_op jit(solution)/shard_map/all_to_all | solution.py:440
  220.9 21.6 %all-to-all-done.5.y_ref = bf16[64,32,128]{2,1,0:T(8,128)(2,1)S(1)} async-done(((bf16[64,32,128]{2,1,0:T(8,128)(2,1)}), bf16[64,32,128]{2,1,0:T(8,128)(2,1)S(1)}, u32[]{:S(2)}, u32[]{:S(2)}) %all-to-all-start.5) | async-done | bytes 524320 | tf_op jit(solution)/shard_map/all_to_all | solution.py:440
  242.5 0.9 weigh.1
  243.4 22.2 %all-to-all-start.6 = ((bf16[8,32,128]{2,1,0:T(8,128)(2,1)}), bf16[8,32,128]{2,1,0:T(8,128)(2,1)S(1)}, u32[]{:S(2)}, u32[]{:S(2)}) async-start(bf16[8,32,128]{2,1,0:T(8,128)(2,1)} %weigh.1), calls=%async_computation.6 | async-start | bytes 131072 | tf_op jit(solution)/shard_map/all_to_all | solution.py:444
  265.6 4.8 %all-to-all-done.6.y_ref = bf16[8,32,128]{2,1,0:T(8,128)(2,1)S(1)} async-done(((bf16[8,32,128]{2,1,0:T(8,128)(2,1)}), bf16[8,32,128]{2,1,0:T(8,128)(2,1)S(1)}, u32[]{:S(2)}, u32[]{:S(2)}) %all-to-all-start.6) | async-done | bytes 65568 | tf_op jit(solution)/shard_map/all_to_all | solution.py:444
  270.4 1.0 add.6
  (51 shorter events, 0.4 us)
Async XLA Ops:
  0.0 1.0 copy-start.2
  1.0 1.0 copy-start.4
  3.3 46.9 %all-to-all-start = ((bf16[64,16,128]{2,1,0:T(8,128)(2,1)}), bf16[64,16,128]{2,1,0:T(8,128)(2,1)}, u32[]{:S(2)}, u32[]{:S(2)}) async-start(bf16[64,16,128]{2,1,0:T(8,128)(2,1)} %state.1), calls=%async_computation | async-start | bytes 524288 | tf_op jit(solution)/shard_map/all_to_all | solution.py:342
  23.5 1.5 copy-start
  25.0 7.8 %copy-start.1 = (bf16[1,96,9216]{2,1,0:T(8,128)(2,1)S(1)}, bf16[1,96,9216]{2,1,0:T(8,128)(2,1)}, u32[]{:S(2)}) copy-start(bf16[1,96,9216]{2,1,0:T(8,128)(2,1)} %param.15) | copy-start | bytes 5308420
  25.9 6.8 %copy-start.10 = (bf16[2,144,768]{2,1,0:T(8,128)(2,1)}, bf16[2,144,768]{2,1,0:T(8,128)(2,1)S(1)}, u32[]{:S(2)}) copy-start(bf16[2,144,768]{2,1,0:T(8,128)(2,1)S(1)} %get-tuple-element.85.refs_0_) | copy-start | bytes 1327108
  25.9 6.8 %copy-start.16 = (bf16[1,144,768]{2,1,0:T(8,128)(2,1)}, bf16[1,144,768]{2,1,0:T(8,128)(2,1)S(1)}, u32[]{:S(2)}) copy-start(bf16[1,144,768]{2,1,0:T(8,128)(2,1)S(1)} %get-tuple-element.105.refs_0_) | copy-start | bytes 663556
  25.9 10.3 %copy-start.20 = (bf16[1,144,768]{2,1,0:T(8,128)(2,1)}, bf16[1,144,768]{2,1,0:T(8,128)(2,1)S(1)}, u32[]{:S(2)}) copy-start(bf16[1,144,768]{2,1,0:T(8,128)(2,1)S(1)} %get-tuple-element.117.w0) | copy-start | bytes 663556
  25.9 24.2 %collective-permute-start = (bf16[4,144,768]{2,1,0:T(8,128)(2,1)S(1)}, bf16[4,144,768]{2,1,0:T(8,128)(2,1)S(1)}, u32[]{:S(2)}, u32[]{:S(2)}) collective-permute-start(bf16[4,144,768]{2,1,0:T(8,128)(2,1)S(1)} %get-tuple-element.65), channel_id=1, source_target_pairs={{0,8},{8,0},{16,24},{24,16},{32,40},{40,32},{48,56},{56,48},{1,9},... | collective-permute-start | bytes 2654216 | tf_op jit(solution)/shard_map/ppermute | solution.py:285
  28.8 1.0 copy-start.3
  29.8 1.0 copy-start.5
  30.8 1.0 copy-start.6
  36.2 0.8 copy-start.8
  37.0 0.7 copy-start.14
  37.7 0.7 copy-start.18
  38.3 36.4 %copy-start.23 = (s32[1,8,5]{1,0,2:T(1,128)S(1)}, s32[1,8,5]{1,0,2:T(1,128)}, u32[]{:S(2)}) copy-start(s32[1,8,5]{1,0,2:T(1,128)} %param.12) | copy-start | bytes 484
  51.8 44.4 %all-to-all-start.1 = ((bf16[64,16,128]{2,1,0:T(8,128)(2,1)}), bf16[64,16,128]{2,1,0:T(8,128)(2,1)}, u32[]{:S(2)}, u32[]{:S(2)}) async-start(bf16[64,16,128]{2,1,0:T(8,128)(2,1)} %prefix.1), calls=%async_computation.1 | async-start | bytes 524288 | tf_op jit(solution)/shard_map/all_to_all | solution.py:368
  65.5 1.0 copy-start.11
  67.5 25.1 %collective-permute-start.1 = (bf16[4,144,768]{2,1,0:T(8,128)(2,1)}, bf16[4,144,768]{2,1,0:T(8,128)(2,1)S(1)}, u32[]{:S(2)}, u32[]{:S(2)}) collective-permute-start(bf16[4,144,768]{2,1,0:T(8,128)(2,1)} %join.4), channel_id=1, source_target_pairs={{0,24},{8,16},{16,8},{24,0},{32,56},{40,48},{48,40},{56,32},{1,25}... | collective-permute-start | bytes 2654216 | tf_op jit(solution)/shard_map/ppermute | solution.py:285
  71.6 24.7 %collective-permute-start.2 = (bf16[4,96,1152]{2,1,0:T(8,128)(2,1)}, bf16[4,96,1152]{2,1,0:T(8,128)(2,1)S(1)}, u32[]{:S(2)}, u32[]{:S(2)}) collective-permute-start(bf16[4,96,1152]{2,1,0:T(8,128)(2,1)} %get-tuple-element.89), channel_id=1, source_target_pairs={{0,32},{8,40},{16,48},{24,56},{32,0},{40,8},{48,16},{56,24},{1,33}... | collective-permute-start | bytes 2654216 | tf_op jit(solution)/shard_map/ppermute | solution.py:285
  96.3 1.0 copy-start.7
  97.3 8.1 %copy-start.17 = (bf16[1,144,768]{2,1,0:T(8,128)(2,1)S(1)}, bf16[1,144,768]{2,1,0:T(8,128)(2,1)}, u32[]{:S(2)}) copy-start(bf16[1,144,768]{2,1,0:T(8,128)(2,1)} %copy-done.16) | copy-start | bytes 663556
  99.4 2.3 copy-start.12
  99.4 1.2 copy-start.9
  101.7 29.3 %copy-start.15 = (bf16[1,96,1152]{2,1,0:T(8,128)(2,1)S(1)}, bf16[1,96,1152]{2,1,0:T(8,128)(2,1)}, u32[]{:S(2)}) copy-start(bf16[1,96,1152]{2,1,0:T(8,128)(2,1)} %copy-done.14) | copy-start | bytes 663556
  101.7 29.3 %collective-permute-start.4 = (bf16[4,96,1152]{2,1,0:T(8,128)(2,1)S(1)}, bf16[4,96,1152]{2,1,0:T(8,128)(2,1)S(1)}, u32[]{:S(2)}, u32[]{:S(2)}) collective-permute-start(bf16[4,96,1152]{2,1,0:T(8,128)(2,1)S(1)} %join.6), channel_id=1, source_target_pairs={{0,8},{8,0},{16,24},{24,16},{32,40},{40,32},{48,56},{56,48},{1,9},... | collective-permute-start | bytes 2654216 | tf_op jit(solution)/shard_map/ppermute | solution.py:285
  106.5 24.4 %collective-permute-start.3 = (bf16[4,144,768]{2,1,0:T(8,128)(2,1)S(1)}, bf16[4,144,768]{2,1,0:T(8,128)(2,1)S(1)}, u32[]{:S(2)}, u32[]{:S(2)}) collective-permute-start(bf16[4,144,768]{2,1,0:T(8,128)(2,1)S(1)} %join.5), channel_id=1, source_target_pairs={{0,32},{8,40},{16,48},{24,56},{32,0},{40,8},{48,16},{56,24},{1,33}... | collective-permute-start | bytes 2654216 | tf_op jit(solution)/shard_map/ppermute | solution.py:285
  120.5 41.3 %copy-start.21 = (bf16[1,144,768]{2,1,0:T(8,128)(2,1)S(1)}, bf16[1,144,768]{2,1,0:T(8,128)(2,1)}, u32[]{:S(2)}) copy-start(bf16[1,144,768]{2,1,0:T(8,128)(2,1)} %copy-done.20) | copy-start | bytes 663556
  132.2 29.6 %collective-permute-start.5 = (bf16[4,96,1152]{2,1,0:T(8,128)(2,1)S(1)}, bf16[4,96,1152]{2,1,0:T(8,128)(2,1)S(1)}, u32[]{:S(2)}, u32[]{:S(2)}) collective-permute-start(bf16[4,96,1152]{2,1,0:T(8,128)(2,1)S(1)} %join.7), channel_id=1, source_target_pairs={{0,24},{8,16},{16,8},{24,0},{32,56},{40,48},{48,40},{56,32},{1,25}... | collective-permute-start | bytes 2654216 | tf_op jit(solution)/shard_map/ppermute | solution.py:285
  166.5 41.6 %copy-start.19 = (bf16[1,96,1152]{2,1,0:T(8,128)(2,1)S(1)}, bf16[1,96,1152]{2,1,0:T(8,128)(2,1)}, u32[]{:S(2)}) copy-start(bf16[1,96,1152]{2,1,0:T(8,128)(2,1)} %copy-done.18) | copy-start | bytes 663556
  208.1 12.7 %copy-start.22 = (bf16[6144,1]{0,1:T(2,128)(2,1)S(1)}, bf16[6144,1]{0,1:T(2,128)(2,1)}, u32[]{:S(2)}) copy-start(bf16[6144,1]{0,1:T(2,128)(2,1)} %param.13) | copy-start | bytes 36868
  213.4 57.1 %copy-start.13 = (bf16[256,768]{1,0:T(8,128)(2,1)S(1)}, bf16[256,768]{1,0:T(8,128)(2,1)}, u32[]{:S(2)}) copy-start(bf16[256,768]{1,0:T(8,128)(2,1)} %copy-done.12) | copy-start | bytes 1179652
  213.4 29.1 %all-to-all-start.5 = ((bf16[64,32,128]{2,1,0:T(8,128)(2,1)}), bf16[64,32,128]{2,1,0:T(8,128)(2,1)S(1)}, u32[]{:S(2)}, u32[]{:S(2)}) async-start(bf16[64,32,128]{2,1,0:T(8,128)(2,1)} %down.1), calls=%async_computation.5 | async-start | bytes 1048576 | tf_op jit(solution)/shard_map/all_to_all | solution.py:440
  243.4 27.1 %all-to-all-start.6 = ((bf16[8,32,128]{2,1,0:T(8,128)(2,1)}), bf16[8,32,128]{2,1,0:T(8,128)(2,1)S(1)}, u32[]{:S(2)}, u32[]{:S(2)}) async-start(bf16[8,32,128]{2,1,0:T(8,128)(2,1)} %weigh.1), calls=%async_computation.6 | async-start | bytes 131072 | tf_op jit(solution)/shard_map/all_to_all | solution.py:444

commit v6 on v4

--- a/solution.py
+++ b/solution.py
@@ -132,9 +132,9 @@
 
 
 def cut_up_kernel(w_ref, out_ref, sems):
-    width = out_ref.shape[2]
+    parts, width = out_ref.shape[0], out_ref.shape[2]
     copies = []
-    for part in range(8):
+    for part in range(parts):
         source = w_ref.at[:, part * width : (part + 1) * width]
         copies.append(pltpu.make_async_copy(source, out_ref.at[part], sems.at[part]))
         copies[-1].start()
@@ -150,13 +150,24 @@
             out_ref[part, :, group * run : (group + 1) * run] = w_ref[:, low : low + run]
 
 
+def near_kernel(place_ref, row_ref, out_ref, rows):
+    for block in range(4):
+        for part in range(2):
+            low = (block * 2 + part) * 30
+            piece = row_ref[block * 8 + 2 * place_ref[0] + part].astype(F32)
+            rows[low : low + 30] = piece[:30]
+    out_ref[...] = rows[...].astype(BF16)
+
+
 def up_kernel(x_ref, w_ref, out_ref, rows, picked):
-    rows[...] = x_ref[...].astype(F32).reshape(64 * SLOTS, LANES)
+    rows[...] = x_ref[...].astype(F32)
     picked[320:] = jnp.zeros((64, picked.shape[1]), BF16)
     for i in range(5):
-        for tile in range(6):
-            piece = rows[pl.ds(i * 6 + tile, 64, stride=SLOTS), :]
-            picked[i * 64 : i * 64 + 64, tile * LANES : (tile + 1) * LANES] = piece.astype(BF16)
+        for part in range(2):
+            for tile in range(6):
+                piece = rows[pl.ds(part * 30 + i * 6 + tile, 64, stride=60), :]
+                low = (part * 6 + tile) * LANES
+                picked[i * 64 : i * 64 + 64, low : low + LANES] = piece.astype(BF16)
     out_ref[...] = lax.dot_general(
         w_ref[...], picked[...], (((1,), (1,)), ((), ())), preferred_element_type=F32
     ).astype(BF16)
@@ -164,7 +175,7 @@
 
 def act_kernel(in_ref, out_ref):
     up = in_ref[0].astype(F32)
-    for part in range(1, 8):
+    for part in range(1, in_ref.shape[0]):
         up = up + in_ref[part].astype(F32)
     out_ref[...] = (up / (1.0 + jnp.exp(-up))).astype(BF16)
 
@@ -183,10 +194,11 @@
     out_ref[...] = rows[...].reshape(64, SLOTS, LANES).astype(BF16)
 
 
-def weigh_kernel(y_ref, row_ref, router_ref, out_ref):
+def weigh_kernel(place_ref, y_ref, row_ref, router_ref, out_ref):
     products = jnp.zeros((SLOTS, LANES), F32)
+    own = place_ref[0] * 8
     for part in range(8):
-        products = products + row_ref[part].astype(F32) * router_ref[part].astype(F32)
+        products = products + row_ref[own + part].astype(F32) * router_ref[part].astype(F32)
     one = lax.broadcasted_iota(jnp.int32, (SLOTS, SLOTS), 0) // 6
     two = lax.broadcasted_iota(jnp.int32, (SLOTS, SLOTS), 1) // 6
     alike = jnp.where(one == two, 1.0, 0.0)
@@ -223,8 +235,11 @@
 def body(queries, keys, values, selections, router, w_up, w_down):
     length, width = queries.shape
     parts = lax.axis_size("p")
-    seq = ("r", "c")
+    seq = ("r", "l", "y")
+    patch = ("l", "y")
     units = w_up.shape[1]
+    quarter = w_up.shape[2] // 4
+    place = lax.axis_index("y").astype(jnp.int32)
     columns = w_down.shape[1]
     group = w_down.shape[2] // parts
     sel = selections[0].T.reshape(-1)
@@ -246,9 +261,9 @@
     inner = call(inner_kernel, shape((length, width), F32), queries, keys, values, name="inner")
     up_cut = call(
         cut_up_kernel,
-        shape((8, units, width)),
+        shape((4, units, quarter)),
         w_up[0],
-        scratch=[pltpu.SemaphoreType.DMA((8,))],
+        scratch=[pltpu.SemaphoreType.DMA((4,))],
         spaces=([HBM], HBM),
         name="cut_up",
     )
@@ -273,23 +288,31 @@
         ],
         name="attn",
     )
-    whole_rows = lax.all_to_all(pay, "p", 0, 0, tiled=True)
-    near_rows = lax.all_to_all(whole_rows, "c", 0, 0, tiled=True)
+    whole_rows = lax.all_to_all(jnp.tile(pay, (4, 1, 1)), ("y", "p"), 0, 0, tiled=True)
+    near_rows = call(
+        near_kernel,
+        shape((240, LANES)),
+        place.reshape(1),
+        whole_rows,
+        scratch=[pltpu.VMEM((240, LANES), F32)],
+        spaces=([pltpu.SMEM, pltpu.VMEM], pltpu.VMEM),
+        name="near",
+    )
     near_rows, up_cut = lax.optimization_barrier((near_rows, up_cut))
-    up_mine = lax.all_to_all(up_cut, "c", 0, 0, tiled=True).reshape(8 * units, width)
-    arrived = lax.all_gather(near_rows, "r", axis=0, tiled=True)
+    up_mine = lax.all_to_all(up_cut, "y", 0, 0, tiled=True).reshape(4 * units, quarter)
+    arrived = lax.all_gather(near_rows, ("r", "l"), axis=0, tiled=True)
     partial = call(
         up_kernel,
-        shape((8 * units, 384)),
+        shape((4 * units, 384)),
         arrived,
         up_mine,
-        scratch=[pltpu.VMEM((64 * SLOTS, LANES), F32), pltpu.VMEM((384, width), BF16)],
+        scratch=[pltpu.VMEM((64 * 60, LANES), F32), pltpu.VMEM((384, quarter), BF16)],
         name="up",
     )
-    sums = lax.all_to_all(partial.reshape(8, units, 384), "c", 0, 0, tiled=True)
+    sums = lax.all_to_all(partial.reshape(4, units, 384), "y", 0, 0, tiled=True)
     act = call(act_kernel, shape((units, 384)), sums, name="act")
     act, down_cut = lax.optimization_barrier((act, down_cut))
-    down_mine = lax.all_to_all(down_cut, "c", 0, 0, tiled=True).reshape(8 * columns, group)
+    down_mine = lax.all_to_all(down_cut, patch, 0, 0, tiled=True).reshape(8 * columns, group)
     act = lax.all_gather(act, "r", axis=0, tiled=True)
     out = call(
         down_kernel,
@@ -301,7 +324,14 @@
     )
     back = lax.all_to_all(out, seq, 0, 0, tiled=True)
     weighted = call(
-        weigh_kernel, shape((8, SLOTS, LANES)), back, whole_rows, router_rows, name="weigh"
+        weigh_kernel,
+        shape((8, SLOTS, LANES)),
+        place.reshape(1),
+        back,
+        whole_rows,
+        router_rows,
+        spaces=([pltpu.SMEM] + [pltpu.VMEM] * 3, pltpu.VMEM),
+        name="weigh",
     )
     weighted = lax.all_to_all(weighted, "p", 0, 0, tiled=True)
     return call(
@@ -316,9 +346,8 @@
 
 
 def solution(mesh):
-    parts = mesh.devices.shape[1]
-    split = Mesh(mesh.devices.reshape(-1, parts, parts), ("r", "c", "p"))
-    seq = ("r", "c")
+    split = Mesh(mesh.devices.reshape(8, 2, 4, 8), ("r", "l", "y", "p"))
+    seq = ("r", "l", "y")
     placed = (
         P(seq, "p"),
         P(seq, "p"),

time: 259 us -> 238 us (0.919)
  blocking collectives: 112 us -> 73.4 us
  waiting for transfers between devices: 55.2 us -> 64.1 us
  starting transfers between devices: 71.3 us -> 78.9 us
    all_to_all x3 -> x1, blocking collectives: 36.9 us -> 10.4 us  [body(): sums = lax.all_to_all(partial.reshape(4, units, 384), 'y', 0, 0, tiled=True)]
    all_gather x1, blocking collectives: 38 us -> 26.6 us  [body(): arrived = lax.all_gather(near_rows, ('r', 'l'), axis=0, tiled=True)]
    all_to_all x2 -> x3, starting transfers between devices: 7.19 us -> 18.2 us  [the longest x1 11 us: body(): lax.all_to_all(jnp.tile(pay, (4, 1, 1)), ('y', 'p'), 0, 0, tiled=True)]
    all_to_all x2 -> x3, waiting for transfers between devices: 0.01 us -> 8.9 us  [the longest x1 8.9 us: body(): lax.all_to_all(jnp.tile(pay, (4, 1, 1)), ('y', 'p'), 0, 0, tiled=True)]
    all_to_all x1, starting transfers between devices: 27.1 us -> 24.3 us  [body(): weighted = lax.all_to_all(weighted, 'p', 0, 0, tiled=True)]
    pallas_call x11 -> x12, Pallas kernels: 13.2 us -> 13 us  [call(): pl.pallas_call(kernel, out_shape=out, scratch_shapes=list(scratch), compi...]
  transfers between devices with their start and end apart: 6 -> 7, of which waited for: 4 -> 5; matrix products, arithmetic and copies ran while one was open for 0% -> 0% of each run, Pallas kernels for 2% -> 2%
where the time goes in v6:
time: 238 us; the launch traced here: 237 us
  starting transfers between devices  78.9 us (33%)
  blocking collectives  73.4 us (31%)
  waiting for transfers between devices  64.1 us (27%)
  Pallas kernels  13 us (5%)
  local copies, waits for them, and re-layouts  7.55 us (3%)
    all_gather x1, blocking collectives, body(): act = lax.all_gather(act, 'r', axis=0, tiled=True)  36.4 us
    all_gather x1, blocking collectives, body(): arrived = lax.all_gather(near_rows, ('r', 'l'), axis=0, tiled=True)  26.6 us
    all_to_all x1, starting transfers between devices, body(): weighted = lax.all_to_all(weighted, 'p', 0, 0, tiled=True)  24.3 us
    all_to_all x1, waiting for transfers between devices, body(): back = lax.all_to_all(out, seq, 0, 0, tiled=True)  21.6 us
    all_to_all x1, starting transfers between devices, body(): chunks = lax.all_to_all(state, seq, 0, 0, tiled=True)  19.3 us
    all_to_all x1, waiting for transfers between devices, body(): before = lax.all_to_all(before, seq, 0, 0, tiled=True)  14.8 us
    all_to_all x1, waiting for transfers between devices, body(): chunks = lax.all_to_all(state, seq, 0, 0, tiled=True)  14 us
    pallas_call x12, Pallas kernels, call(): pl.pallas_call(kernel, out_shape=out, scratch_shapes=list(scratch), compi...  13 us
  transfers between devices with their start and end apart: 7, of which 5 were waited for; matrix products, arithmetic and copies ran while one was open for 0% of the time, Pallas kernels for 2%

profile of v6, /device:TPU:1, one launch (start us, length us, event | category | flops | bytes accessed | tf_op | source)
XLA Modules:
  0.0 237.2 jit_solution(15509777132947935860)
XLA Ops:
  0.0 0.0 copy-start
  0.0 0.0 copy-start.2
  0.0 1.1 copy-done.2
  1.1 0.0 copy-start.4
  1.1 1.0 copy-done.4
  2.1 1.3 state.1
  3.4 19.3 %all-to-all-start = ((bf16[64,16,128]{2,1,0:T(8,128)(2,1)}), bf16[64,16,128]{2,1,0:T(8,128)(2,1)S(1)}, u32[]{:S(2)}, u32[]{:S(2)}) async-start(bf16[64,16,128]{2,1,0:T(8,128)(2,1)} %state.1), calls=%async_computation | async-start | bytes 524288 | tf_op jit(solution)/shard_map/all_to_all | solution.py:260
  22.7 0.0 copy-start.3
  22.7 1.0 copy-done.3
  23.7 1.0 copy-done.5
  24.7 0.0 copy-start.6
  24.7 1.0 copy-done.6
  25.7 0.9 inner.1.inner_ref
  26.6 0.0 copy-done
  26.6 0.0 copy-start.9
  26.6 1.3 cut_up.1
  27.9 14.0 %all-to-all-done.in_ref = bf16[64,16,128]{2,1,0:T(8,128)(2,1)S(1)} async-done(((bf16[64,16,128]{2,1,0:T(8,128)(2,1)}), bf16[64,16,128]{2,1,0:T(8,128)(2,1)S(1)}, u32[]{:S(2)}, u32[]{:S(2)}) %all-to-all-start) | async-done | bytes 262176 | tf_op jit(solution)/shard_map/all_to_all | solution.py:260
  41.9 0.8 prefix.1
  42.7 7.4 %all-to-all-start.1 = ((bf16[64,16,128]{2,1,0:T(8,128)(2,1)}), bf16[64,16,128]{2,1,0:T(8,128)(2,1)S(1)}, u32[]{:S(2)}, u32[]{:S(2)}) async-start(bf16[64,16,128]{2,1,0:T(8,128)(2,1)} %prefix.1), calls=%async_computation.1 | async-start | bytes 524288 | tf_op jit(solution)/shard_map/all_to_all | solution.py:273
  50.0 0.0 copy-done.9
  50.0 0.1 broadcast_in_dim_reshape.4.sel_ref
  50.1 1.5 copy-done.1
  51.6 2.0 cut_down.1
  53.6 14.8 %all-to-all-done.1.p_ref = bf16[64,16,128]{2,1,0:T(8,128)(2,1)S(1)} async-done(((bf16[64,16,128]{2,1,0:T(8,128)(2,1)}), bf16[64,16,128]{2,1,0:T(8,128)(2,1)S(1)}, u32[]{:S(2)}, u32[]{:S(2)}) %all-to-all-start.1) | async-done | bytes 262176 | tf_op jit(solution)/shard_map/all_to_all | solution.py:273
  68.4 0.0 copy-done.7
  68.4 1.1 attn.1
  69.5 0.7 tile.19
  70.2 11.0 %all-to-all-start.2 = ((bf16[32,32,128]{2,1,0:T(8,128)(2,1)}), bf16[32,32,128]{2,1,0:T(8,128)(2,1)S(1)}, u32[]{:S(2)}, u32[]{:S(2)}) async-start(bf16[32,32,128]{2,1,0:T(8,128)(2,1)} %bitcast.6), calls=%async_computation.2 | async-start | bytes 524288 | tf_op jit(solution)/shard_map/all_to_all | solution.py:291
  81.2 8.9 %all-to-all-done.2.row_ref = bf16[32,32,128]{2,1,0:T(8,128)(2,1)S(1)} async-done(((bf16[32,32,128]{2,1,0:T(8,128)(2,1)}), bf16[32,32,128]{2,1,0:T(8,128)(2,1)S(1)}, u32[]{:S(2)}, u32[]{:S(2)}) %all-to-all-start.2) | async-done | bytes 262176 | tf_op jit(solution)/shard_map/all_to_all | solution.py:291
  90.1 3.6 %all-to-all-start.3 = ((bf16[4,144,1536]{2,1,0:T(8,128)(2,1)}), bf16[4,144,1536]{2,1,0:T(8,128)(2,1)S(1)}, u32[]{:S(2)}, u32[]{:S(2)}) async-start(bf16[4,144,1536]{2,1,0:T(8,128)(2,1)} %cut_up.1), calls=%async_computation.3 | async-start | bytes 3538944 | tf_op jit(solution)/shard_map/all_to_all | solution.py:302
  93.7 26.6 %all_gather.6.x_ref = bf16[3840,128]{1,0:T(8,128)(2,1)S(1)} all-gather(bf16[240,128]{1,0:T(8,128)(2,1)S(1)} %near.1), channel_id=1, replica_groups=mesh['r'=8,'l'=2,'y'=4,'p'=8] {'r','l'}, dimensions={0}, use_global_device_ids=true | all-gather | bytes 1044480 | tf_op jit(solution)/shard_map/all_gather | solution.py:303
  120.4 0.0 all-to-all-done.3
  120.4 1.3 up.1
  121.7 10.4 %all_to_all.40.in_ref = bf16[4,144,384]{2,1,0:T(8,128)(2,1)S(1)} all-to-all(bf16[4,144,384]{2,1,0:T(8,128)(2,1)S(1)} %bitcast.19), channel_id=1, replica_groups=mesh['r'=8,'l'=2,'y'=4,'p'=8] {'y'}, dimensions={0} | all-to-all | bytes 884736 | tf_op jit(solution)/shard_map/all_to_all | solution.py:312
  132.1 0.1 act.1
  132.2 3.6 %all-to-all-start.5 = ((bf16[8,96,1152]{2,1,0:T(8,128)(2,1)}), bf16[8,96,1152]{2,1,0:T(8,128)(2,1)S(1)}, u32[]{:S(2)}, u32[]{:S(2)}) async-start(bf16[8,96,1152]{2,1,0:T(8,128)(2,1)} %cut_down.1), calls=%async_computation.5 | async-start | bytes 3538944 | tf_op jit(solution)/shard_map/all_to_all | solution.py:315
  135.8 36.4 %all_gather.7.h_ref = bf16[1152,384]{1,0:T(8,128)(2,1)S(1)} all-gather(bf16[144,384]{1,0:T(8,128)(2,1)S(1)} %act.1), channel_id=1, replica_groups=mesh['r'=8,'l'=2,'y'=4,'p'=8] {'r'}, dimensions={0}, use_global_device_ids=true | all-gather | bytes 995328 | tf_op jit(solution)/shard_map/all_gather | solution.py:316
  172.2 0.0 all-to-all-done.5
  172.2 2.3 down.1
  174.5 9.8 %all-to-all-start.6 = ((bf16[64,32,128]{2,1,0:T(8,128)(2,1)}), bf16[64,32,128]{2,1,0:T(8,128)(2,1)S(1)}, u32[]{:S(2)}, u32[]{:S(2)}) async-start(bf16[64,32,128]{2,1,0:T(8,128)(2,1)} %down.1), calls=%async_computation.6 | async-start | bytes 1048576 | tf_op jit(solution)/shard_map/all_to_all | solution.py:325
  184.3 0.1 reshape.28
  184.4 0.0 copy-done.8
  184.4 0.1 reduce
  184.5 21.6 %all-to-all-done.6.y_ref = bf16[64,32,128]{2,1,0:T(8,128)(2,1)S(1)} async-done(((bf16[64,32,128]{2,1,0:T(8,128)(2,1)}), bf16[64,32,128]{2,1,0:T(8,128)(2,1)S(1)}, u32[]{:S(2)}, u32[]{:S(2)}) %all-to-all-start.6) | async-done | bytes 524320 | tf_op jit(solution)/shard_map/all_to_all | solution.py:325
  206.2 0.9 weigh.1
  207.0 24.3 %all-to-all-start.7 = ((bf16[8,32,128]{2,1,0:T(8,128)(2,1)}), bf16[8,32,128]{2,1,0:T(8,128)(2,1)S(1)}, u32[]{:S(2)}, u32[]{:S(2)}) async-start(bf16[8,32,128]{2,1,0:T(8,128)(2,1)} %weigh.1), calls=%async_computation.7 | async-start | bytes 131072 | tf_op jit(solution)/shard_map/all_to_all | solution.py:336
  231.4 4.8 %all-to-all-done.7.y_ref = bf16[8,32,128]{2,1,0:T(8,128)(2,1)S(1)} async-done(((bf16[8,32,128]{2,1,0:T(8,128)(2,1)}), bf16[8,32,128]{2,1,0:T(8,128)(2,1)S(1)}, u32[]{:S(2)}, u32[]{:S(2)}) %all-to-all-start.7) | async-done | bytes 65568 | tf_op jit(solution)/shard_map/all_to_all | solution.py:336
  236.2 1.0 add.6
  (12 shorter events, 0.1 us)
Async XLA Ops:
  0.0 26.6 %copy-start = (bf16[1,144,6144]{2,1,0:T(8,128)(2,1)S(1)}, bf16[1,144,6144]{2,1,0:T(8,128)(2,1)}, u32[]{:S(2)}) copy-start(bf16[1,144,6144]{2,1,0:T(8,128)(2,1)} %param.12) | copy-start | bytes 5308420
  0.0 1.1 copy-start.2
  1.1 1.0 copy-start.4
  3.4 38.5 %all-to-all-start = ((bf16[64,16,128]{2,1,0:T(8,128)(2,1)}), bf16[64,16,128]{2,1,0:T(8,128)(2,1)S(1)}, u32[]{:S(2)}, u32[]{:S(2)}) async-start(bf16[64,16,128]{2,1,0:T(8,128)(2,1)} %state.1), calls=%async_computation | async-start | bytes 524288 | tf_op jit(solution)/shard_map/all_to_all | solution.py:260
  22.7 1.0 copy-start.3
  23.7 1.0 copy-start.5
  24.7 1.0 copy-start.6
  26.6 23.4 %copy-start.9 = (s32[1,8,5]{1,0,2:T(1,128)S(1)}, s32[1,8,5]{1,0,2:T(1,128)}, u32[]{:S(2)}) copy-start(s32[1,8,5]{1,0,2:T(1,128)} %param.10) | copy-start | bytes 484
  42.7 25.7 %all-to-all-start.1 = ((bf16[64,16,128]{2,1,0:T(8,128)(2,1)}), bf16[64,16,128]{2,1,0:T(8,128)(2,1)S(1)}, u32[]{:S(2)}, u32[]{:S(2)}) async-start(bf16[64,16,128]{2,1,0:T(8,128)(2,1)} %prefix.1), calls=%async_computation.1 | async-start | bytes 524288 | tf_op jit(solution)/shard_map/all_to_all | solution.py:273
  50.1 1.5 copy-start.1
  51.6 16.8 %copy-start.7 = (bf16[256,768]{1,0:T(8,128)(2,1)S(1)}, bf16[256,768]{1,0:T(8,128)(2,1)}, u32[]{:S(2)}) copy-start(bf16[256,768]{1,0:T(8,128)(2,1)} %q_ref.3) | copy-start | bytes 1179652
  70.2 19.9 %all-to-all-start.2 = ((bf16[32,32,128]{2,1,0:T(8,128)(2,1)}), bf16[32,32,128]{2,1,0:T(8,128)(2,1)S(1)}, u32[]{:S(2)}, u32[]{:S(2)}) async-start(bf16[32,32,128]{2,1,0:T(8,128)(2,1)} %bitcast.6), calls=%async_computation.2 | async-start | bytes 524288 | tf_op jit(solution)/shard_map/all_to_all | solution.py:291
  90.1 30.2 %all-to-all-start.3 = ((bf16[4,144,1536]{2,1,0:T(8,128)(2,1)}), bf16[4,144,1536]{2,1,0:T(8,128)(2,1)S(1)}, u32[]{:S(2)}, u32[]{:S(2)}) async-start(bf16[4,144,1536]{2,1,0:T(8,128)(2,1)} %cut_up.1), calls=%async_computation.3 | async-start | bytes 3538944 | tf_op jit(solution)/shard_map/all_to_all | solution.py:302
  132.2 40.0 %all-to-all-start.5 = ((bf16[8,96,1152]{2,1,0:T(8,128)(2,1)}), bf16[8,96,1152]{2,1,0:T(8,128)(2,1)S(1)}, u32[]{:S(2)}, u32[]{:S(2)}) async-start(bf16[8,96,1152]{2,1,0:T(8,128)(2,1)} %cut_down.1), calls=%async_computation.5 | async-start | bytes 3538944 | tf_op jit(solution)/shard_map/all_to_all | solution.py:315
  172.2 12.2 %copy-start.8 = (bf16[6144,1]{0,1:T(2,128)(2,1)S(1)}, bf16[6144,1]{0,1:T(2,128)(2,1)}, u32[]{:S(2)}) copy-start(bf16[6144,1]{0,1:T(2,128)(2,1)} %param.11) | copy-start | bytes 36868
  174.5 31.6 %all-to-all-start.6 = ((bf16[64,32,128]{2,1,0:T(8,128)(2,1)}), bf16[64,32,128]{2,1,0:T(8,128)(2,1)S(1)}, u32[]{:S(2)}, u32[]{:S(2)}) async-start(bf16[64,32,128]{2,1,0:T(8,128)(2,1)} %down.1), calls=%async_computation.6 | async-start | bytes 1048576 | tf_op jit(solution)/shard_map/all_to_all | solution.py:325
  207.0 29.2 %all-to-all-start.7 = ((bf16[8,32,128]{2,1,0:T(8,128)(2,1)}), bf16[8,32,128]{2,1,0:T(8,128)(2,1)S(1)}, u32[]{:S(2)}, u32[]{:S(2)}) async-start(bf16[8,32,128]{2,1,0:T(8,128)(2,1)} %weigh.1), calls=%async_computation.7 | async-start | bytes 131072 | tf_op jit(solution)/shard_map/all_to_all | solution.py:336

commit v7 on v6

--- a/solution.py
+++ b/solution.py
@@ -142,12 +142,36 @@
         copy.wait()
 
 
-def cut_down_kernel(w_ref, out_ref):
+def cut_down_kernel(place_ref, w_ref, keep_ref, one_ref, two_ref, cut, sems):
     run = w_ref.shape[1] // 64
     for part in range(8):
         for group in range(8):
             low = (group * 8 + part) * run
-            out_ref[part, :, group * run : (group + 1) * run] = w_ref[:, low : low + run]
+            cut[part, :, group * run : (group + 1) * run] = w_ref[:, low : low + run]
+    own = place_ref[0] * 4
+    other = 4 - own
+    copies = []
+    for n in range(4):
+        away = (one_ref, two_ref)[n // 2].at[n % 2]
+        copies.append(pltpu.make_async_copy(cut.at[own + n], keep_ref.at[n], sems.at[n]))
+        copies.append(pltpu.make_async_copy(cut.at[other + n], away, sems.at[4 + n]))
+    for copy in copies:
+        copy.start()
+    for copy in copies:
+        copy.wait()
+
+
+def join_kernel(place_ref, keep_ref, one_ref, two_ref, out_ref, sems):
+    own = place_ref[0]
+    copies = []
+    for n in range(4):
+        away = (one_ref, two_ref)[n // 2].at[n % 2]
+        copies.append(pltpu.make_async_copy(keep_ref.at[n], out_ref.at[n, own], sems.at[n]))
+        copies.append(pltpu.make_async_copy(away, out_ref.at[n, 1 - own], sems.at[4 + n]))
+    for copy in copies:
+        copy.start()
+    for copy in copies:
+        copy.wait()
 
 
 def near_kernel(place_ref, row_ref, out_ref, rows):
@@ -180,18 +204,32 @@
     out_ref[...] = (up / (1.0 + jnp.exp(-up))).astype(BF16)
 
 
-def down_kernel(h_ref, w_ref, out_ref, rows):
+def down_kernel(h_ref, w_ref, out_ref, rows, whole):
+    columns = w_ref.shape[2]
+    for y in range(4):
+        for pair in range(2):
+            low = (pair * 4 + y) * columns
+            whole[low : low + columns] = w_ref[y, pair]
     for slot in (30, 31):
         rows[pl.ds(slot, 64, stride=SLOTS), :] = jnp.zeros((64, LANES), F32)
-    y = lax.dot_general(
-        h_ref[...], w_ref[...], (((0,), (1,)), ((), ())), preferred_element_type=F32
+    out = lax.dot_general(
+        h_ref[...], whole[...], (((0,), (1,)), ((), ())), preferred_element_type=F32
     )
     for i in range(5):
         for tile in range(6):
-            rows[pl.ds(i * 6 + tile, 64, stride=SLOTS), :] = y[
+            rows[pl.ds(i * 6 + tile, 64, stride=SLOTS), :] = out[
                 i * 64 : i * 64 + 64, tile * LANES : (tile + 1) * LANES
             ]
-    out_ref[...] = rows[...].reshape(64, SLOTS, LANES).astype(BF16)
+    for block in range(64):
+        z, y = divmod(block, 4)
+        out_ref[y * 16 + z] = rows[block * SLOTS : (block + 1) * SLOTS].astype(BF16)
+
+
+def sum_kernel(in_ref, out_ref):
+    total = in_ref[0:16].astype(F32)
+    for part in range(1, 4):
+        total = total + in_ref[part * 16 : part * 16 + 16].astype(F32)
+    out_ref[...] = total.astype(BF16)
 
 
 def weigh_kernel(place_ref, y_ref, row_ref, router_ref, out_ref):
@@ -207,9 +245,7 @@
     )
     gate = jax.nn.sigmoid(jnp.sum(sums, axis=-1, keepdims=True))
     for group in range(8):
-        total = y_ref[group * 8].astype(F32)
-        for part in range(1, 8):
-            total = total + y_ref[group * 8 + part].astype(F32)
+        total = y_ref[group * 2].astype(F32) + y_ref[group * 2 + 1].astype(F32)
         out_ref[group] = (total * gate).astype(BF16)
 
 
@@ -236,7 +272,6 @@
     length, width = queries.shape
     parts = lax.axis_size("p")
     seq = ("r", "l", "y")
-    patch = ("l", "y")
     units = w_up.shape[1]
     quarter = w_up.shape[2] // 4
     place = lax.axis_index("y").astype(jnp.int32)
@@ -267,12 +302,22 @@
         spaces=([HBM], HBM),
         name="cut_up",
     )
-    chunks, inner, up_cut = lax.optimization_barrier((chunks, inner, up_cut))
+    pair = lax.axis_index("l").astype(jnp.int32).reshape(1)
+    down_keep, down_one, down_two = call(
+        cut_down_kernel,
+        [shape((n, columns, group)) for n in (4, 2, 2)],
+        pair,
+        w_down[0],
+        scratch=[pltpu.VMEM((8, columns, group), BF16), pltpu.SemaphoreType.DMA((8,))],
+        spaces=([pltpu.SMEM, pltpu.VMEM], [HBM] * 3),
+        name="cut_down",
+    )
+    down_one = lax.ppermute(down_one, "l", [(0, 1), (1, 0)])
+    chunks, inner, up_cut, down_keep, down_one, down_two = lax.optimization_barrier(
+        (chunks, inner, up_cut, down_keep, down_one, down_two)
+    )
     before = call(prefix_kernel, shape((64, 16, LANES)), chunks, name="prefix")
-    before, w_down = lax.optimization_barrier((before, w_down))
     before = lax.all_to_all(before, seq, 0, 0, tiled=True)
-    down_cut = call(cut_down_kernel, shape((8, columns, group)), w_down[0], name="cut_down")
-    before, down_cut = lax.optimization_barrier((before, down_cut))
     attn, pay = call(
         attn_kernel,
         (shape((length, width)), shape((8, SLOTS, LANES))),
@@ -288,7 +333,10 @@
         ],
         name="attn",
     )
+    pay, down_two = lax.optimization_barrier((pay, down_two))
+    down_two = lax.ppermute(down_two, "l", [(0, 1), (1, 0)])
     whole_rows = lax.all_to_all(jnp.tile(pay, (4, 1, 1)), ("y", "p"), 0, 0, tiled=True)
+    whole_rows, down_two = lax.optimization_barrier((whole_rows, down_two))
     near_rows = call(
         near_kernel,
         shape((240, LANES)),
@@ -309,20 +357,38 @@
         scratch=[pltpu.VMEM((64 * 60, LANES), F32), pltpu.VMEM((384, quarter), BF16)],
         name="up",
     )
+    partial, down_keep = lax.optimization_barrier((partial, down_keep))
     sums = lax.all_to_all(partial.reshape(4, units, 384), "y", 0, 0, tiled=True)
+    down_cut = call(
+        join_kernel,
+        shape((4, 2, columns, group)),
+        pair,
+        down_keep,
+        down_one,
+        down_two,
+        scratch=[pltpu.SemaphoreType.DMA((8,))],
+        spaces=([pltpu.SMEM] + [HBM] * 3, HBM),
+        name="join",
+    )
+    sums, down_cut = lax.optimization_barrier((sums, down_cut))
     act = call(act_kernel, shape((units, 384)), sums, name="act")
     act, down_cut = lax.optimization_barrier((act, down_cut))
-    down_mine = lax.all_to_all(down_cut, patch, 0, 0, tiled=True).reshape(8 * columns, group)
+    down_mine = lax.all_to_all(down_cut, "y", 0, 0, tiled=True)
     act = lax.all_gather(act, "r", axis=0, tiled=True)
     out = call(
         down_kernel,
         shape((64, SLOTS, LANES)),
         act,
         down_mine,
-        scratch=[pltpu.VMEM((64 * SLOTS, LANES), F32)],
+        scratch=[
+            pltpu.VMEM((64 * SLOTS, LANES), F32),
+            pltpu.VMEM((8 * columns, group), BF16),
+        ],
         name="down",
     )
-    back = lax.all_to_all(out, seq, 0, 0, tiled=True)
+    back = lax.all_to_all(out, "y", 0, 0, tiled=True)
+    back = call(sum_kernel, shape((16, SLOTS, LANES)), back, name="sum")
+    back = lax.all_to_all(back, ("r", "l"), 0, 0, tiled=True)
     weighted = call(
         weigh_kernel,
         shape((8, SLOTS, LANES)),

time: 238 us -> 235 us (0.987)
  blocking collectives: 73.4 us -> 64.2 us
  starting transfers between devices: 78.9 us -> 85.9 us
  waiting for transfers between devices: 64.1 us -> 59.7 us
  Pallas kernels: 13 us -> 16.1 us
    all_to_all x1, waiting for transfers between devices: 14 us -> 0.01 us  [body(): chunks = lax.all_to_all(state, seq, 0, 0, tiled=True)]
    ppermute x0 -> x2, waiting for transfers between devices: none -> 12.2 us  [the longest x1 12.2 us: body(): down_one = lax.ppermute(down_one, 'l', [(0, 1), (1, 0)])]
    all_gather x1, blocking collectives: 36.4 us -> 25 us  [body(): act = lax.all_gather(act, 'r', axis=0, tiled=True)]
    all_to_all x2 -> x3, waiting for transfers between devices: 21.6 us -> 14.8 us  [the longest x1 11.7 us: body(): back = lax.all_to_all(back, ('r', 'l'), 0, 0, tiled=True)]
    all_to_all x1, starting transfers between devices: 7.35 us -> 14 us  [body(): before = lax.all_to_all(before, seq, 0, 0, tiled=True)]
    ppermute x0 -> x2, starting transfers between devices: none -> 5.85 us  [the longest x1 2.93 us: body(): down_two = lax.ppermute(down_two, 'l', [(0, 1), (1, 0)])]
    all_to_all x1, starting transfers between devices: 24.3 us -> 19 us  [body(): weighted = lax.all_to_all(weighted, 'p', 0, 0, tiled=True)]
    all_to_all x1, waiting for transfers between devices: 14.8 us -> 18.9 us  [body(): before = lax.all_to_all(before, seq, 0, 0, tiled=True)]
  transfers between devices with their start and end apart: 7 -> 10, of which waited for: 5 -> 6; matrix products, arithmetic and copies ran while one was open for 0% -> 0% of each run, Pallas kernels for 2% -> 3%
where the time goes in v7:
time: 235 us; the launch traced here: 234 us
  starting transfers between devices  85.9 us (37%)
  blocking collectives  64.2 us (27%)
  waiting for transfers between devices  59.7 us (25%)
  Pallas kernels  16.1 us (7%)
  local copies, waits for them, and re-layouts  8.14 us (3%)
    all_gather x1, blocking collectives, body(): arrived = lax.all_gather(near_rows, ('r', 'l'), axis=0, tiled=True)  27.4 us
    all_gather x1, blocking collectives, body(): act = lax.all_gather(act, 'r', axis=0, tiled=True)  25 us
    all_to_all x1, starting transfers between devices, body(): chunks = lax.all_to_all(state, seq, 0, 0, tiled=True)  19.3 us
    all_to_all x1, starting transfers between devices, body(): weighted = lax.all_to_all(weighted, 'p', 0, 0, tiled=True)  19 us
    all_to_all x1, waiting for transfers between devices, body(): before = lax.all_to_all(before, seq, 0, 0, tiled=True)  18.9 us
    pallas_call x14, Pallas kernels, call(): pl.pallas_call(kernel, out_shape=out, scratch_shapes=list(scratch), compi...  16.1 us
    all_to_all x1, starting transfers between devices, body(): before = lax.all_to_all(before, seq, 0, 0, tiled=True)  14 us
    ppermute x1, waiting for transfers between devices, body(): down_one = lax.ppermute(down_one, 'l', [(0, 1), (1, 0)])  12.2 us
  transfers between devices with their start and end apart: 10, of which 6 were waited for; matrix products, arithmetic and copies ran while one was open for 0% of the time, Pallas kernels for 3%

profile of v7, /device:TPU:1, one launch (start us, length us, event | category | flops | bytes accessed | tf_op | source)
XLA Modules:
  0.0 234.4 jit_solution(13104272756249934355)
XLA Ops:
  0.0 1.0 copy-done.2
  1.0 1.0 copy-done.4
  2.0 1.3 state.1
  3.3 19.3 %all-to-all-start = ((bf16[64,16,128]{2,1,0:T(8,128)(2,1)}), bf16[64,16,128]{2,1,0:T(8,128)(2,1)S(1)}, u32[]{:S(2)}, u32[]{:S(2)}) async-start(bf16[64,16,128]{2,1,0:T(8,128)(2,1)} %state.1), calls=%async_computation | async-start | bytes 524288 | tf_op jit(solution)/shard_map/all_to_all | solution.py:295
  22.6 0.0 copy-start.1
  22.6 1.5 copy-done.1
  24.0 3.1 %cut_down.1 = (bf16[4,96,1152]{2,1,0:T(8,128)(2,1)S(1)}, bf16[2,96,1152]{2,1,0:T(8,128)(2,1)S(1)}, bf16[2,96,1152]{2,1,0:T(8,128)(2,1)S(1)}) custom-call(s32[1]{0:T(128)} %bitcast.1.place_ref, bf16[96,9216]{1,0:T(8,128)(2,1)S(1)} %bitcast.17), custom_call_target="tpu_custom_call" | custom-call | tf_op jit(solution)/shard_map/cut_down/pallas_call | solution.py:29
  27.2 2.9 %collective-permute-start = (bf16[2,96,1152]{2,1,0:T(8,128)(2,1)S(1)}, bf16[2,96,1152]{2,1,0:T(8,128)(2,1)S(1)}, u32[]{:S(2)}, u32[]{:S(2)}) collective-permute-start(bf16[2,96,1152]{2,1,0:T(8,128)(2,1)S(1)} %get-tuple-element.35), channel_id=1, source_target_pairs={{0,32},{32,0},{1,33},{33,1},{2,34},{34,2},{3,35},{35,3},{4,36},{36... | collective-permute-start | bytes 1327112 | tf_op jit(solution)/shard_map/ppermute | solution.py:315
  30.1 0.9 inner.1.inner_ref
  31.1 0.0 copy-start.14
  31.1 1.2 cut_up.1
  32.4 12.2 %collective-permute-done.one_ref = bf16[2,96,1152]{2,1,0:T(8,128)(2,1)S(1)} collective-permute-done((bf16[2,96,1152]{2,1,0:T(8,128)(2,1)S(1)}, bf16[2,96,1152]{2,1,0:T(8,128)(2,1)S(1)}, u32[]{:S(2)}, u32[]{:S(2)}) %collective-permute-start) | collective-permute-done | bytes 442400 | tf_op jit(solution)/shard_map/ppermute | solution.py:315
  44.6 0.8 prefix.1
  45.4 14.0 %all-to-all-start.1 = ((bf16[64,16,128]{2,1,0:T(8,128)(2,1)}), bf16[64,16,128]{2,1,0:T(8,128)(2,1)S(1)}, u32[]{:S(2)}, u32[]{:S(2)}) async-start(bf16[64,16,128]{2,1,0:T(8,128)(2,1)} %prefix.1), calls=%async_computation.1 | async-start | bytes 524288 | tf_op jit(solution)/shard_map/all_to_all | solution.py:320
  59.4 0.1 broadcast_in_dim_reshape.4.sel_ref
  59.5 18.9 %all-to-all-done.1.p_ref = bf16[64,16,128]{2,1,0:T(8,128)(2,1)S(1)} async-done(((bf16[64,16,128]{2,1,0:T(8,128)(2,1)}), bf16[64,16,128]{2,1,0:T(8,128)(2,1)S(1)}, u32[]{:S(2)}, u32[]{:S(2)}) %all-to-all-start.1) | async-done | bytes 262176 | tf_op jit(solution)/shard_map/all_to_all | solution.py:320
  78.4 1.1 attn.1
  79.5 0.0 copy-start.11
  79.5 0.7 copy-done.11
  80.2 2.9 %collective-permute-start.1 = (bf16[2,96,1152]{2,1,0:T(8,128)(2,1)S(1)}, bf16[2,96,1152]{2,1,0:T(8,128)(2,1)S(1)}, u32[]{:S(2)}, u32[]{:S(2)}) collective-permute-start(bf16[2,96,1152]{2,1,0:T(8,128)(2,1)S(1)} %get-tuple-element.43), channel_id=1, source_target_pairs={{0,32},{32,0},{1,33},{33,1},{2,34},{34,2},{3,35},{35,3},{4,36},{36... | collective-permute-start | bytes 1327112 | tf_op jit(solution)/shard_map/ppermute | solution.py:337
  83.2 0.7 tile.19
  83.9 10.1 %all-to-all-start.2 = ((bf16[32,32,128]{2,1,0:T(8,128)(2,1)}), bf16[32,32,128]{2,1,0:T(8,128)(2,1)S(1)}, u32[]{:S(2)}, u32[]{:S(2)}) async-start(bf16[32,32,128]{2,1,0:T(8,128)(2,1)} %bitcast.7), calls=%async_computation.2 | async-start | bytes 524288 | tf_op jit(solution)/shard_map/all_to_all | solution.py:338
  94.1 8.9 %all-to-all-done.2.row_ref = bf16[32,32,128]{2,1,0:T(8,128)(2,1)S(1)} async-done(((bf16[32,32,128]{2,1,0:T(8,128)(2,1)}), bf16[32,32,128]{2,1,0:T(8,128)(2,1)S(1)}, u32[]{:S(2)}, u32[]{:S(2)}) %all-to-all-start.2) | async-done | bytes 262176 | tf_op jit(solution)/shard_map/all_to_all | solution.py:338
  103.0 0.8 copy-done.9
  103.8 3.6 %all-to-all-start.3 = ((bf16[4,144,1536]{2,1,0:T(8,128)(2,1)}), bf16[4,144,1536]{2,1,0:T(8,128)(2,1)S(1)}, u32[]{:S(2)}, u32[]{:S(2)}) async-start(bf16[4,144,1536]{2,1,0:T(8,128)(2,1)} %cut_up.1), calls=%async_computation.3 | async-start | bytes 3538944 | tf_op jit(solution)/shard_map/all_to_all | solution.py:350
  107.4 27.4 %all_gather.6.x_ref = bf16[3840,128]{1,0:T(8,128)(2,1)S(1)} all-gather(bf16[240,128]{1,0:T(8,128)(2,1)S(1)} %near.1), channel_id=1, replica_groups=mesh['r'=8,'l'=2,'y'=4,'p'=8] {'r','l'}, dimensions={0}, use_global_device_ids=true | all-gather | bytes 1044480 | tf_op jit(solution)/shard_map/all_gather | solution.py:351
  134.8 2.1 up.1
  136.8 3.7 %all-to-all-start.4 = ((bf16[4,144,384]{2,1,0:T(8,128)(2,1)}), bf16[4,144,384]{2,1,0:T(8,128)(2,1)S(1)}, u32[]{:S(2)}, u32[]{:S(2)}) async-start(bf16[4,144,384]{2,1,0:T(8,128)(2,1)} %bitcast.9), calls=%async_computation.4 | async-start | bytes 884736 | tf_op jit(solution)/shard_map/all_to_all | solution.py:361
  140.6 1.2 copy-done.8
  141.8 1.0 copy-done.10
  142.8 1.3 join.1
  144.1 3.0 %all-to-all-done.4.in_ref = bf16[4,144,384]{2,1,0:T(8,128)(2,1)S(1)} async-done(((bf16[4,144,384]{2,1,0:T(8,128)(2,1)}), bf16[4,144,384]{2,1,0:T(8,128)(2,1)S(1)}, u32[]{:S(2)}, u32[]{:S(2)}) %all-to-all-start.4) | async-done | bytes 442400 | tf_op jit(solution)/shard_map/all_to_all | solution.py:361
  147.1 0.1 act.1
  147.2 3.6 %all-to-all-start.5 = ((bf16[4,2,96,1152]{3,2,1,0:T(8,128)(2,1)}), bf16[4,2,96,1152]{3,2,1,0:T(8,128)(2,1)S(1)}, u32[]{:S(2)}, u32[]{:S(2)}) async-start(bf16[4,2,96,1152]{3,2,1,0:T(8,128)(2,1)} %join.1), calls=%async_computation.5 | async-start | bytes 3538944 | tf_op jit(solution)/shard_map/all_to_all | solution.py:376
  150.8 25.0 %all_gather.7.h_ref = bf16[1152,384]{1,0:T(8,128)(2,1)S(1)} all-gather(bf16[144,384]{1,0:T(8,128)(2,1)S(1)} %act.1), channel_id=1, replica_groups=mesh['r'=8,'l'=2,'y'=4,'p'=8] {'r'}, dimensions={0}, use_global_device_ids=true | all-gather | bytes 995328 | tf_op jit(solution)/shard_map/all_gather | solution.py:377
  175.8 1.5 down.1
  177.3 0.0 copy-start.13
  177.3 0.0 copy-start.12
  177.4 11.9 %all_to_all.45.in_ref = bf16[64,32,128]{2,1,0:T(8,128)(2,1)S(1)} all-to-all(bf16[64,32,128]{2,1,0:T(8,128)(2,1)S(1)} %down.1), channel_id=1, replica_groups=mesh['r'=8,'l'=2,'y'=4,'p'=8] {'y'}, dimensions={0} | all-to-all | bytes 1048576 | tf_op jit(solution)/shard_map/all_to_all | solution.py:389
  189.2 0.7 sum.1
  189.9 6.8 %all-to-all-start.7 = ((bf16[16,32,128]{2,1,0:T(8,128)(2,1)}), bf16[16,32,128]{2,1,0:T(8,128)(2,1)S(1)}, u32[]{:S(2)}, u32[]{:S(2)}) async-start(bf16[16,32,128]{2,1,0:T(8,128)(2,1)} %sum.1), calls=%async_computation.7 | async-start | bytes 262144 | tf_op jit(solution)/shard_map/all_to_all | solution.py:391
  196.7 0.1 reshape.28
  196.8 0.1 reduce
  196.9 11.7 %all-to-all-done.7.y_ref = bf16[16,32,128]{2,1,0:T(8,128)(2,1)S(1)} async-done(((bf16[16,32,128]{2,1,0:T(8,128)(2,1)}), bf16[16,32,128]{2,1,0:T(8,128)(2,1)S(1)}, u32[]{:S(2)}, u32[]{:S(2)}) %all-to-all-start.7) | async-done | bytes 131104 | tf_op jit(solution)/shard_map/all_to_all | solution.py:391
  208.7 0.9 weigh.1
  209.5 19.0 %all-to-all-start.8 = ((bf16[8,32,128]{2,1,0:T(8,128)(2,1)}), bf16[8,32,128]{2,1,0:T(8,128)(2,1)S(1)}, u32[]{:S(2)}, u32[]{:S(2)}) async-start(bf16[8,32,128]{2,1,0:T(8,128)(2,1)} %weigh.1), calls=%async_computation.8 | async-start | bytes 131072 | tf_op jit(solution)/shard_map/all_to_all | solution.py:402
  228.5 4.8 %all-to-all-done.8.y_ref = bf16[8,32,128]{2,1,0:T(8,128)(2,1)S(1)} async-done(((bf16[8,32,128]{2,1,0:T(8,128)(2,1)}), bf16[8,32,128]{2,1,0:T(8,128)(2,1)S(1)}, u32[]{:S(2)}, u32[]{:S(2)}) %all-to-all-start.8) | async-done | bytes 65568 | tf_op jit(solution)/shard_map/all_to_all | solution.py:402
  233.4 1.0 add.6
  (30 shorter events, 0.1 us)
Async XLA Ops:
  0.0 1.0 copy-start.2
  1.0 1.0 copy-start.4
  2.0 28.1 %copy-start.3 = (bf16[256,768]{1,0:T(8,128)(2,1)S(1)}, bf16[256,768]{1,0:T(8,128)(2,1)}, u32[]{:S(2)}) copy-start(bf16[256,768]{1,0:T(8,128)(2,1)} %k_ref.3) | copy-start | bytes 1179652
  2.0 28.1 %copy-start.5 = (bf16[256,768]{1,0:T(8,128)(2,1)S(1)}, bf16[256,768]{1,0:T(8,128)(2,1)}, u32[]{:S(2)}) copy-start(bf16[256,768]{1,0:T(8,128)(2,1)} %v_ref.3) | copy-start | bytes 1179652
  2.0 28.1 %copy-start.6 = (bf16[256,768]{1,0:T(8,128)(2,1)S(1)}, bf16[256,768]{1,0:T(8,128)(2,1)}, u32[]{:S(2)}) copy-start(bf16[256,768]{1,0:T(8,128)(2,1)} %q_ref.3) | copy-start | bytes 1179652
  3.3 41.4 %all-to-all-start = ((bf16[64,16,128]{2,1,0:T(8,128)(2,1)}), bf16[64,16,128]{2,1,0:T(8,128)(2,1)S(1)}, u32[]{:S(2)}, u32[]{:S(2)}) async-start(bf16[64,16,128]{2,1,0:T(8,128)(2,1)} %state.1), calls=%async_computation | async-start | bytes 524288 | tf_op jit(solution)/shard_map/all_to_all | solution.py:295
  22.6 1.5 copy-start.1
  24.0 7.1 %copy-start = (bf16[1,144,6144]{2,1,0:T(8,128)(2,1)S(1)}, bf16[1,144,6144]{2,1,0:T(8,128)(2,1)}, u32[]{:S(2)}) copy-start(bf16[1,144,6144]{2,1,0:T(8,128)(2,1)} %param.12) | copy-start | bytes 5308420
  27.2 3.9 %copy-start.7 = (bf16[4,96,1152]{2,1,0:T(8,128)(2,1)}, bf16[4,96,1152]{2,1,0:T(8,128)(2,1)S(1)}, u32[]{:S(2)}) copy-start(bf16[4,96,1152]{2,1,0:T(8,128)(2,1)S(1)} %get-tuple-element.50.keep_ref) | copy-start | bytes 2654212
  27.2 17.4 %collective-permute-start = (bf16[2,96,1152]{2,1,0:T(8,128)(2,1)S(1)}, bf16[2,96,1152]{2,1,0:T(8,128)(2,1)S(1)}, u32[]{:S(2)}, u32[]{:S(2)}) collective-permute-start(bf16[2,96,1152]{2,1,0:T(8,128)(2,1)S(1)} %get-tuple-element.35), channel_id=1, source_target_pairs={{0,32},{32,0},{1,33},{33,1},{2,34},{34,2},{3,35},{35,3},{4,36},{36... | collective-permute-start | bytes 1327112 | tf_op jit(solution)/shard_map/ppermute | solution.py:315
  31.1 28.3 %copy-start.14 = (s32[1,8,5]{1,0,2:T(1,128)S(1)}, s32[1,8,5]{1,0,2:T(1,128)}, u32[]{:S(2)}) copy-start(s32[1,8,5]{1,0,2:T(1,128)} %param.10) | copy-start | bytes 484
  45.4 33.0 %all-to-all-start.1 = ((bf16[64,16,128]{2,1,0:T(8,128)(2,1)}), bf16[64,16,128]{2,1,0:T(8,128)(2,1)S(1)}, u32[]{:S(2)}, u32[]{:S(2)}) async-start(bf16[64,16,128]{2,1,0:T(8,128)(2,1)} %prefix.1), calls=%async_computation.1 | async-start | bytes 524288 | tf_op jit(solution)/shard_map/all_to_all | solution.py:320
  79.5 0.7 copy-start.11
  80.2 22.7 %collective-permute-start.1 = (bf16[2,96,1152]{2,1,0:T(8,128)(2,1)S(1)}, bf16[2,96,1152]{2,1,0:T(8,128)(2,1)S(1)}, u32[]{:S(2)}, u32[]{:S(2)}) collective-permute-start(bf16[2,96,1152]{2,1,0:T(8,128)(2,1)S(1)} %get-tuple-element.43), channel_id=1, source_target_pairs={{0,32},{32,0},{1,33},{33,1},{2,34},{34,2},{3,35},{35,3},{4,36},{36... | collective-permute-start | bytes 1327112 | tf_op jit(solution)/shard_map/ppermute | solution.py:337
  83.9 19.1 %all-to-all-start.2 = ((bf16[32,32,128]{2,1,0:T(8,128)(2,1)}), bf16[32,32,128]{2,1,0:T(8,128)(2,1)S(1)}, u32[]{:S(2)}, u32[]{:S(2)}) async-start(bf16[32,32,128]{2,1,0:T(8,128)(2,1)} %bitcast.7), calls=%async_computation.2 | async-start | bytes 524288 | tf_op jit(solution)/shard_map/all_to_all | solution.py:338
  103.0 0.8 copy-start.9
  103.8 31.0 %all-to-all-start.3 = ((bf16[4,144,1536]{2,1,0:T(8,128)(2,1)}), bf16[4,144,1536]{2,1,0:T(8,128)(2,1)S(1)}, u32[]{:S(2)}, u32[]{:S(2)}) async-start(bf16[4,144,1536]{2,1,0:T(8,128)(2,1)} %cut_up.1), calls=%async_computation.3 | async-start | bytes 3538944 | tf_op jit(solution)/shard_map/all_to_all | solution.py:350
  136.8 10.2 %all-to-all-start.4 = ((bf16[4,144,384]{2,1,0:T(8,128)(2,1)}), bf16[4,144,384]{2,1,0:T(8,128)(2,1)S(1)}, u32[]{:S(2)}, u32[]{:S(2)}) async-start(bf16[4,144,384]{2,1,0:T(8,128)(2,1)} %bitcast.9), calls=%async_computation.4 | async-start | bytes 884736 | tf_op jit(solution)/shard_map/all_to_all | solution.py:361
  140.6 1.2 copy-start.8
  141.8 1.0 copy-start.10
  147.2 28.6 %all-to-all-start.5 = ((bf16[4,2,96,1152]{3,2,1,0:T(8,128)(2,1)}), bf16[4,2,96,1152]{3,2,1,0:T(8,128)(2,1)S(1)}, u32[]{:S(2)}, u32[]{:S(2)}) async-start(bf16[4,2,96,1152]{3,2,1,0:T(8,128)(2,1)} %join.1), calls=%async_computation.5 | async-start | bytes 3538944 | tf_op jit(solution)/shard_map/all_to_all | solution.py:376
  177.3 19.5 %copy-start.13 = (bf16[6144,1]{0,1:T(2,128)(2,1)S(1)}, bf16[6144,1]{0,1:T(2,128)(2,1)}, u32[]{:S(2)}) copy-start(bf16[6144,1]{0,1:T(2,128)(2,1)} %param.11) | copy-start | bytes 36868
  177.3 56.0 %copy-start.12 = (bf16[256,768]{1,0:T(8,128)(2,1)S(1)}, bf16[256,768]{1,0:T(8,128)(2,1)}, u32[]{:S(2)}) copy-start(bf16[256,768]{1,0:T(8,128)(2,1)} %copy-done.11) | copy-start | bytes 1179652
  189.9 18.7 %all-to-all-start.7 = ((bf16[16,32,128]{2,1,0:T(8,128)(2,1)}), bf16[16,32,128]{2,1,0:T(8,128)(2,1)S(1)}, u32[]{:S(2)}, u32[]{:S(2)}) async-start(bf16[16,32,128]{2,1,0:T(8,128)(2,1)} %sum.1), calls=%async_computation.7 | async-start | bytes 262144 | tf_op jit(solution)/shard_map/all_to_all | solution.py:391
  209.5 23.8 %all-to-all-start.8 = ((bf16[8,32,128]{2,1,0:T(8,128)(2,1)}), bf16[8,32,128]{2,1,0:T(8,128)(2,1)S(1)}, u32[]{:S(2)}, u32[]{:S(2)}) async-start(bf16[8,32,128]{2,1,0:T(8,128)(2,1)} %weigh.1), calls=%async_computation.8 | async-start | bytes 131072 | tf_op jit(solution)/shard_map/all_to_all | solution.py:402

commit v8 on v7

--- a/solution.py
+++ b/solution.py
@@ -47,16 +47,10 @@
     return first * LANES, (last + 1) * LANES, head * HEAD - first * LANES
 
 
-def chunk_rows(tile, third):
-    upper, kind = divmod(tile, 3)
-    return upper * 32 * 16 + kind * 3 + third
-
-
 def state_kernel(k_ref, v_ref, out_ref, grand, rows):
     grand[...] = lax.dot_general(
         k_ref[...], v_ref[...], (((0,), (0,)), ((), ())), preferred_element_type=F32
     )
-    rows[...] = jnp.zeros_like(rows)
     lane = lax.broadcasted_iota(jnp.int32, (HEAD, LANES), 1)
     for tile in range(6):
         head, split = tile_heads(tile)
@@ -64,16 +58,35 @@
         one = grand[head * HEAD : (head + 1) * HEAD, at]
         two = grand[(head + 1) * HEAD : (head + 2) * HEAD, at]
         block = jnp.where(lane < split, one, two)
-        for third in range(3):
-            rows[pl.ds(chunk_rows(tile, third), 32, stride=16), :] = block[third * 32 : third * 32 + 32]
-    out_ref[...] = rows[...].reshape(64, 16, LANES).astype(BF16)
+        for quarter in range(4):
+            rows[quarter, tile * 24 : tile * 24 + 24] = block[quarter * 24 : quarter * 24 + 24]
+    out_ref[...] = rows[...].astype(BF16)
+
+
+def total_kernel(in_ref, out_ref, rows):
+    total = in_ref[0].astype(F32)
+    for y in range(1, 4):
+        total = total + in_ref[y].astype(F32)
+    rows[0:144] = total
+    rows[144:152] = jnp.zeros((8, LANES), F32)
+    for z in range(16):
+        out_ref[z] = rows[z * 9 : z * 9 + 16].astype(BF16)
 
 
 def prefix_kernel(in_ref, out_ref):
     total = jnp.zeros((16, LANES), F32)
-    for block in range(in_ref.shape[0]):
-        out_ref[block] = total.astype(BF16)
-        total = total + in_ref[block].astype(F32)
+    for z in range(16):
+        out_ref[z] = total.astype(BF16)
+        total = total + in_ref[z].astype(F32)
+
+
+def spread_kernel(base_ref, in_ref, out_ref, rows):
+    for z in range(16):
+        rows[z * 9 : z * 9 + 9] = base_ref[z].astype(F32)[0:9]
+    total = rows[...]
+    for y in range(4):
+        out_ref[y] = total.astype(BF16)
+        total = total + in_ref[y].astype(F32)
 
 
 def inner_kernel(q_ref, k_ref, v_ref, out_ref):
@@ -97,18 +110,21 @@
 
 def attn_kernel(q_ref, inner_ref, p_ref, sel_ref, attn_ref, pay_ref, rows, wide, normed, picks):
     length = q_ref.shape[0]
-    rows[...] = p_ref[...].astype(F32).reshape(64 * 16, LANES)
+    for quarter in range(4):
+        part = p_ref[quarter].astype(F32)
+        for tile in range(6):
+            low = tile * HEAD + quarter * 24
+            rows[low : low + 24] = part[tile * 24 : tile * 24 + 24]
     wide[...] = jnp.zeros_like(wide)
-    lane = lax.broadcasted_iota(jnp.int32, (32, LANES), 1)
+    lane = lax.broadcasted_iota(jnp.int32, (HEAD, LANES), 1)
     for tile in range(6):
         head, split = tile_heads(tile)
         at = slice(tile * LANES, (tile + 1) * LANES)
-        for third in range(3):
-            block = rows[pl.ds(chunk_rows(tile, third), 32, stride=16), :]
-            low = head * HEAD + third * 32
-            wide[low : low + 32, at] = jnp.where(lane < split, block, 0.0).astype(BF16)
-            low = low + HEAD
-            wide[low : low + 32, at] = jnp.where(lane < split, 0.0, block).astype(BF16)
+        block = rows[tile * HEAD : (tile + 1) * HEAD]
+        low = head * HEAD
+        wide[low : low + HEAD, at] = jnp.where(lane < split, block, 0.0).astype(BF16)
+        low = low + HEAD
+        wide[low : low + HEAD, at] = jnp.where(lane < split, 0.0, block).astype(BF16)
     normed[...] = inner_ref[...] + jnp.dot(q_ref[...], wide[...], preferred_element_type=F32)
     for head in range(8):
         start, stop, low = head_window(head)
@@ -285,14 +301,22 @@
 
     state = call(
         state_kernel,
-        shape((64, 16, LANES)),
+        shape((4, 144, LANES)),
         keys,
         values,
-        scratch=[pltpu.VMEM((width, width), F32), pltpu.VMEM((64 * 16, LANES), F32)],
+        scratch=[pltpu.VMEM((width, width), F32), pltpu.VMEM((4, 144, LANES), F32)],
         name="state",
     )
-    w_up, w_down, state = lax.optimization_barrier((w_up, w_down, state))
-    chunks = lax.all_to_all(state, seq, 0, 0, tiled=True)
+    quarters = lax.all_to_all(state, "y", 0, 0, tiled=True)
+    quarters, queries, w_up, w_down = lax.optimization_barrier((quarters, queries, w_up, w_down))
+    totals = call(
+        total_kernel,
+        shape((16, 16, LANES)),
+        quarters,
+        scratch=[pltpu.VMEM((152, LANES), F32)],
+        name="total",
+    )
+    totals = lax.all_to_all(totals, ("r", "l"), 0, 0, tiled=True)
     inner = call(inner_kernel, shape((length, width), F32), queries, keys, values, name="inner")
     up_cut = call(
         cut_up_kernel,
@@ -302,6 +326,9 @@
         spaces=([HBM], HBM),
         name="cut_up",
     )
+    totals, inner, up_cut, w_down = lax.optimization_barrier((totals, inner, up_cut, w_down))
+    bases = call(prefix_kernel, shape((16, 16, LANES)), totals, name="prefix")
+    bases = lax.all_to_all(bases, ("r", "l"), 0, 0, tiled=True)
     pair = lax.axis_index("l").astype(jnp.int32).reshape(1)
     down_keep, down_one, down_two = call(
         cut_down_kernel,
@@ -312,12 +339,21 @@
         spaces=([pltpu.SMEM, pltpu.VMEM], [HBM] * 3),
         name="cut_down",
     )
+    bases, down_keep, down_one, down_two = lax.optimization_barrier(
+        (bases, down_keep, down_one, down_two)
+    )
+    before = call(
+        spread_kernel,
+        shape((4, 144, LANES)),
+        bases,
+        quarters,
+        scratch=[pltpu.VMEM((144, LANES), F32)],
+        name="spread",
+    )
+    before, down_one = lax.optimization_barrier((before, down_one))
+    before = lax.all_to_all(before, "y", 0, 0, tiled=True)
     down_one = lax.ppermute(down_one, "l", [(0, 1), (1, 0)])
-    chunks, inner, up_cut, down_keep, down_one, down_two = lax.optimization_barrier(
-        (chunks, inner, up_cut, down_keep, down_one, down_two)
-    )
-    before = call(prefix_kernel, shape((64, 16, LANES)), chunks, name="prefix")
-    before = lax.all_to_all(before, seq, 0, 0, tiled=True)
+    before, down_one, down_two = lax.optimization_barrier((before, down_one, down_two))
     attn, pay = call(
         attn_kernel,
         (shape((length, width)), shape((8, SLOTS, LANES))),
@@ -326,7 +362,7 @@
         before,
         sel_column,
         scratch=[
-            pltpu.VMEM((64 * 16, LANES), F32),
+            pltpu.VMEM((6 * HEAD, LANES), F32),
             pltpu.VMEM((width, width), BF16),
             pltpu.VMEM((length, width), F32),
             pltpu.VMEM((8 * SLOTS, LANES), F32),

time: 235 us -> 227 us (0.966)
  waiting for transfers between devices: 59.7 us -> 45.7 us
  blocking collectives: 64.2 us -> 75.8 us
  starting transfers between devices: 85.9 us -> 74.8 us
  local copies, waits for them, and re-layouts: 8.14 us -> 12.2 us
    ppermute x1, waiting for transfers between devices: 12.2 us -> 0.01 us  [body(): down_one = lax.ppermute(down_one, 'l', [(0, 1), (1, 0)])]
    all_to_all x2 -> x3, starting transfers between devices: 33.3 us -> 23.3 us  [the longest x1 14.9 us: body(): totals = lax.all_to_all(totals, ('r', 'l'), 0, 0, tiled=True)]
    all_to_all x0 -> x1, blocking collectives: none -> 9.73 us  [body(): quarters = lax.all_to_all(state, 'y', 0, 0, tiled=True)]
    unnamed x30 -> x32, local copies, waits for them, and re-layouts: 7.18 us -> 11.2 us
    all_to_all x2 -> x3, waiting for transfers between devices: 18.9 us -> 17.2 us  [the longest x1 6.41 us: body(): totals = lax.all_to_all(totals, ('r', 'l'), 0, 0, tiled=True)]
    pallas_call x14 -> x16, Pallas kernels: 16.1 us -> 16.6 us  [call(): pl.pallas_call(kernel, out_shape=out, scratch_shapes=list(scratch), compi...]
  transfers between devices with their start and end apart: 10 -> 11, of which waited for: 6 -> 7; matrix products, arithmetic and copies ran while one was open for 0% -> 0% of each run, Pallas kernels for 3% -> 3%
where the time goes in v8:
time: 227 us; the launch traced here: 225 us
  blocking collectives  75.8 us (33%)
  starting transfers between devices  74.8 us (33%)
  waiting for transfers between devices  45.7 us (20%)
  Pallas kernels  16.6 us (7%)
  local copies, waits for them, and re-layouts  12.2 us (5%)
    all_gather x1, blocking collectives, body(): arrived = lax.all_gather(near_rows, ('r', 'l'), axis=0, tiled=True)  28.4 us
    all_gather x1, blocking collectives, body(): act = lax.all_gather(act, 'r', axis=0, tiled=True)  26.7 us
    all_to_all x1, starting transfers between devices, body(): weighted = lax.all_to_all(weighted, 'p', 0, 0, tiled=True)  19.4 us
    pallas_call x16, Pallas kernels, call(): pl.pallas_call(kernel, out_shape=out, scratch_shapes=list(scratch), compi...  16.6 us
    all_to_all x1, starting transfers between devices, body(): totals = lax.all_to_all(totals, ('r', 'l'), 0, 0, tiled=True)  14.9 us
    all_to_all x1, waiting for transfers between devices, body(): back = lax.all_to_all(back, ('r', 'l'), 0, 0, tiled=True)  11.7 us
    unnamed x32, local copies, waits for them, and re-layouts  11.2 us
    all_to_all x1, blocking collectives, body(): back = lax.all_to_all(out, 'y', 0, 0, tiled=True)  11 us
  transfers between devices with their start and end apart: 11, of which 7 were waited for; matrix products, arithmetic and copies ran while one was open for 0% of the time, Pallas kernels for 3%

profile of v8, /device:TPU:1, one launch (start us, length us, event | category | flops | bytes accessed | tf_op | source)
XLA Modules:
  0.0 225.4 jit_solution(17260488100123297254)
XLA Ops:
  0.0 1.1 copy-done.2
  1.1 1.0 copy-done.4
  2.1 0.5 state.1
  2.6 9.7 %all_to_all.55.in_ref = bf16[4,144,128]{2,1,0:T(8,128)(2,1)S(1)} all-to-all(bf16[4,144,128]{2,1,0:T(8,128)(2,1)S(1)} %state.1), channel_id=1, replica_groups=mesh['r'=8,'l'=2,'y'=4,'p'=8] {'y'}, dimensions={0} | all-to-all | bytes 294912 | tf_op jit(solution)/shard_map/all_to_all | solution.py:310
  12.4 0.7 total.1
  13.0 14.9 %all-to-all-start.1 = ((bf16[16,16,128]{2,1,0:T(8,128)(2,1)}), bf16[16,16,128]{2,1,0:T(8,128)(2,1)S(1)}, u32[]{:S(2)}, u32[]{:S(2)}) async-start(bf16[16,16,128]{2,1,0:T(8,128)(2,1)} %total.1), calls=%async_computation.1 | async-start | bytes 131072 | tf_op jit(solution)/shard_map/all_to_all | solution.py:319
  28.0 1.0 copy-done.3
  28.9 1.0 copy-done.5
  29.9 1.0 copy-done.6
  30.9 0.9 inner.1.inner_ref
  31.9 1.3 cut_up.1
  33.2 6.4 %all-to-all-done.1.in_ref = bf16[16,16,128]{2,1,0:T(8,128)(2,1)S(1)} async-done(((bf16[16,16,128]{2,1,0:T(8,128)(2,1)}), bf16[16,16,128]{2,1,0:T(8,128)(2,1)S(1)}, u32[]{:S(2)}, u32[]{:S(2)}) %all-to-all-start.1) | async-done | bytes 65568 | tf_op jit(solution)/shard_map/all_to_all | solution.py:319
  39.6 0.6 prefix.1
  40.3 5.1 %all-to-all-start.2 = ((bf16[16,16,128]{2,1,0:T(8,128)(2,1)}), bf16[16,16,128]{2,1,0:T(8,128)(2,1)S(1)}, u32[]{:S(2)}, u32[]{:S(2)}) async-start(bf16[16,16,128]{2,1,0:T(8,128)(2,1)} %prefix.1), calls=%async_computation.2 | async-start | bytes 131072 | tf_op jit(solution)/shard_map/all_to_all | solution.py:331
  45.3 1.5 copy-done.1
  46.8 3.1 %cut_down.1 = (bf16[4,96,1152]{2,1,0:T(8,128)(2,1)S(1)}, bf16[2,96,1152]{2,1,0:T(8,128)(2,1)S(1)}, bf16[2,96,1152]{2,1,0:T(8,128)(2,1)S(1)}) custom-call(s32[1]{0:T(128)} %bitcast.1.place_ref, bf16[96,9216]{1,0:T(8,128)(2,1)S(1)} %bitcast.17), custom_call_target="tpu_custom_call" | custom-call | tf_op jit(solution)/shard_map/cut_down/pallas_call | solution.py:29
  50.0 0.9 copy-done.8
  50.9 6.0 %all-to-all-done.2.base_ref = bf16[16,16,128]{2,1,0:T(8,128)(2,1)S(1)} async-done(((bf16[16,16,128]{2,1,0:T(8,128)(2,1)}), bf16[16,16,128]{2,1,0:T(8,128)(2,1)S(1)}, u32[]{:S(2)}, u32[]{:S(2)}) %all-to-all-start.2) | async-done | bytes 65568 | tf_op jit(solution)/shard_map/all_to_all | solution.py:331
  56.9 0.7 spread.1
  57.6 2.7 %collective-permute-start = (bf16[2,96,1152]{2,1,0:T(8,128)(2,1)S(1)}, bf16[2,96,1152]{2,1,0:T(8,128)(2,1)S(1)}, u32[]{:S(2)}, u32[]{:S(2)}) collective-permute-start(bf16[2,96,1152]{2,1,0:T(8,128)(2,1)S(1)} %get-tuple-element.52), channel_id=1, source_target_pairs={{0,32},{32,0},{1,33},{33,1},{2,34},{34,2},{3,35},{35,3},{4,36},{36... | collective-permute-start | bytes 1327112 | tf_op jit(solution)/shard_map/ppermute | solution.py:355
  60.2 3.3 %all-to-all-start.3 = ((bf16[4,144,128]{2,1,0:T(8,128)(2,1)}), bf16[4,144,128]{2,1,0:T(8,128)(2,1)S(1)}, u32[]{:S(2)}, u32[]{:S(2)}) async-start(bf16[4,144,128]{2,1,0:T(8,128)(2,1)} %spread.1), calls=%async_computation.3 | async-start | bytes 294912 | tf_op jit(solution)/shard_map/all_to_all | solution.py:354
  63.7 4.8 %all-to-all-done.3.p_ref = bf16[4,144,128]{2,1,0:T(8,128)(2,1)S(1)} async-done(((bf16[4,144,128]{2,1,0:T(8,128)(2,1)}), bf16[4,144,128]{2,1,0:T(8,128)(2,1)S(1)}, u32[]{:S(2)}, u32[]{:S(2)}) %all-to-all-start.3) | async-done | bytes 147488 | tf_op jit(solution)/shard_map/all_to_all | solution.py:354
  68.5 1.0 attn.1
  69.5 0.7 copy-done.12
  70.3 2.6 %collective-permute-start.1 = (bf16[2,96,1152]{2,1,0:T(8,128)(2,1)S(1)}, bf16[2,96,1152]{2,1,0:T(8,128)(2,1)S(1)}, u32[]{:S(2)}, u32[]{:S(2)}) collective-permute-start(bf16[2,96,1152]{2,1,0:T(8,128)(2,1)S(1)} %get-tuple-element.59), channel_id=1, source_target_pairs={{0,32},{32,0},{1,33},{33,1},{2,34},{34,2},{3,35},{35,3},{4,36},{36... | collective-permute-start | bytes 1327112 | tf_op jit(solution)/shard_map/ppermute | solution.py:373
  72.9 0.7 tile.19
  73.6 10.9 %all-to-all-start.4 = ((bf16[32,32,128]{2,1,0:T(8,128)(2,1)}), bf16[32,32,128]{2,1,0:T(8,128)(2,1)S(1)}, u32[]{:S(2)}, u32[]{:S(2)}) async-start(bf16[32,32,128]{2,1,0:T(8,128)(2,1)} %bitcast.7), calls=%async_computation.4 | async-start | bytes 524288 | tf_op jit(solution)/shard_map/all_to_all | solution.py:374
  84.5 8.9 %all-to-all-done.4.row_ref = bf16[32,32,128]{2,1,0:T(8,128)(2,1)S(1)} async-done(((bf16[32,32,128]{2,1,0:T(8,128)(2,1)}), bf16[32,32,128]{2,1,0:T(8,128)(2,1)S(1)}, u32[]{:S(2)}, u32[]{:S(2)}) %all-to-all-start.4) | async-done | bytes 262176 | tf_op jit(solution)/shard_map/all_to_all | solution.py:374
  93.4 0.8 copy-done.10
  94.2 3.6 %all-to-all-start.5 = ((bf16[4,144,1536]{2,1,0:T(8,128)(2,1)}), bf16[4,144,1536]{2,1,0:T(8,128)(2,1)S(1)}, u32[]{:S(2)}, u32[]{:S(2)}) async-start(bf16[4,144,1536]{2,1,0:T(8,128)(2,1)} %cut_up.1), calls=%async_computation.5 | async-start | bytes 3538944 | tf_op jit(solution)/shard_map/all_to_all | solution.py:386
  97.8 28.4 %all_gather.6.x_ref = bf16[3840,128]{1,0:T(8,128)(2,1)S(1)} all-gather(bf16[240,128]{1,0:T(8,128)(2,1)S(1)} %near.1), channel_id=1, replica_groups=mesh['r'=8,'l'=2,'y'=4,'p'=8] {'r','l'}, dimensions={0}, use_global_device_ids=true | all-gather | bytes 1044480 | tf_op jit(solution)/shard_map/all_gather | solution.py:387
  126.2 2.1 up.1
  128.2 3.5 %all-to-all-start.6 = ((bf16[4,144,384]{2,1,0:T(8,128)(2,1)}), bf16[4,144,384]{2,1,0:T(8,128)(2,1)S(1)}, u32[]{:S(2)}, u32[]{:S(2)}) async-start(bf16[4,144,384]{2,1,0:T(8,128)(2,1)} %bitcast.9), calls=%async_computation.6 | async-start | bytes 884736 | tf_op jit(solution)/shard_map/all_to_all | solution.py:397
  131.7 1.2 copy-done.9
  132.9 1.0 copy-done.11
  133.9 1.3 join.1
  135.2 2.9 %all-to-all-done.6.in_ref = bf16[4,144,384]{2,1,0:T(8,128)(2,1)S(1)} async-done(((bf16[4,144,384]{2,1,0:T(8,128)(2,1)}), bf16[4,144,384]{2,1,0:T(8,128)(2,1)S(1)}, u32[]{:S(2)}, u32[]{:S(2)}) %all-to-all-start.6) | async-done | bytes 442400 | tf_op jit(solution)/shard_map/all_to_all | solution.py:397
  138.3 3.6 %all-to-all-start.7 = ((bf16[4,2,96,1152]{3,2,1,0:T(8,128)(2,1)}), bf16[4,2,96,1152]{3,2,1,0:T(8,128)(2,1)S(1)}, u32[]{:S(2)}, u32[]{:S(2)}) async-start(bf16[4,2,96,1152]{3,2,1,0:T(8,128)(2,1)} %join.1), calls=%async_computation.7 | async-start | bytes 3538944 | tf_op jit(solution)/shard_map/all_to_all | solution.py:412
  141.9 26.7 %all_gather.7.h_ref = bf16[1152,384]{1,0:T(8,128)(2,1)S(1)} all-gather(bf16[144,384]{1,0:T(8,128)(2,1)S(1)} %act.1), channel_id=1, replica_groups=mesh['r'=8,'l'=2,'y'=4,'p'=8] {'r'}, dimensions={0}, use_global_device_ids=true | all-gather | bytes 995328 | tf_op jit(solution)/shard_map/all_gather | solution.py:413
  168.6 1.5 down.1
  170.2 11.0 %all_to_all.56.in_ref = bf16[64,32,128]{2,1,0:T(8,128)(2,1)S(1)} all-to-all(bf16[64,32,128]{2,1,0:T(8,128)(2,1)S(1)} %down.1), channel_id=1, replica_groups=mesh['r'=8,'l'=2,'y'=4,'p'=8] {'y'}, dimensions={0} | all-to-all | bytes 1048576 | tf_op jit(solution)/shard_map/all_to_all | solution.py:425
  181.2 0.7 sum.1
  181.9 5.4 %all-to-all-start.9 = ((bf16[16,32,128]{2,1,0:T(8,128)(2,1)}), bf16[16,32,128]{2,1,0:T(8,128)(2,1)S(1)}, u32[]{:S(2)}, u32[]{:S(2)}) async-start(bf16[16,32,128]{2,1,0:T(8,128)(2,1)} %sum.1), calls=%async_computation.9 | async-start | bytes 262144 | tf_op jit(solution)/shard_map/all_to_all | solution.py:427
  187.5 11.7 %all-to-all-done.9.y_ref = bf16[16,32,128]{2,1,0:T(8,128)(2,1)S(1)} async-done(((bf16[16,32,128]{2,1,0:T(8,128)(2,1)}), bf16[16,32,128]{2,1,0:T(8,128)(2,1)S(1)}, u32[]{:S(2)}, u32[]{:S(2)}) %all-to-all-start.9) | async-done | bytes 131104 | tf_op jit(solution)/shard_map/all_to_all | solution.py:427
  199.3 0.9 weigh.1
  200.1 19.4 %all-to-all-start.10 = ((bf16[8,32,128]{2,1,0:T(8,128)(2,1)}), bf16[8,32,128]{2,1,0:T(8,128)(2,1)S(1)}, u32[]{:S(2)}, u32[]{:S(2)}) async-start(bf16[8,32,128]{2,1,0:T(8,128)(2,1)} %weigh.1), calls=%async_computation.10 | async-start | bytes 131072 | tf_op jit(solution)/shard_map/all_to_all | solution.py:438
  219.5 4.9 %all-to-all-done.10.y_ref = bf16[8,32,128]{2,1,0:T(8,128)(2,1)S(1)} async-done(((bf16[8,32,128]{2,1,0:T(8,128)(2,1)}), bf16[8,32,128]{2,1,0:T(8,128)(2,1)S(1)}, u32[]{:S(2)}, u32[]{:S(2)}) %all-to-all-start.10) | async-done | bytes 65568 | tf_op jit(solution)/shard_map/all_to_all | solution.py:438
  224.4 1.0 add.6
  (37 shorter events, 0.5 us)
Async XLA Ops:
  0.0 31.9 %copy-start = (bf16[1,144,6144]{2,1,0:T(8,128)(2,1)S(1)}, bf16[1,144,6144]{2,1,0:T(8,128)(2,1)}, u32[]{:S(2)}) copy-start(bf16[1,144,6144]{2,1,0:T(8,128)(2,1)} %param.12) | copy-start | bytes 5308420
  0.0 1.1 copy-start.2
  1.1 1.0 copy-start.4
  13.0 26.6 %all-to-all-start.1 = ((bf16[16,16,128]{2,1,0:T(8,128)(2,1)}), bf16[16,16,128]{2,1,0:T(8,128)(2,1)S(1)}, u32[]{:S(2)}, u32[]{:S(2)}) async-start(bf16[16,16,128]{2,1,0:T(8,128)(2,1)} %total.1), calls=%async_computation.1 | async-start | bytes 131072 | tf_op jit(solution)/shard_map/all_to_all | solution.py:319
  27.9 1.0 copy-start.3
  28.9 1.0 copy-start.5
  29.9 1.0 copy-start.6
  31.9 36.6 %copy-start.7 = (bf16[256,768]{1,0:T(8,128)(2,1)S(1)}, bf16[256,768]{1,0:T(8,128)(2,1)}, u32[]{:S(2)}) copy-start(bf16[256,768]{1,0:T(8,128)(2,1)} %q_ref.1) | copy-start | bytes 1179652
  33.2 30.4 %copy-start.15 = (s32[1,8,5]{1,0,2:T(1,128)S(1)}, s32[1,8,5]{1,0,2:T(1,128)}, u32[]{:S(2)}) copy-start(s32[1,8,5]{1,0,2:T(1,128)} %param.10) | copy-start | bytes 484
  40.3 16.6 %all-to-all-start.2 = ((bf16[16,16,128]{2,1,0:T(8,128)(2,1)}), bf16[16,16,128]{2,1,0:T(8,128)(2,1)S(1)}, u32[]{:S(2)}, u32[]{:S(2)}) async-start(bf16[16,16,128]{2,1,0:T(8,128)(2,1)} %prefix.1), calls=%async_computation.2 | async-start | bytes 131072 | tf_op jit(solution)/shard_map/all_to_all | solution.py:331
  45.3 1.5 copy-start.1
  50.0 0.9 copy-start.8
  57.6 10.9 %collective-permute-start = (bf16[2,96,1152]{2,1,0:T(8,128)(2,1)S(1)}, bf16[2,96,1152]{2,1,0:T(8,128)(2,1)S(1)}, u32[]{:S(2)}, u32[]{:S(2)}) collective-permute-start(bf16[2,96,1152]{2,1,0:T(8,128)(2,1)S(1)} %get-tuple-element.52), channel_id=1, source_target_pairs={{0,32},{32,0},{1,33},{33,1},{2,34},{34,2},{3,35},{35,3},{4,36},{36... | collective-permute-start | bytes 1327112 | tf_op jit(solution)/shard_map/ppermute | solution.py:355
  60.2 8.2 %all-to-all-start.3 = ((bf16[4,144,128]{2,1,0:T(8,128)(2,1)}), bf16[4,144,128]{2,1,0:T(8,128)(2,1)S(1)}, u32[]{:S(2)}, u32[]{:S(2)}) async-start(bf16[4,144,128]{2,1,0:T(8,128)(2,1)} %spread.1), calls=%async_computation.3 | async-start | bytes 294912 | tf_op jit(solution)/shard_map/all_to_all | solution.py:354
  69.5 0.7 copy-start.12
  70.3 23.1 %collective-permute-start.1 = (bf16[2,96,1152]{2,1,0:T(8,128)(2,1)S(1)}, bf16[2,96,1152]{2,1,0:T(8,128)(2,1)S(1)}, u32[]{:S(2)}, u32[]{:S(2)}) collective-permute-start(bf16[2,96,1152]{2,1,0:T(8,128)(2,1)S(1)} %get-tuple-element.59), channel_id=1, source_target_pairs={{0,32},{32,0},{1,33},{33,1},{2,34},{34,2},{3,35},{35,3},{4,36},{36... | collective-permute-start | bytes 1327112 | tf_op jit(solution)/shard_map/ppermute | solution.py:373
  73.6 19.8 %all-to-all-start.4 = ((bf16[32,32,128]{2,1,0:T(8,128)(2,1)}), bf16[32,32,128]{2,1,0:T(8,128)(2,1)S(1)}, u32[]{:S(2)}, u32[]{:S(2)}) async-start(bf16[32,32,128]{2,1,0:T(8,128)(2,1)} %bitcast.7), calls=%async_computation.4 | async-start | bytes 524288 | tf_op jit(solution)/shard_map/all_to_all | solution.py:374
  93.4 0.8 copy-start.10
  94.2 32.0 %all-to-all-start.5 = ((bf16[4,144,1536]{2,1,0:T(8,128)(2,1)}), bf16[4,144,1536]{2,1,0:T(8,128)(2,1)S(1)}, u32[]{:S(2)}, u32[]{:S(2)}) async-start(bf16[4,144,1536]{2,1,0:T(8,128)(2,1)} %cut_up.1), calls=%async_computation.5 | async-start | bytes 3538944 | tf_op jit(solution)/shard_map/all_to_all | solution.py:386
  128.2 9.9 %all-to-all-start.6 = ((bf16[4,144,384]{2,1,0:T(8,128)(2,1)}), bf16[4,144,384]{2,1,0:T(8,128)(2,1)S(1)}, u32[]{:S(2)}, u32[]{:S(2)}) async-start(bf16[4,144,384]{2,1,0:T(8,128)(2,1)} %bitcast.9), calls=%async_computation.6 | async-start | bytes 884736 | tf_op jit(solution)/shard_map/all_to_all | solution.py:397
  131.7 1.2 copy-start.9
  132.9 1.0 copy-start.11
  138.3 30.3 %all-to-all-start.7 = ((bf16[4,2,96,1152]{3,2,1,0:T(8,128)(2,1)}), bf16[4,2,96,1152]{3,2,1,0:T(8,128)(2,1)S(1)}, u32[]{:S(2)}, u32[]{:S(2)}) async-start(bf16[4,2,96,1152]{3,2,1,0:T(8,128)(2,1)} %join.1), calls=%async_computation.7 | async-start | bytes 3538944 | tf_op jit(solution)/shard_map/all_to_all | solution.py:412
  170.2 17.2 %copy-start.14 = (bf16[6144,1]{0,1:T(2,128)(2,1)S(1)}, bf16[6144,1]{0,1:T(2,128)(2,1)}, u32[]{:S(2)}) copy-start(bf16[6144,1]{0,1:T(2,128)(2,1)} %param.11) | copy-start | bytes 36868
  170.2 54.2 %copy-start.13 = (bf16[256,768]{1,0:T(8,128)(2,1)S(1)}, bf16[256,768]{1,0:T(8,128)(2,1)}, u32[]{:S(2)}) copy-start(bf16[256,768]{1,0:T(8,128)(2,1)} %copy-done.12) | copy-start | bytes 1179652
  181.9 17.3 %all-to-all-start.9 = ((bf16[16,32,128]{2,1,0:T(8,128)(2,1)}), bf16[16,32,128]{2,1,0:T(8,128)(2,1)S(1)}, u32[]{:S(2)}, u32[]{:S(2)}) async-start(bf16[16,32,128]{2,1,0:T(8,128)(2,1)} %sum.1), calls=%async_computation.9 | async-start | bytes 262144 | tf_op jit(solution)/shard_map/all_to_all | solution.py:427
  200.1 24.3 %all-to-all-start.10 = ((bf16[8,32,128]{2,1,0:T(8,128)(2,1)}), bf16[8,32,128]{2,1,0:T(8,128)(2,1)S(1)}, u32[]{:S(2)}, u32[]{:S(2)}) async-start(bf16[8,32,128]{2,1,0:T(8,128)(2,1)} %weigh.1), calls=%async_computation.10 | async-start | bytes 131072 | tf_op jit(solution)/shard_map/all_to_all | solution.py:438

commit v9 on v8

--- a/solution.py
+++ b/solution.py
@@ -47,6 +47,11 @@
     return first * LANES, (last + 1) * LANES, head * HEAD - first * LANES
 
 
+def eighth(tile, rows8):
+    group = tile * 12 + rows8
+    return group % 8, group // 8 * 8
+
+
 def state_kernel(k_ref, v_ref, out_ref, grand, rows):
     grand[...] = lax.dot_general(
         k_ref[...], v_ref[...], (((0,), (0,)), ((), ())), preferred_element_type=F32
@@ -58,35 +63,36 @@
         one = grand[head * HEAD : (head + 1) * HEAD, at]
         two = grand[(head + 1) * HEAD : (head + 2) * HEAD, at]
         block = jnp.where(lane < split, one, two)
-        for quarter in range(4):
-            rows[quarter, tile * 24 : tile * 24 + 24] = block[quarter * 24 : quarter * 24 + 24]
+        for rows8 in range(12):
+            part, low = eighth(tile, rows8)
+            rows[part, low : low + 8] = block[rows8 * 8 : rows8 * 8 + 8]
     out_ref[...] = rows[...].astype(BF16)
 
 
 def total_kernel(in_ref, out_ref, rows):
     total = in_ref[0].astype(F32)
-    for y in range(1, 4):
-        total = total + in_ref[y].astype(F32)
-    rows[0:144] = total
-    rows[144:152] = jnp.zeros((8, LANES), F32)
-    for z in range(16):
-        out_ref[z] = rows[z * 9 : z * 9 + 16].astype(BF16)
+    for part in range(1, 8):
+        total = total + in_ref[part].astype(F32)
+    rows[0:72] = total
+    rows[72:128] = jnp.zeros((56, LANES), F32)
+    for part in range(8):
+        out_ref[part] = rows[pl.ds(part, 16, stride=8), :].astype(BF16)
 
 
 def prefix_kernel(in_ref, out_ref):
     total = jnp.zeros((16, LANES), F32)
-    for z in range(16):
-        out_ref[z] = total.astype(BF16)
-        total = total + in_ref[z].astype(F32)
+    for part in range(8):
+        out_ref[part] = total.astype(BF16)
+        total = total + in_ref[part].astype(F32)
 
 
 def spread_kernel(base_ref, in_ref, out_ref, rows):
-    for z in range(16):
-        rows[z * 9 : z * 9 + 9] = base_ref[z].astype(F32)[0:9]
-    total = rows[...]
-    for y in range(4):
-        out_ref[y] = total.astype(BF16)
-        total = total + in_ref[y].astype(F32)
+    for part in range(8):
+        rows[pl.ds(part, 16, stride=8), :] = base_ref[part].astype(F32)
+    total = rows[0:72]
+    for part in range(8):
+        out_ref[part] = total.astype(BF16)
+        total = total + in_ref[part].astype(F32)
 
 
 def inner_kernel(q_ref, k_ref, v_ref, out_ref):
@@ -110,11 +116,12 @@
 
 def attn_kernel(q_ref, inner_ref, p_ref, sel_ref, attn_ref, pay_ref, rows, wide, normed, picks):
     length = q_ref.shape[0]
-    for quarter in range(4):
-        part = p_ref[quarter].astype(F32)
-        for tile in range(6):
-            low = tile * HEAD + quarter * 24
-            rows[low : low + 24] = part[tile * 24 : tile * 24 + 24]
+    parts = [p_ref[part].astype(F32) for part in range(8)]
+    for tile in range(6):
+        for rows8 in range(12):
+            part, low = eighth(tile, rows8)
+            at = tile * HEAD + rows8 * 8
+            rows[at : at + 8] = parts[part][low : low + 8]
     wide[...] = jnp.zeros_like(wide)
     lane = lax.broadcasted_iota(jnp.int32, (HEAD, LANES), 1)
     for tile in range(6):
@@ -237,14 +244,14 @@
                 i * 64 : i * 64 + 64, tile * LANES : (tile + 1) * LANES
             ]
     for block in range(64):
-        z, y = divmod(block, 4)
-        out_ref[y * 16 + z] = rows[block * SLOTS : (block + 1) * SLOTS].astype(BF16)
+        r, place = divmod(block, 8)
+        out_ref[place * 8 + r] = rows[block * SLOTS : (block + 1) * SLOTS].astype(BF16)
 
 
 def sum_kernel(in_ref, out_ref):
-    total = in_ref[0:16].astype(F32)
-    for part in range(1, 4):
-        total = total + in_ref[part * 16 : part * 16 + 16].astype(F32)
+    total = in_ref[0:8].astype(F32)
+    for part in range(1, 8):
+        total = total + in_ref[part * 8 : part * 8 + 8].astype(F32)
     out_ref[...] = total.astype(BF16)
 
 
@@ -261,8 +268,7 @@
     )
     gate = jax.nn.sigmoid(jnp.sum(sums, axis=-1, keepdims=True))
     for group in range(8):
-        total = y_ref[group * 2].astype(F32) + y_ref[group * 2 + 1].astype(F32)
-        out_ref[group] = (total * gate).astype(BF16)
+        out_ref[group] = (y_ref[group].astype(F32) * gate).astype(BF16)
 
 
 def add_kernel(attn_ref, y_ref, sel_ref, out_ref, rows, weighted):
@@ -287,7 +293,7 @@
 def body(queries, keys, values, selections, router, w_up, w_down):
     length, width = queries.shape
     parts = lax.axis_size("p")
-    seq = ("r", "l", "y")
+    patch = ("l", "y")
     units = w_up.shape[1]
     quarter = w_up.shape[2] // 4
     place = lax.axis_index("y").astype(jnp.int32)
@@ -301,22 +307,24 @@
 
     state = call(
         state_kernel,
-        shape((4, 144, LANES)),
+        shape((8, 72, LANES)),
         keys,
         values,
-        scratch=[pltpu.VMEM((width, width), F32), pltpu.VMEM((4, 144, LANES), F32)],
+        scratch=[pltpu.VMEM((width, width), F32), pltpu.VMEM((8, 72, LANES), F32)],
         name="state",
     )
-    quarters = lax.all_to_all(state, "y", 0, 0, tiled=True)
-    quarters, queries, w_up, w_down = lax.optimization_barrier((quarters, queries, w_up, w_down))
+    parts_here = lax.all_to_all(state, patch, 0, 0, tiled=True)
+    parts_here, queries, w_up, w_down = lax.optimization_barrier(
+        (parts_here, queries, w_up, w_down)
+    )
     totals = call(
         total_kernel,
-        shape((16, 16, LANES)),
-        quarters,
-        scratch=[pltpu.VMEM((152, LANES), F32)],
+        shape((8, 16, LANES)),
+        parts_here,
+        scratch=[pltpu.VMEM((128, LANES), F32)],
         name="total",
     )
-    totals = lax.all_to_all(totals, ("r", "l"), 0, 0, tiled=True)
+    totals = lax.all_to_all(totals, "r", 0, 0, tiled=True)
     inner = call(inner_kernel, shape((length, width), F32), queries, keys, values, name="inner")
     up_cut = call(
         cut_up_kernel,
@@ -327,8 +335,8 @@
         name="cut_up",
     )
     totals, inner, up_cut, w_down = lax.optimization_barrier((totals, inner, up_cut, w_down))
-    bases = call(prefix_kernel, shape((16, 16, LANES)), totals, name="prefix")
-    bases = lax.all_to_all(bases, ("r", "l"), 0, 0, tiled=True)
+    bases = call(prefix_kernel, shape((8, 16, LANES)), totals, name="prefix")
+    bases = lax.all_to_all(bases, "r", 0, 0, tiled=True)
     pair = lax.axis_index("l").astype(jnp.int32).reshape(1)
     down_keep, down_one, down_two = call(
         cut_down_kernel,
@@ -344,14 +352,14 @@
     )
     before = call(
         spread_kernel,
-        shape((4, 144, LANES)),
+        shape((8, 72, LANES)),
         bases,
-        quarters,
-        scratch=[pltpu.VMEM((144, LANES), F32)],
+        parts_here,
+        scratch=[pltpu.VMEM((128, LANES), F32)],
         name="spread",
     )
     before, down_one = lax.optimization_barrier((before, down_one))
-    before = lax.all_to_all(before, "y", 0, 0, tiled=True)
+    before = lax.all_to_all(before, patch, 0, 0, tiled=True)
     down_one = lax.ppermute(down_one, "l", [(0, 1), (1, 0)])
     before, down_one, down_two = lax.optimization_barrier((before, down_one, down_two))
     attn, pay = call(
@@ -422,9 +430,9 @@
         ],
         name="down",
     )
-    back = lax.all_to_all(out, "y", 0, 0, tiled=True)
-    back = call(sum_kernel, shape((16, SLOTS, LANES)), back, name="sum")
-    back = lax.all_to_all(back, ("r", "l"), 0, 0, tiled=True)
+    back = lax.all_to_all(out, patch, 0, 0, tiled=True)
+    back = call(sum_kernel, shape((8, SLOTS, LANES)), back, name="sum")
+    back = lax.all_to_all(back, "r", 0, 0, tiled=True)
     weighted = call(
         weigh_kernel,
         shape((8, SLOTS, LANES)),

time: 227 us -> 233 us (1.026)
  waiting for transfers between devices: 45.7 us -> 49.1 us
  blocking collectives: 75.8 us -> 78.3 us
    ppermute x1, waiting for transfers between devices: 0.01 us -> 7.69 us  [body(): down_one = lax.ppermute(down_one, 'l', [(0, 1), (1, 0)])]
    all_to_all x4, waiting for transfers between devices: 28.9 us -> 24.7 us  [the longest x1 11.9 us: body(): back = lax.all_to_all(back, 'r', 0, 0, tiled=True)]
    all_to_all x2, blocking collectives: 20.8 us -> 24.2 us  [the longest x1 12.5 us: body(): back = lax.all_to_all(out, patch, 0, 0, tiled=True)]
where the time goes in v9:
time: 233 us; the launch traced here: 232 us
  blocking collectives  78.3 us (34%)
  starting transfers between devices  75.3 us (32%)
  waiting for transfers between devices  49.1 us (21%)
  Pallas kernels  16.5 us (7%)
  local copies, waits for them, and re-layouts  12.2 us (5%)
    all_gather x1, blocking collectives, body(): act = lax.all_gather(act, 'r', axis=0, tiled=True)  27.6 us
    all_gather x1, blocking collectives, body(): arrived = lax.all_gather(near_rows, ('r', 'l'), axis=0, tiled=True)  26.5 us
    all_to_all x1, starting transfers between devices, body(): weighted = lax.all_to_all(weighted, 'p', 0, 0, tiled=True)  17.8 us
    pallas_call x16, Pallas kernels, call(): pl.pallas_call(kernel, out_shape=out, scratch_shapes=list(scratch), compi...  16.5 us
    all_to_all x1, starting transfers between devices, body(): totals = lax.all_to_all(totals, 'r', 0, 0, tiled=True)  13.9 us
    all_to_all x1, blocking collectives, body(): back = lax.all_to_all(out, patch, 0, 0, tiled=True)  12.5 us
    all_to_all x1, waiting for transfers between devices, body(): back = lax.all_to_all(back, 'r', 0, 0, tiled=True)  11.9 us
    all_to_all x1, blocking collectives, body(): parts_here = lax.all_to_all(state, patch, 0, 0, tiled=True)  11.7 us
  transfers between devices with their start and end apart: 11, of which 7 were waited for; matrix products, arithmetic and copies ran while one was open for 0% of the time, Pallas kernels for 3%

profile of v9, /device:TPU:1, one launch (start us, length us, event | category | flops | bytes accessed | tf_op | source)
XLA Modules:
  0.0 231.7 jit_solution(9173901843481474153)
XLA Ops:
  0.0 1.1 copy-done.2
  1.1 1.0 copy-done.4
  2.1 0.5 state.1
  2.6 11.7 %all_to_all.55.in_ref = bf16[8,72,128]{2,1,0:T(8,128)(2,1)S(1)} all-to-all(bf16[8,72,128]{2,1,0:T(8,128)(2,1)S(1)} %state.1), channel_id=1, replica_groups=mesh['r'=8,'l'=2,'y'=4,'p'=8] {'l','y'}, dimensions={0} | all-to-all | bytes 294912 | tf_op jit(solution)/shard_map/all_to_all | solution.py:316
  14.3 0.6 total.1
  15.0 13.9 %all-to-all-start.1 = ((bf16[8,16,128]{2,1,0:T(8,128)(2,1)}), bf16[8,16,128]{2,1,0:T(8,128)(2,1)S(1)}, u32[]{:S(2)}, u32[]{:S(2)}) async-start(bf16[8,16,128]{2,1,0:T(8,128)(2,1)} %total.1), calls=%async_computation.1 | async-start | bytes 65536 | tf_op jit(solution)/shard_map/all_to_all | solution.py:327
  28.9 1.0 copy-done.3
  29.9 1.0 copy-done.5
  30.9 1.0 copy-done.6
  31.9 0.9 inner.1.inner_ref
  32.9 1.3 cut_up.1
  34.2 6.6 %all-to-all-done.1.in_ref = bf16[8,16,128]{2,1,0:T(8,128)(2,1)S(1)} async-done(((bf16[8,16,128]{2,1,0:T(8,128)(2,1)}), bf16[8,16,128]{2,1,0:T(8,128)(2,1)S(1)}, u32[]{:S(2)}, u32[]{:S(2)}) %all-to-all-start.1) | async-done | bytes 32800 | tf_op jit(solution)/shard_map/all_to_all | solution.py:327
  40.7 0.6 prefix.1
  41.3 4.9 %all-to-all-start.2 = ((bf16[8,16,128]{2,1,0:T(8,128)(2,1)}), bf16[8,16,128]{2,1,0:T(8,128)(2,1)S(1)}, u32[]{:S(2)}, u32[]{:S(2)}) async-start(bf16[8,16,128]{2,1,0:T(8,128)(2,1)} %prefix.1), calls=%async_computation.2 | async-start | bytes 65536 | tf_op jit(solution)/shard_map/all_to_all | solution.py:339
  46.3 1.5 copy-done.1
  47.7 3.1 %cut_down.1 = (bf16[4,96,1152]{2,1,0:T(8,128)(2,1)S(1)}, bf16[2,96,1152]{2,1,0:T(8,128)(2,1)S(1)}, bf16[2,96,1152]{2,1,0:T(8,128)(2,1)S(1)}) custom-call(s32[1]{0:T(128)} %bitcast.1.place_ref, bf16[96,9216]{1,0:T(8,128)(2,1)S(1)} %bitcast.17), custom_call_target="tpu_custom_call" | custom-call | tf_op jit(solution)/shard_map/cut_down/pallas_call | solution.py:29
  50.9 0.9 copy-done.8
  51.8 6.2 %all-to-all-done.2.base_ref = bf16[8,16,128]{2,1,0:T(8,128)(2,1)S(1)} async-done(((bf16[8,16,128]{2,1,0:T(8,128)(2,1)}), bf16[8,16,128]{2,1,0:T(8,128)(2,1)S(1)}, u32[]{:S(2)}, u32[]{:S(2)}) %all-to-all-start.2) | async-done | bytes 32800 | tf_op jit(solution)/shard_map/all_to_all | solution.py:339
  58.0 0.7 spread.1
  58.7 3.4 %all-to-all-start.3 = ((bf16[8,72,128]{2,1,0:T(8,128)(2,1)}), bf16[8,72,128]{2,1,0:T(8,128)(2,1)S(1)}, u32[]{:S(2)}, u32[]{:S(2)}) async-start(bf16[8,72,128]{2,1,0:T(8,128)(2,1)} %spread.1), calls=%async_computation.3 | async-start | bytes 294912 | tf_op jit(solution)/shard_map/all_to_all | solution.py:362
  62.1 3.3 %collective-permute-start = (bf16[2,96,1152]{2,1,0:T(8,128)(2,1)S(1)}, bf16[2,96,1152]{2,1,0:T(8,128)(2,1)S(1)}, u32[]{:S(2)}, u32[]{:S(2)}) collective-permute-start(bf16[2,96,1152]{2,1,0:T(8,128)(2,1)S(1)} %get-tuple-element.52), channel_id=1, source_target_pairs={{0,32},{32,0},{1,33},{33,1},{2,34},{34,2},{3,35},{35,3},{4,36},{36... | collective-permute-start | bytes 1327112 | tf_op jit(solution)/shard_map/ppermute | solution.py:363
  65.5 7.7 %collective-permute-done.one_ref = bf16[2,96,1152]{2,1,0:T(8,128)(2,1)S(1)} collective-permute-done((bf16[2,96,1152]{2,1,0:T(8,128)(2,1)S(1)}, bf16[2,96,1152]{2,1,0:T(8,128)(2,1)S(1)}, u32[]{:S(2)}, u32[]{:S(2)}) %collective-permute-start) | collective-permute-done | bytes 442400 | tf_op jit(solution)/shard_map/ppermute | solution.py:363
  73.2 1.0 attn.1
  74.2 0.7 copy-done.12
  75.0 3.0 %collective-permute-start.1 = (bf16[2,96,1152]{2,1,0:T(8,128)(2,1)S(1)}, bf16[2,96,1152]{2,1,0:T(8,128)(2,1)S(1)}, u32[]{:S(2)}, u32[]{:S(2)}) collective-permute-start(bf16[2,96,1152]{2,1,0:T(8,128)(2,1)S(1)} %get-tuple-element.59), channel_id=1, source_target_pairs={{0,32},{32,0},{1,33},{33,1},{2,34},{34,2},{3,35},{35,3},{4,36},{36... | collective-permute-start | bytes 1327112 | tf_op jit(solution)/shard_map/ppermute | solution.py:381
  77.9 0.7 tile.19
  78.7 11.6 %all-to-all-start.4 = ((bf16[32,32,128]{2,1,0:T(8,128)(2,1)}), bf16[32,32,128]{2,1,0:T(8,128)(2,1)S(1)}, u32[]{:S(2)}, u32[]{:S(2)}) async-start(bf16[32,32,128]{2,1,0:T(8,128)(2,1)} %bitcast.7), calls=%async_computation.4 | async-start | bytes 524288 | tf_op jit(solution)/shard_map/all_to_all | solution.py:382
  90.3 8.9 %all-to-all-done.4.row_ref = bf16[32,32,128]{2,1,0:T(8,128)(2,1)S(1)} async-done(((bf16[32,32,128]{2,1,0:T(8,128)(2,1)}), bf16[32,32,128]{2,1,0:T(8,128)(2,1)S(1)}, u32[]{:S(2)}, u32[]{:S(2)}) %all-to-all-start.4) | async-done | bytes 262176 | tf_op jit(solution)/shard_map/all_to_all | solution.py:382
  99.2 0.8 copy-done.10
  100.0 3.6 %all-to-all-start.5 = ((bf16[4,144,1536]{2,1,0:T(8,128)(2,1)}), bf16[4,144,1536]{2,1,0:T(8,128)(2,1)S(1)}, u32[]{:S(2)}, u32[]{:S(2)}) async-start(bf16[4,144,1536]{2,1,0:T(8,128)(2,1)} %cut_up.1), calls=%async_computation.5 | async-start | bytes 3538944 | tf_op jit(solution)/shard_map/all_to_all | solution.py:394
  103.6 26.5 %all_gather.6.x_ref = bf16[3840,128]{1,0:T(8,128)(2,1)S(1)} all-gather(bf16[240,128]{1,0:T(8,128)(2,1)S(1)} %near.1), channel_id=1, replica_groups=mesh['r'=8,'l'=2,'y'=4,'p'=8] {'r','l'}, dimensions={0}, use_global_device_ids=true | all-gather | bytes 1044480 | tf_op jit(solution)/shard_map/all_gather | solution.py:395
  130.1 2.1 up.1
  132.2 3.8 %all-to-all-start.6 = ((bf16[4,144,384]{2,1,0:T(8,128)(2,1)}), bf16[4,144,384]{2,1,0:T(8,128)(2,1)S(1)}, u32[]{:S(2)}, u32[]{:S(2)}) async-start(bf16[4,144,384]{2,1,0:T(8,128)(2,1)} %bitcast.9), calls=%async_computation.6 | async-start | bytes 884736 | tf_op jit(solution)/shard_map/all_to_all | solution.py:405
  136.0 1.2 copy-done.9
  137.1 1.0 copy-done.11
  138.2 1.3 join.1
  139.5 3.0 %all-to-all-done.6.in_ref = bf16[4,144,384]{2,1,0:T(8,128)(2,1)S(1)} async-done(((bf16[4,144,384]{2,1,0:T(8,128)(2,1)}), bf16[4,144,384]{2,1,0:T(8,128)(2,1)S(1)}, u32[]{:S(2)}, u32[]{:S(2)}) %all-to-all-start.6) | async-done | bytes 442400 | tf_op jit(solution)/shard_map/all_to_all | solution.py:405
  142.6 3.6 %all-to-all-start.7 = ((bf16[4,2,96,1152]{3,2,1,0:T(8,128)(2,1)}), bf16[4,2,96,1152]{3,2,1,0:T(8,128)(2,1)S(1)}, u32[]{:S(2)}, u32[]{:S(2)}) async-start(bf16[4,2,96,1152]{3,2,1,0:T(8,128)(2,1)} %join.1), calls=%async_computation.7 | async-start | bytes 3538944 | tf_op jit(solution)/shard_map/all_to_all | solution.py:420
  146.2 27.6 %all_gather.7.h_ref = bf16[1152,384]{1,0:T(8,128)(2,1)S(1)} all-gather(bf16[144,384]{1,0:T(8,128)(2,1)S(1)} %act.1), channel_id=1, replica_groups=mesh['r'=8,'l'=2,'y'=4,'p'=8] {'r'}, dimensions={0}, use_global_device_ids=true | all-gather | bytes 995328 | tf_op jit(solution)/shard_map/all_gather | solution.py:421
  173.8 1.5 down.1
  175.4 12.5 %all_to_all.56.in_ref = bf16[64,32,128]{2,1,0:T(8,128)(2,1)S(1)} all-to-all(bf16[64,32,128]{2,1,0:T(8,128)(2,1)S(1)} %down.1), channel_id=1, replica_groups=mesh['r'=8,'l'=2,'y'=4,'p'=8] {'l','y'}, dimensions={0} | all-to-all | bytes 1048576 | tf_op jit(solution)/shard_map/all_to_all | solution.py:433
  187.9 0.7 sum.1
  188.6 6.4 %all-to-all-start.9 = ((bf16[8,32,128]{2,1,0:T(8,128)(2,1)}), bf16[8,32,128]{2,1,0:T(8,128)(2,1)S(1)}, u32[]{:S(2)}, u32[]{:S(2)}) async-start(bf16[8,32,128]{2,1,0:T(8,128)(2,1)} %sum.1), calls=%async_computation.9 | async-start | bytes 131072 | tf_op jit(solution)/shard_map/all_to_all | solution.py:435
  195.2 11.9 %all-to-all-done.9.y_ref = bf16[8,32,128]{2,1,0:T(8,128)(2,1)S(1)} async-done(((bf16[8,32,128]{2,1,0:T(8,128)(2,1)}), bf16[8,32,128]{2,1,0:T(8,128)(2,1)S(1)}, u32[]{:S(2)}, u32[]{:S(2)}) %all-to-all-start.9) | async-done | bytes 65568 | tf_op jit(solution)/shard_map/all_to_all | solution.py:435
  207.1 0.9 weigh.1
  208.0 17.8 %all-to-all-start.10 = ((bf16[8,32,128]{2,1,0:T(8,128)(2,1)}), bf16[8,32,128]{2,1,0:T(8,128)(2,1)S(1)}, u32[]{:S(2)}, u32[]{:S(2)}) async-start(bf16[8,32,128]{2,1,0:T(8,128)(2,1)} %weigh.1), calls=%async_computation.10 | async-start | bytes 131072 | tf_op jit(solution)/shard_map/all_to_all | solution.py:446
  225.8 4.8 %all-to-all-done.10.y_ref = bf16[8,32,128]{2,1,0:T(8,128)(2,1)S(1)} async-done(((bf16[8,32,128]{2,1,0:T(8,128)(2,1)}), bf16[8,32,128]{2,1,0:T(8,128)(2,1)S(1)}, u32[]{:S(2)}, u32[]{:S(2)}) %all-to-all-start.10) | async-done | bytes 65568 | tf_op jit(solution)/shard_map/all_to_all | solution.py:446
  230.6 1.0 add.6
  (37 shorter events, 0.5 us)
Async XLA Ops:
  0.0 32.8 %copy-start = (bf16[1,144,6144]{2,1,0:T(8,128)(2,1)S(1)}, bf16[1,144,6144]{2,1,0:T(8,128)(2,1)}, u32[]{:S(2)}) copy-start(bf16[1,144,6144]{2,1,0:T(8,128)(2,1)} %param.12) | copy-start | bytes 5308420
  0.0 1.1 copy-start.2
  1.1 1.0 copy-start.4
  15.0 25.7 %all-to-all-start.1 = ((bf16[8,16,128]{2,1,0:T(8,128)(2,1)}), bf16[8,16,128]{2,1,0:T(8,128)(2,1)S(1)}, u32[]{:S(2)}, u32[]{:S(2)}) async-start(bf16[8,16,128]{2,1,0:T(8,128)(2,1)} %total.1), calls=%async_computation.1 | async-start | bytes 65536 | tf_op jit(solution)/shard_map/all_to_all | solution.py:327
  28.9 1.0 copy-start.3
  29.9 1.0 copy-start.5
  30.9 1.0 copy-start.6
  32.8 40.3 %copy-start.7 = (bf16[256,768]{1,0:T(8,128)(2,1)S(1)}, bf16[256,768]{1,0:T(8,128)(2,1)}, u32[]{:S(2)}) copy-start(bf16[256,768]{1,0:T(8,128)(2,1)} %q_ref.1) | copy-start | bytes 1179652
  34.1 31.2 %copy-start.15 = (s32[1,8,5]{1,0,2:T(1,128)S(1)}, s32[1,8,5]{1,0,2:T(1,128)}, u32[]{:S(2)}) copy-start(s32[1,8,5]{1,0,2:T(1,128)} %param.10) | copy-start | bytes 484
  41.3 16.7 %all-to-all-start.2 = ((bf16[8,16,128]{2,1,0:T(8,128)(2,1)}), bf16[8,16,128]{2,1,0:T(8,128)(2,1)S(1)}, u32[]{:S(2)}, u32[]{:S(2)}) async-start(bf16[8,16,128]{2,1,0:T(8,128)(2,1)} %prefix.1), calls=%async_computation.2 | async-start | bytes 65536 | tf_op jit(solution)/shard_map/all_to_all | solution.py:339
  46.2 1.5 copy-start.1
  50.9 0.9 copy-start.8
  58.7 14.5 %all-to-all-start.3 = ((bf16[8,72,128]{2,1,0:T(8,128)(2,1)}), bf16[8,72,128]{2,1,0:T(8,128)(2,1)S(1)}, u32[]{:S(2)}, u32[]{:S(2)}) async-start(bf16[8,72,128]{2,1,0:T(8,128)(2,1)} %spread.1), calls=%async_computation.3 | async-start | bytes 294912 | tf_op jit(solution)/shard_map/all_to_all | solution.py:362
  62.1 11.1 %collective-permute-start = (bf16[2,96,1152]{2,1,0:T(8,128)(2,1)S(1)}, bf16[2,96,1152]{2,1,0:T(8,128)(2,1)S(1)}, u32[]{:S(2)}, u32[]{:S(2)}) collective-permute-start(bf16[2,96,1152]{2,1,0:T(8,128)(2,1)S(1)} %get-tuple-element.52), channel_id=1, source_target_pairs={{0,32},{32,0},{1,33},{33,1},{2,34},{34,2},{3,35},{35,3},{4,36},{36... | collective-permute-start | bytes 1327112 | tf_op jit(solution)/shard_map/ppermute | solution.py:363
  74.2 0.7 copy-start.12
  75.0 24.3 %collective-permute-start.1 = (bf16[2,96,1152]{2,1,0:T(8,128)(2,1)S(1)}, bf16[2,96,1152]{2,1,0:T(8,128)(2,1)S(1)}, u32[]{:S(2)}, u32[]{:S(2)}) collective-permute-start(bf16[2,96,1152]{2,1,0:T(8,128)(2,1)S(1)} %get-tuple-element.59), channel_id=1, source_target_pairs={{0,32},{32,0},{1,33},{33,1},{2,34},{34,2},{3,35},{35,3},{4,36},{36... | collective-permute-start | bytes 1327112 | tf_op jit(solution)/shard_map/ppermute | solution.py:381
  78.7 20.5 %all-to-all-start.4 = ((bf16[32,32,128]{2,1,0:T(8,128)(2,1)}), bf16[32,32,128]{2,1,0:T(8,128)(2,1)S(1)}, u32[]{:S(2)}, u32[]{:S(2)}) async-start(bf16[32,32,128]{2,1,0:T(8,128)(2,1)} %bitcast.7), calls=%async_computation.4 | async-start | bytes 524288 | tf_op jit(solution)/shard_map/all_to_all | solution.py:382
  99.2 0.8 copy-start.10
  100.0 30.1 %all-to-all-start.5 = ((bf16[4,144,1536]{2,1,0:T(8,128)(2,1)}), bf16[4,144,1536]{2,1,0:T(8,128)(2,1)S(1)}, u32[]{:S(2)}, u32[]{:S(2)}) async-start(bf16[4,144,1536]{2,1,0:T(8,128)(2,1)} %cut_up.1), calls=%async_computation.5 | async-start | bytes 3538944 | tf_op jit(solution)/shard_map/all_to_all | solution.py:394
  132.2 10.3 %all-to-all-start.6 = ((bf16[4,144,384]{2,1,0:T(8,128)(2,1)}), bf16[4,144,384]{2,1,0:T(8,128)(2,1)S(1)}, u32[]{:S(2)}, u32[]{:S(2)}) async-start(bf16[4,144,384]{2,1,0:T(8,128)(2,1)} %bitcast.9), calls=%async_computation.6 | async-start | bytes 884736 | tf_op jit(solution)/shard_map/all_to_all | solution.py:405
  136.0 1.2 copy-start.9
  137.1 1.0 copy-start.11
  142.6 31.2 %all-to-all-start.7 = ((bf16[4,2,96,1152]{3,2,1,0:T(8,128)(2,1)}), bf16[4,2,96,1152]{3,2,1,0:T(8,128)(2,1)S(1)}, u32[]{:S(2)}, u32[]{:S(2)}) async-start(bf16[4,2,96,1152]{3,2,1,0:T(8,128)(2,1)} %join.1), calls=%async_computation.7 | async-start | bytes 3538944 | tf_op jit(solution)/shard_map/all_to_all | solution.py:420
  173.8 21.3 %copy-start.14 = (bf16[6144,1]{0,1:T(2,128)(2,1)S(1)}, bf16[6144,1]{0,1:T(2,128)(2,1)}, u32[]{:S(2)}) copy-start(bf16[6144,1]{0,1:T(2,128)(2,1)} %param.11) | copy-start | bytes 36868
  175.4 55.3 %copy-start.13 = (bf16[256,768]{1,0:T(8,128)(2,1)S(1)}, bf16[256,768]{1,0:T(8,128)(2,1)}, u32[]{:S(2)}) copy-start(bf16[256,768]{1,0:T(8,128)(2,1)} %copy-done.12) | copy-start | bytes 1179652
  188.6 18.5 %all-to-all-start.9 = ((bf16[8,32,128]{2,1,0:T(8,128)(2,1)}), bf16[8,32,128]{2,1,0:T(8,128)(2,1)S(1)}, u32[]{:S(2)}, u32[]{:S(2)}) async-start(bf16[8,32,128]{2,1,0:T(8,128)(2,1)} %sum.1), calls=%async_computation.9 | async-start | bytes 131072 | tf_op jit(solution)/shard_map/all_to_all | solution.py:435
  208.0 22.6 %all-to-all-start.10 = ((bf16[8,32,128]{2,1,0:T(8,128)(2,1)}), bf16[8,32,128]{2,1,0:T(8,128)(2,1)S(1)}, u32[]{:S(2)}, u32[]{:S(2)}) async-start(bf16[8,32,128]{2,1,0:T(8,128)(2,1)} %weigh.1), calls=%async_computation.10 | async-start | bytes 131072 | tf_op jit(solution)/shard_map/all_to_all | solution.py:446

commit v10 on v8

--- a/solution.py
+++ b/solution.py
@@ -144,7 +144,9 @@
             picks[pl.ds(i * 6 + tile, 8, stride=SLOTS), :] = picked[
                 i * 8 : i * 8 + 8, tile * LANES : (tile + 1) * LANES
             ]
-    pay_ref[...] = picks[...].reshape(8, SLOTS, LANES).astype(BF16)
+    pay = picks[...].reshape(8, SLOTS, LANES).astype(BF16)
+    for y in range(4):
+        pay_ref[y * 8 : y * 8 + 8] = pay
 
 
 def cut_up_kernel(w_ref, out_ref, sems):
@@ -284,6 +286,10 @@
     return jax.ShapeDtypeStruct(dims, dtype)
 
 
+def in_hbm(array):
+    return array if INTERPRET else pltpu.with_memory_space_constraint(array, HBM)
+
+
 def body(queries, keys, values, selections, router, w_up, w_down):
     length, width = queries.shape
     parts = lax.axis_size("p")
@@ -302,8 +308,8 @@
     state = call(
         state_kernel,
         shape((4, 144, LANES)),
-        keys,
-        values,
+        in_hbm(keys),
+        in_hbm(values),
         scratch=[pltpu.VMEM((width, width), F32), pltpu.VMEM((4, 144, LANES), F32)],
         name="state",
     )
@@ -317,7 +323,14 @@
         name="total",
     )
     totals = lax.all_to_all(totals, ("r", "l"), 0, 0, tiled=True)
-    inner = call(inner_kernel, shape((length, width), F32), queries, keys, values, name="inner")
+    inner = call(
+        inner_kernel,
+        shape((length, width), F32),
+        in_hbm(queries),
+        in_hbm(keys),
+        in_hbm(values),
+        name="inner",
+    )
     up_cut = call(
         cut_up_kernel,
         shape((4, units, quarter)),
@@ -332,7 +345,7 @@
     pair = lax.axis_index("l").astype(jnp.int32).reshape(1)
     down_keep, down_one, down_two = call(
         cut_down_kernel,
-        [shape((n, columns, group)) for n in (4, 2, 2)],
+        [HBM((n, columns, group), BF16) for n in (4, 2, 2)],
         pair,
         w_down[0],
         scratch=[pltpu.VMEM((8, columns, group), BF16), pltpu.SemaphoreType.DMA((8,))],
@@ -356,7 +369,7 @@
     before, down_one, down_two = lax.optimization_barrier((before, down_one, down_two))
     attn, pay = call(
         attn_kernel,
-        (shape((length, width)), shape((8, SLOTS, LANES))),
+        (pltpu.HBM((length, width), BF16), shape((32, SLOTS, LANES))),
         queries,
         inner,
         before,
@@ -371,7 +384,7 @@
     )
     pay, down_two = lax.optimization_barrier((pay, down_two))
     down_two = lax.ppermute(down_two, "l", [(0, 1), (1, 0)])
-    whole_rows = lax.all_to_all(jnp.tile(pay, (4, 1, 1)), ("y", "p"), 0, 0, tiled=True)
+    whole_rows = lax.all_to_all(pay, ("y", "p"), 0, 0, tiled=True)
     whole_rows, down_two = lax.optimization_barrier((whole_rows, down_two))
     near_rows = call(
         near_kernel,
@@ -399,9 +412,9 @@
         join_kernel,
         shape((4, 2, columns, group)),
         pair,
-        down_keep,
-        down_one,
-        down_two,
+        in_hbm(down_keep),
+        in_hbm(down_one),
+        in_hbm(down_two),
         scratch=[pltpu.SemaphoreType.DMA((8,))],
         spaces=([pltpu.SMEM] + [HBM] * 3, HBM),
         name="join",

time: 227 us -> 272 us (1.20)
  Pallas kernels: 16.6 us -> 72.1 us
  local copies, waits for them, and re-layouts: 12.2 us -> 2.45 us
    pallas_call x16, Pallas kernels: 16.6 us -> 72.1 us  [call(): pl.pallas_call(kernel, out_shape=out, scratch_shapes=list(scratch), compi...]
    unnamed x32 -> x18, local copies, waits for them, and re-layouts: 11.2 us -> 2.24 us
    all_to_all x1, waiting for transfers between devices: 2.95 us -> 0.01 us  [body(): sums = lax.all_to_all(partial.reshape(4, units, 384), 'y', 0, 0, tiled=True)]
  transfers between devices with their start and end apart: 11 -> 11, of which waited for: 7 -> 6; matrix products, arithmetic and copies ran while one was open for 0% -> 0% of each run, Pallas kernels for 3% -> 22%
where the time goes in v10:
time: 272 us; the launch traced here: 271 us
  starting transfers between devices  75.1 us (28%)
  blocking collectives  74.7 us (27%)
  Pallas kernels  72.1 us (27%)
  waiting for transfers between devices  46.5 us (17%)
    pallas_call x16, Pallas kernels, call(): pl.pallas_call(kernel, out_shape=out, scratch_shapes=list(scratch), compi...  72.1 us
    all_gather x1, blocking collectives, body(): arrived = lax.all_gather(near_rows, ('r', 'l'), axis=0, tiled=True)  28.3 us
    all_gather x1, blocking collectives, body(): act = lax.all_gather(act, 'r', axis=0, tiled=True)  25.8 us
    all_to_all x1, starting transfers between devices, body(): weighted = lax.all_to_all(weighted, 'p', 0, 0, tiled=True)  18.6 us
    all_to_all x1, starting transfers between devices, body(): totals = lax.all_to_all(totals, ('r', 'l'), 0, 0, tiled=True)  14.9 us
    all_to_all x1, waiting for transfers between devices, body(): back = lax.all_to_all(back, ('r', 'l'), 0, 0, tiled=True)  11.7 us
    all_to_all x1, starting transfers between devices, body(): whole_rows = lax.all_to_all(pay, ('y', 'p'), 0, 0, tiled=True)  11.5 us
    all_to_all x1, blocking collectives, body(): back = lax.all_to_all(out, 'y', 0, 0, tiled=True)  10.9 us
  transfers between devices with their start and end apart: 11, of which 6 were waited for; matrix products, arithmetic and copies ran while one was open for 0% of the time, Pallas kernels for 22%

profile of v10, /device:TPU:1, one launch (start us, length us, event | category | flops | bytes accessed | tf_op | source)
XLA Modules:
  0.0 271.3 jit_solution(7307218246810238697)
XLA Ops:
  0.0 1.7 state.1
  1.8 9.7 %all_to_all.55.in_ref = bf16[4,144,128]{2,1,0:T(8,128)(2,1)S(1)} all-to-all(bf16[4,144,128]{2,1,0:T(8,128)(2,1)S(1)} %state.1), channel_id=1, replica_groups=mesh['r'=8,'l'=2,'y'=4,'p'=8] {'y'}, dimensions={0} | all-to-all | bytes 294912 | tf_op jit(solution)/shard_map/all_to_all | solution.py:316
  11.5 0.7 total.1
  12.1 14.9 %all-to-all-start.1 = ((bf16[16,16,128]{2,1,0:T(8,128)(2,1)}), bf16[16,16,128]{2,1,0:T(8,128)(2,1)S(1)}, u32[]{:S(2)}, u32[]{:S(2)}) async-start(bf16[16,16,128]{2,1,0:T(8,128)(2,1)} %total.1), calls=%async_computation.1 | async-start | bytes 131072 | tf_op jit(solution)/shard_map/all_to_all | solution.py:325
  27.1 2.2 inner.1.inner_ref
  29.2 0.0 copy-start.2
  29.3 1.3 cut_up.1
  30.5 0.0 copy-start.7
  30.6 8.2 %all-to-all-done.1.in_ref = bf16[16,16,128]{2,1,0:T(8,128)(2,1)S(1)} async-done(((bf16[16,16,128]{2,1,0:T(8,128)(2,1)}), bf16[16,16,128]{2,1,0:T(8,128)(2,1)S(1)}, u32[]{:S(2)}, u32[]{:S(2)}) %all-to-all-start.1) | async-done | bytes 65568 | tf_op jit(solution)/shard_map/all_to_all | solution.py:325
  38.7 0.6 prefix.1
  39.4 3.5 %all-to-all-start.2 = ((bf16[16,16,128]{2,1,0:T(8,128)(2,1)}), bf16[16,16,128]{2,1,0:T(8,128)(2,1)S(1)}, u32[]{:S(2)}, u32[]{:S(2)}) async-start(bf16[16,16,128]{2,1,0:T(8,128)(2,1)} %prefix.1), calls=%async_computation.2 | async-start | bytes 131072 | tf_op jit(solution)/shard_map/all_to_all | solution.py:344
  42.9 0.0 copy-start.1
  42.9 1.5 copy-done.1
  44.4 2.0 cut_down.1
  46.4 8.0 %all-to-all-done.2.base_ref = bf16[16,16,128]{2,1,0:T(8,128)(2,1)S(1)} async-done(((bf16[16,16,128]{2,1,0:T(8,128)(2,1)}), bf16[16,16,128]{2,1,0:T(8,128)(2,1)S(1)}, u32[]{:S(2)}, u32[]{:S(2)}) %all-to-all-start.2) | async-done | bytes 65568 | tf_op jit(solution)/shard_map/all_to_all | solution.py:344
  54.5 0.7 spread.1
  55.2 2.4 collective-permute-start
  57.6 3.3 %all-to-all-start.3 = ((bf16[4,144,128]{2,1,0:T(8,128)(2,1)}), bf16[4,144,128]{2,1,0:T(8,128)(2,1)S(1)}, u32[]{:S(2)}, u32[]{:S(2)}) async-start(bf16[4,144,128]{2,1,0:T(8,128)(2,1)} %spread.1), calls=%async_computation.3 | async-start | bytes 294912 | tf_op jit(solution)/shard_map/all_to_all | solution.py:367
  61.0 0.1 broadcast_in_dim_reshape.4.sel_ref
  61.0 4.8 %all-to-all-done.3.p_ref = bf16[4,144,128]{2,1,0:T(8,128)(2,1)S(1)} async-done(((bf16[4,144,128]{2,1,0:T(8,128)(2,1)}), bf16[4,144,128]{2,1,0:T(8,128)(2,1)S(1)}, u32[]{:S(2)}, u32[]{:S(2)}) %all-to-all-start.3) | async-done | bytes 147488 | tf_op jit(solution)/shard_map/all_to_all | solution.py:367
  65.8 0.0 collective-permute-done.one_ref
  65.8 1.7 attn.1
  67.6 2.9 %collective-permute-start.1 = (bf16[2,96,1152]{2,1,0:T(8,128)(2,1)S(1)}, bf16[2,96,1152]{2,1,0:T(8,128)(2,1)S(1)}, u32[]{:S(2)}, u32[]{:S(2)}) collective-permute-start(bf16[2,96,1152]{2,1,0:T(8,128)(2,1)S(1)} %copy-done.8), channel_id=1, source_target_pairs={{0,32},{32,0},{1,33},{33,1},{2,34},{34,2},{3,35},{35,3},{4,36},{36... | collective-permute-start | bytes 1327112 | tf_op jit(solution)/shard_map/ppermute | solution.py:386
  70.4 11.5 %all-to-all-start.4 = ((bf16[32,32,128]{2,1,0:T(8,128)(2,1)}), bf16[32,32,128]{2,1,0:T(8,128)(2,1)S(1)}, u32[]{:S(2)}, u32[]{:S(2)}) async-start(bf16[32,32,128]{2,1,0:T(8,128)(2,1)} %get-tuple-element.58), calls=%async_computation.4 | async-start | bytes 524288 | tf_op jit(solution)/shard_map/all_to_all | solution.py:387
  81.9 8.9 %all-to-all-done.4.row_ref = bf16[32,32,128]{2,1,0:T(8,128)(2,1)S(1)} async-done(((bf16[32,32,128]{2,1,0:T(8,128)(2,1)}), bf16[32,32,128]{2,1,0:T(8,128)(2,1)S(1)}, u32[]{:S(2)}, u32[]{:S(2)}) %all-to-all-start.4) | async-done | bytes 262176 | tf_op jit(solution)/shard_map/all_to_all | solution.py:387
  90.8 0.0 collective-permute-done.1.two_ref
  90.8 0.7 copy-done.5
  91.6 3.6 %all-to-all-start.5 = ((bf16[4,144,1536]{2,1,0:T(8,128)(2,1)}), bf16[4,144,1536]{2,1,0:T(8,128)(2,1)S(1)}, u32[]{:S(2)}, u32[]{:S(2)}) async-start(bf16[4,144,1536]{2,1,0:T(8,128)(2,1)} %cut_up.1), calls=%async_computation.5 | async-start | bytes 3538944 | tf_op jit(solution)/shard_map/all_to_all | solution.py:399
  95.2 28.3 %all_gather.6.x_ref = bf16[3840,128]{1,0:T(8,128)(2,1)S(1)} all-gather(bf16[240,128]{1,0:T(8,128)(2,1)S(1)} %near.1), channel_id=1, replica_groups=mesh['r'=8,'l'=2,'y'=4,'p'=8] {'r','l'}, dimensions={0}, use_global_device_ids=true | all-gather | bytes 1044480 | tf_op jit(solution)/shard_map/all_gather | solution.py:400
  123.4 2.1 up.1
  125.5 3.5 %all-to-all-start.6 = ((bf16[4,144,384]{2,1,0:T(8,128)(2,1)}), bf16[4,144,384]{2,1,0:T(8,128)(2,1)S(1)}, u32[]{:S(2)}, u32[]{:S(2)}) async-start(bf16[4,144,384]{2,1,0:T(8,128)(2,1)} %bitcast.8), calls=%async_computation.6 | async-start | bytes 884736 | tf_op jit(solution)/shard_map/all_to_all | solution.py:410
  129.0 54.8 %join.1 = bf16[4,2,96,1152]{3,2,1,0:T(8,128)(2,1)} custom-call(s32[1]{0:T(128)} %bitcast.1.place_ref, bf16[4,96,1152]{2,1,0:T(8,128)(2,1)} %get-tuple-element.66.keep_ref, bf16[2,96,1152]{2,1,0:T(8,128)(2,1)} %copy-done.4, bf16[2,96,1152]{2,1,0:T(8,128)(2,1)} %copy-done.5), custom_call_target="tpu_custom_call" | custom-call | tf_op jit(solution)/shard_map/join/pallas_call | solution.py:29
  183.8 0.1 act.1
  183.9 4.2 %all-to-all-start.7 = ((bf16[4,2,96,1152]{3,2,1,0:T(8,128)(2,1)}), bf16[4,2,96,1152]{3,2,1,0:T(8,128)(2,1)S(1)}, u32[]{:S(2)}, u32[]{:S(2)}) async-start(bf16[4,2,96,1152]{3,2,1,0:T(8,128)(2,1)} %join.1), calls=%async_computation.7 | async-start | bytes 3538944 | tf_op jit(solution)/shard_map/all_to_all | solution.py:425
  188.1 25.8 %all_gather.7.h_ref = bf16[1152,384]{1,0:T(8,128)(2,1)S(1)} all-gather(bf16[144,384]{1,0:T(8,128)(2,1)S(1)} %act.1), channel_id=1, replica_groups=mesh['r'=8,'l'=2,'y'=4,'p'=8] {'r'}, dimensions={0}, use_global_device_ids=true | all-gather | bytes 995328 | tf_op jit(solution)/shard_map/all_gather | solution.py:426
  213.9 1.5 down.1
  215.4 0.0 copy-start.6
  215.5 0.0 copy-start.3
  215.5 10.9 %all_to_all.56.in_ref = bf16[64,32,128]{2,1,0:T(8,128)(2,1)S(1)} all-to-all(bf16[64,32,128]{2,1,0:T(8,128)(2,1)S(1)} %down.1), channel_id=1, replica_groups=mesh['r'=8,'l'=2,'y'=4,'p'=8] {'y'}, dimensions={0} | all-to-all | bytes 1048576 | tf_op jit(solution)/shard_map/all_to_all | solution.py:438
  226.4 0.7 sum.1
  227.1 6.8 %all-to-all-start.9 = ((bf16[16,32,128]{2,1,0:T(8,128)(2,1)}), bf16[16,32,128]{2,1,0:T(8,128)(2,1)S(1)}, u32[]{:S(2)}, u32[]{:S(2)}) async-start(bf16[16,32,128]{2,1,0:T(8,128)(2,1)} %sum.1), calls=%async_computation.9 | async-start | bytes 262144 | tf_op jit(solution)/shard_map/all_to_all | solution.py:440
  233.9 0.1 reshape.24
  234.0 0.1 reduce
  234.1 11.7 %all-to-all-done.9.y_ref = bf16[16,32,128]{2,1,0:T(8,128)(2,1)S(1)} async-done(((bf16[16,32,128]{2,1,0:T(8,128)(2,1)}), bf16[16,32,128]{2,1,0:T(8,128)(2,1)S(1)}, u32[]{:S(2)}, u32[]{:S(2)}) %all-to-all-start.9) | async-done | bytes 131104 | tf_op jit(solution)/shard_map/all_to_all | solution.py:440
  245.8 0.9 weigh.1
  246.7 18.6 %all-to-all-start.10 = ((bf16[8,32,128]{2,1,0:T(8,128)(2,1)}), bf16[8,32,128]{2,1,0:T(8,128)(2,1)S(1)}, u32[]{:S(2)}, u32[]{:S(2)}) async-start(bf16[8,32,128]{2,1,0:T(8,128)(2,1)} %weigh.1), calls=%async_computation.10 | async-start | bytes 131072 | tf_op jit(solution)/shard_map/all_to_all | solution.py:451
  265.4 4.9 %all-to-all-done.10.y_ref = bf16[8,32,128]{2,1,0:T(8,128)(2,1)S(1)} async-done(((bf16[8,32,128]{2,1,0:T(8,128)(2,1)}), bf16[8,32,128]{2,1,0:T(8,128)(2,1)S(1)}, u32[]{:S(2)}, u32[]{:S(2)}) %all-to-all-start.10) | async-done | bytes 65568 | tf_op jit(solution)/shard_map/all_to_all | solution.py:451
  270.2 1.0 add.6
  (22 shorter events, 0.1 us)
Async XLA Ops:
  0.0 29.2 %copy-start = (bf16[1,144,6144]{2,1,0:T(8,128)(2,1)S(1)}, bf16[1,144,6144]{2,1,0:T(8,128)(2,1)}, u32[]{:S(2)}) copy-start(bf16[1,144,6144]{2,1,0:T(8,128)(2,1)} %param.12) | copy-start | bytes 5308420
  12.1 26.6 %all-to-all-start.1 = ((bf16[16,16,128]{2,1,0:T(8,128)(2,1)}), bf16[16,16,128]{2,1,0:T(8,128)(2,1)S(1)}, u32[]{:S(2)}, u32[]{:S(2)}) async-start(bf16[16,16,128]{2,1,0:T(8,128)(2,1)} %total.1), calls=%async_computation.1 | async-start | bytes 131072 | tf_op jit(solution)/shard_map/all_to_all | solution.py:325
  29.2 36.6 %copy-start.2 = (bf16[256,768]{1,0:T(8,128)(2,1)S(1)}, bf16[256,768]{1,0:T(8,128)(2,1)}, u32[]{:S(2)}) copy-start(bf16[256,768]{1,0:T(8,128)(2,1)} %q_ref.1) | copy-start | bytes 1179652
  30.5 30.4 %copy-start.7 = (s32[1,8,5]{1,0,2:T(1,128)S(1)}, s32[1,8,5]{1,0,2:T(1,128)}, u32[]{:S(2)}) copy-start(s32[1,8,5]{1,0,2:T(1,128)} %param.10) | copy-start | bytes 484
  39.4 15.1 %all-to-all-start.2 = ((bf16[16,16,128]{2,1,0:T(8,128)(2,1)}), bf16[16,16,128]{2,1,0:T(8,128)(2,1)S(1)}, u32[]{:S(2)}, u32[]{:S(2)}) async-start(bf16[16,16,128]{2,1,0:T(8,128)(2,1)} %prefix.1), calls=%async_computation.2 | async-start | bytes 131072 | tf_op jit(solution)/shard_map/all_to_all | solution.py:344
  42.9 1.5 copy-start.1
  46.4 21.2 %copy-start.8 = (bf16[2,96,1152]{2,1,0:T(8,128)(2,1)S(1)}, bf16[2,96,1152]{2,1,0:T(8,128)(2,1)}, u32[]{:S(2)}) copy-start(bf16[2,96,1152]{2,1,0:T(8,128)(2,1)} %get-tuple-element.59) | copy-start | bytes 1327108
  55.2 10.6 %collective-permute-start = (bf16[2,96,1152]{2,1,0:T(8,128)(2,1)}, bf16[2,96,1152]{2,1,0:T(8,128)(2,1)S(1)}, u32[]{:S(2)}, u32[]{:S(2)}) collective-permute-start(bf16[2,96,1152]{2,1,0:T(8,128)(2,1)} %get-tuple-element.52), channel_id=1, source_target_pairs={{0,32},{32,0},{1,33},{33,1},{2,34},{34,2},{3,35},{35,3},{4,36},{36... | collective-permute-start | bytes 1327112 | tf_op jit(solution)/shard_map/ppermute | solution.py:368
  57.6 8.2 %all-to-all-start.3 = ((bf16[4,144,128]{2,1,0:T(8,128)(2,1)}), bf16[4,144,128]{2,1,0:T(8,128)(2,1)S(1)}, u32[]{:S(2)}, u32[]{:S(2)}) async-start(bf16[4,144,128]{2,1,0:T(8,128)(2,1)} %spread.1), calls=%async_computation.3 | async-start | bytes 294912 | tf_op jit(solution)/shard_map/all_to_all | solution.py:367
  65.8 25.7 %copy-start.4 = (bf16[2,96,1152]{2,1,0:T(8,128)(2,1)}, bf16[2,96,1152]{2,1,0:T(8,128)(2,1)S(1)}, u32[]{:S(2)}) copy-start(bf16[2,96,1152]{2,1,0:T(8,128)(2,1)S(1)} %collective-permute-done.one_ref) | copy-start | bytes 1327108
  67.6 23.2 %collective-permute-start.1 = (bf16[2,96,1152]{2,1,0:T(8,128)(2,1)S(1)}, bf16[2,96,1152]{2,1,0:T(8,128)(2,1)S(1)}, u32[]{:S(2)}, u32[]{:S(2)}) collective-permute-start(bf16[2,96,1152]{2,1,0:T(8,128)(2,1)S(1)} %copy-done.8), channel_id=1, source_target_pairs={{0,32},{32,0},{1,33},{33,1},{2,34},{34,2},{3,35},{35,3},{4,36},{36... | collective-permute-start | bytes 1327112 | tf_op jit(solution)/shard_map/ppermute | solution.py:386
  70.4 20.4 %all-to-all-start.4 = ((bf16[32,32,128]{2,1,0:T(8,128)(2,1)}), bf16[32,32,128]{2,1,0:T(8,128)(2,1)S(1)}, u32[]{:S(2)}, u32[]{:S(2)}) async-start(bf16[32,32,128]{2,1,0:T(8,128)(2,1)} %get-tuple-element.58), calls=%async_computation.4 | async-start | bytes 524288 | tf_op jit(solution)/shard_map/all_to_all | solution.py:387
  90.8 0.8 copy-start.5
  91.6 31.8 %all-to-all-start.5 = ((bf16[4,144,1536]{2,1,0:T(8,128)(2,1)}), bf16[4,144,1536]{2,1,0:T(8,128)(2,1)S(1)}, u32[]{:S(2)}, u32[]{:S(2)}) async-start(bf16[4,144,1536]{2,1,0:T(8,128)(2,1)} %cut_up.1), calls=%async_computation.5 | async-start | bytes 3538944 | tf_op jit(solution)/shard_map/all_to_all | solution.py:399
  125.5 58.3 %all-to-all-start.6 = ((bf16[4,144,384]{2,1,0:T(8,128)(2,1)}), bf16[4,144,384]{2,1,0:T(8,128)(2,1)S(1)}, u32[]{:S(2)}, u32[]{:S(2)}) async-start(bf16[4,144,384]{2,1,0:T(8,128)(2,1)} %bitcast.8), calls=%async_computation.6 | async-start | bytes 884736 | tf_op jit(solution)/shard_map/all_to_all | solution.py:410
  183.9 30.0 %all-to-all-start.7 = ((bf16[4,2,96,1152]{3,2,1,0:T(8,128)(2,1)}), bf16[4,2,96,1152]{3,2,1,0:T(8,128)(2,1)S(1)}, u32[]{:S(2)}, u32[]{:S(2)}) async-start(bf16[4,2,96,1152]{3,2,1,0:T(8,128)(2,1)} %join.1), calls=%async_computation.7 | async-start | bytes 3538944 | tf_op jit(solution)/shard_map/all_to_all | solution.py:425
  215.4 18.5 %copy-start.6 = (bf16[6144,1]{0,1:T(2,128)(2,1)S(1)}, bf16[6144,1]{0,1:T(2,128)(2,1)}, u32[]{:S(2)}) copy-start(bf16[6144,1]{0,1:T(2,128)(2,1)} %param.11) | copy-start | bytes 36868
  215.5 54.8 %copy-start.3 = (bf16[256,768]{1,0:T(8,128)(2,1)S(1)}, bf16[256,768]{1,0:T(8,128)(2,1)}, u32[]{:S(2)}) copy-start(bf16[256,768]{1,0:T(8,128)(2,1)} %get-tuple-element.55.attn_ref) | copy-start | bytes 1179652
  227.1 18.7 %all-to-all-start.9 = ((bf16[16,32,128]{2,1,0:T(8,128)(2,1)}), bf16[16,32,128]{2,1,0:T(8,128)(2,1)S(1)}, u32[]{:S(2)}, u32[]{:S(2)}) async-start(bf16[16,32,128]{2,1,0:T(8,128)(2,1)} %sum.1), calls=%async_computation.9 | async-start | bytes 262144 | tf_op jit(solution)/shard_map/all_to_all | solution.py:440
  246.7 23.5 %all-to-all-start.10 = ((bf16[8,32,128]{2,1,0:T(8,128)(2,1)}), bf16[8,32,128]{2,1,0:T(8,128)(2,1)S(1)}, u32[]{:S(2)}, u32[]{:S(2)}) async-start(bf16[8,32,128]{2,1,0:T(8,128)(2,1)} %weigh.1), calls=%async_computation.10 | async-start | bytes 131072 | tf_op jit(solution)/shard_map/all_to_all | solution.py:451

commit v11 on v10

--- a/solution.py
+++ b/solution.py
@@ -179,17 +179,11 @@
         copy.wait()
 
 
-def join_kernel(place_ref, keep_ref, one_ref, two_ref, out_ref, sems):
+def join_kernel(place_ref, keep_ref, one_ref, two_ref, out_ref):
     own = place_ref[0]
-    copies = []
     for n in range(4):
-        away = (one_ref, two_ref)[n // 2].at[n % 2]
-        copies.append(pltpu.make_async_copy(keep_ref.at[n], out_ref.at[n, own], sems.at[n]))
-        copies.append(pltpu.make_async_copy(away, out_ref.at[n, 1 - own], sems.at[4 + n]))
-    for copy in copies:
-        copy.start()
-    for copy in copies:
-        copy.wait()
+        out_ref[n, own] = keep_ref[n]
+        out_ref[n, 1 - own] = (one_ref, two_ref)[n // 2][n % 2]
 
 
 def near_kernel(place_ref, row_ref, out_ref, rows):
@@ -412,11 +406,10 @@
         join_kernel,
         shape((4, 2, columns, group)),
         pair,
-        in_hbm(down_keep),
-        in_hbm(down_one),
-        in_hbm(down_two),
-        scratch=[pltpu.SemaphoreType.DMA((8,))],
-        spaces=([pltpu.SMEM] + [HBM] * 3, HBM),
+        down_keep,
+        down_one,
+        down_two,
+        spaces=([pltpu.SMEM] + [pltpu.VMEM] * 3, pltpu.VMEM),
         name="join",
     )
     sums, down_cut = lax.optimization_barrier((sums, down_cut))

time: 272 us -> 224 us (0.82)
  Pallas kernels: 72.1 us -> 18.7 us
  waiting for transfers between devices: 46.5 us -> 49.4 us
    pallas_call x16, Pallas kernels: 72.1 us -> 18.7 us  [call(): pl.pallas_call(kernel, out_shape=out, scratch_shapes=list(scratch), compi...]
    all_to_all x1, waiting for transfers between devices: 0.01 us -> 2.91 us  [body(): sums = lax.all_to_all(partial.reshape(4, units, 384), 'y', 0, 0, tiled=True)]
  transfers between devices with their start and end apart: 11 -> 11, of which waited for: 6 -> 7; matrix products, arithmetic and copies ran while one was open for 0% -> 0% of each run, Pallas kernels for 22% -> 3%
where the time goes in v11:
time: 224 us; the launch traced here: 223 us
  blocking collectives  75.9 us (34%)
  starting transfers between devices  73.6 us (33%)
  waiting for transfers between devices  49.4 us (22%)
  Pallas kernels  18.7 us (8%)
  local copies, waits for them, and re-layouts  4.64 us (2%)
    all_gather x1, blocking collectives, body(): arrived = lax.all_gather(near_rows, ('r', 'l'), axis=0, tiled=True)  28.3 us
    all_gather x1, blocking collectives, body(): act = lax.all_gather(act, 'r', axis=0, tiled=True)  26.5 us
    all_to_all x1, starting transfers between devices, body(): weighted = lax.all_to_all(weighted, 'p', 0, 0, tiled=True)  19.5 us
    pallas_call x16, Pallas kernels, call(): pl.pallas_call(kernel, out_shape=out, scratch_shapes=list(scratch), compi...  18.7 us
    all_to_all x1, starting transfers between devices, body(): totals = lax.all_to_all(totals, ('r', 'l'), 0, 0, tiled=True)  14.9 us
    all_to_all x1, waiting for transfers between devices, body(): back = lax.all_to_all(back, ('r', 'l'), 0, 0, tiled=True)  11.7 us
    all_to_all x1, starting transfers between devices, body(): whole_rows = lax.all_to_all(pay, ('y', 'p'), 0, 0, tiled=True)  11.4 us
    all_to_all x1, blocking collectives, body(): back = lax.all_to_all(out, 'y', 0, 0, tiled=True)  11.4 us
  transfers between devices with their start and end apart: 11, of which 7 were waited for; matrix products, arithmetic and copies ran while one was open for 0% of the time, Pallas kernels for 3%

profile of v11, /device:TPU:1, one launch (start us, length us, event | category | flops | bytes accessed | tf_op | source)
XLA Modules:
  0.0 222.6 jit_solution(17306001345926614275)
XLA Ops:
  0.0 1.7 state.1
  1.8 9.7 %all_to_all.55.in_ref = bf16[4,144,128]{2,1,0:T(8,128)(2,1)S(1)} all-to-all(bf16[4,144,128]{2,1,0:T(8,128)(2,1)S(1)} %state.1), channel_id=1, replica_groups=mesh['r'=8,'l'=2,'y'=4,'p'=8] {'y'}, dimensions={0} | all-to-all | bytes 294912 | tf_op jit(solution)/shard_map/all_to_all | solution.py:310
  11.5 0.7 total.1
  12.1 14.9 %all-to-all-start.1 = ((bf16[16,16,128]{2,1,0:T(8,128)(2,1)}), bf16[16,16,128]{2,1,0:T(8,128)(2,1)S(1)}, u32[]{:S(2)}, u32[]{:S(2)}) async-start(bf16[16,16,128]{2,1,0:T(8,128)(2,1)} %total.1), calls=%async_computation.1 | async-start | bytes 131072 | tf_op jit(solution)/shard_map/all_to_all | solution.py:319
  27.1 2.2 inner.1.inner_ref
  29.2 0.0 copy-start.2
  29.3 1.3 cut_up.1
  30.6 8.2 %all-to-all-done.1.in_ref = bf16[16,16,128]{2,1,0:T(8,128)(2,1)S(1)} async-done(((bf16[16,16,128]{2,1,0:T(8,128)(2,1)}), bf16[16,16,128]{2,1,0:T(8,128)(2,1)S(1)}, u32[]{:S(2)}, u32[]{:S(2)}) %all-to-all-start.1) | async-done | bytes 65568 | tf_op jit(solution)/shard_map/all_to_all | solution.py:319
  38.7 0.6 prefix.1
  39.4 3.5 %all-to-all-start.2 = ((bf16[16,16,128]{2,1,0:T(8,128)(2,1)}), bf16[16,16,128]{2,1,0:T(8,128)(2,1)S(1)}, u32[]{:S(2)}, u32[]{:S(2)}) async-start(bf16[16,16,128]{2,1,0:T(8,128)(2,1)} %prefix.1), calls=%async_computation.2 | async-start | bytes 131072 | tf_op jit(solution)/shard_map/all_to_all | solution.py:338
  42.9 0.0 copy-start.1
  42.9 1.5 copy-done.1
  44.4 2.0 cut_down.1
  46.4 8.1 %all-to-all-done.2.base_ref = bf16[16,16,128]{2,1,0:T(8,128)(2,1)S(1)} async-done(((bf16[16,16,128]{2,1,0:T(8,128)(2,1)}), bf16[16,16,128]{2,1,0:T(8,128)(2,1)S(1)}, u32[]{:S(2)}, u32[]{:S(2)}) %all-to-all-start.2) | async-done | bytes 65568 | tf_op jit(solution)/shard_map/all_to_all | solution.py:338
  54.5 0.7 spread.1
  55.2 2.4 %collective-permute-start = (bf16[2,96,1152]{2,1,0:T(8,128)(2,1)}, bf16[2,96,1152]{2,1,0:T(8,128)(2,1)S(1)}, u32[]{:S(2)}, u32[]{:S(2)}) collective-permute-start(bf16[2,96,1152]{2,1,0:T(8,128)(2,1)} %get-tuple-element.52), channel_id=1, source_target_pairs={{0,32},{32,0},{1,33},{33,1},{2,34},{34,2},{3,35},{35,3},{4,36},{36... | collective-permute-start | bytes 1327112 | tf_op jit(solution)/shard_map/ppermute | solution.py:362
  57.6 3.3 %all-to-all-start.3 = ((bf16[4,144,128]{2,1,0:T(8,128)(2,1)}), bf16[4,144,128]{2,1,0:T(8,128)(2,1)S(1)}, u32[]{:S(2)}, u32[]{:S(2)}) async-start(bf16[4,144,128]{2,1,0:T(8,128)(2,1)} %spread.1), calls=%async_computation.3 | async-start | bytes 294912 | tf_op jit(solution)/shard_map/all_to_all | solution.py:361
  61.0 0.1 broadcast_in_dim_reshape.4.sel_ref
  61.0 4.8 %all-to-all-done.3.p_ref = bf16[4,144,128]{2,1,0:T(8,128)(2,1)S(1)} async-done(((bf16[4,144,128]{2,1,0:T(8,128)(2,1)}), bf16[4,144,128]{2,1,0:T(8,128)(2,1)S(1)}, u32[]{:S(2)}, u32[]{:S(2)}) %all-to-all-start.3) | async-done | bytes 147488 | tf_op jit(solution)/shard_map/all_to_all | solution.py:361
  65.8 1.8 attn.1
  67.6 2.9 %collective-permute-start.1 = (bf16[2,96,1152]{2,1,0:T(8,128)(2,1)S(1)}, bf16[2,96,1152]{2,1,0:T(8,128)(2,1)S(1)}, u32[]{:S(2)}, u32[]{:S(2)}) collective-permute-start(bf16[2,96,1152]{2,1,0:T(8,128)(2,1)S(1)} %copy-done.9), channel_id=1, source_target_pairs={{0,32},{32,0},{1,33},{33,1},{2,34},{34,2},{3,35},{35,3},{4,36},{36... | collective-permute-start | bytes 1327112 | tf_op jit(solution)/shard_map/ppermute | solution.py:380
  70.4 11.4 %all-to-all-start.4 = ((bf16[32,32,128]{2,1,0:T(8,128)(2,1)}), bf16[32,32,128]{2,1,0:T(8,128)(2,1)S(1)}, u32[]{:S(2)}, u32[]{:S(2)}) async-start(bf16[32,32,128]{2,1,0:T(8,128)(2,1)} %get-tuple-element.58), calls=%async_computation.4 | async-start | bytes 524288 | tf_op jit(solution)/shard_map/all_to_all | solution.py:381
  81.9 8.9 %all-to-all-done.4.row_ref = bf16[32,32,128]{2,1,0:T(8,128)(2,1)S(1)} async-done(((bf16[32,32,128]{2,1,0:T(8,128)(2,1)}), bf16[32,32,128]{2,1,0:T(8,128)(2,1)S(1)}, u32[]{:S(2)}, u32[]{:S(2)}) %all-to-all-start.4) | async-done | bytes 262176 | tf_op jit(solution)/shard_map/all_to_all | solution.py:381
  90.8 0.7 copy-done.4
  91.6 3.6 %all-to-all-start.5 = ((bf16[4,144,1536]{2,1,0:T(8,128)(2,1)}), bf16[4,144,1536]{2,1,0:T(8,128)(2,1)S(1)}, u32[]{:S(2)}, u32[]{:S(2)}) async-start(bf16[4,144,1536]{2,1,0:T(8,128)(2,1)} %cut_up.1), calls=%async_computation.5 | async-start | bytes 3538944 | tf_op jit(solution)/shard_map/all_to_all | solution.py:393
  95.2 28.3 %all_gather.6.x_ref = bf16[3840,128]{1,0:T(8,128)(2,1)S(1)} all-gather(bf16[240,128]{1,0:T(8,128)(2,1)S(1)} %near.1), channel_id=1, replica_groups=mesh['r'=8,'l'=2,'y'=4,'p'=8] {'r','l'}, dimensions={0}, use_global_device_ids=true | all-gather | bytes 1044480 | tf_op jit(solution)/shard_map/all_gather | solution.py:394
  123.4 2.1 up.1
  125.5 3.5 %all-to-all-start.6 = ((bf16[4,144,384]{2,1,0:T(8,128)(2,1)}), bf16[4,144,384]{2,1,0:T(8,128)(2,1)S(1)}, u32[]{:S(2)}, u32[]{:S(2)}) async-start(bf16[4,144,384]{2,1,0:T(8,128)(2,1)} %bitcast.8), calls=%async_computation.6 | async-start | bytes 884736 | tf_op jit(solution)/shard_map/all_to_all | solution.py:404
  129.0 1.2 copy-done.3
  130.1 1.0 copy-done.5
  131.2 1.4 join.1
  132.5 2.9 %all-to-all-done.6.in_ref = bf16[4,144,384]{2,1,0:T(8,128)(2,1)S(1)} async-done(((bf16[4,144,384]{2,1,0:T(8,128)(2,1)}), bf16[4,144,384]{2,1,0:T(8,128)(2,1)S(1)}, u32[]{:S(2)}, u32[]{:S(2)}) %all-to-all-start.6) | async-done | bytes 442400 | tf_op jit(solution)/shard_map/all_to_all | solution.py:404
  135.4 0.1 act.1
  135.5 3.6 %all-to-all-start.7 = ((bf16[4,2,96,1152]{3,2,1,0:T(8,128)(2,1)}), bf16[4,2,96,1152]{3,2,1,0:T(8,128)(2,1)S(1)}, u32[]{:S(2)}, u32[]{:S(2)}) async-start(bf16[4,2,96,1152]{3,2,1,0:T(8,128)(2,1)} %join.1), calls=%async_computation.7 | async-start | bytes 3538944 | tf_op jit(solution)/shard_map/all_to_all | solution.py:418
  139.1 26.5 %all_gather.7.h_ref = bf16[1152,384]{1,0:T(8,128)(2,1)S(1)} all-gather(bf16[144,384]{1,0:T(8,128)(2,1)S(1)} %act.1), channel_id=1, replica_groups=mesh['r'=8,'l'=2,'y'=4,'p'=8] {'r'}, dimensions={0}, use_global_device_ids=true | all-gather | bytes 995328 | tf_op jit(solution)/shard_map/all_gather | solution.py:419
  165.7 1.5 down.1
  167.2 0.0 copy-start.7
  167.2 0.0 copy-start.6
  167.2 11.4 %all_to_all.56.in_ref = bf16[64,32,128]{2,1,0:T(8,128)(2,1)S(1)} all-to-all(bf16[64,32,128]{2,1,0:T(8,128)(2,1)S(1)} %down.1), channel_id=1, replica_groups=mesh['r'=8,'l'=2,'y'=4,'p'=8] {'y'}, dimensions={0} | all-to-all | bytes 1048576 | tf_op jit(solution)/shard_map/all_to_all | solution.py:431
  178.6 0.7 sum.1
  179.3 5.0 %all-to-all-start.9 = ((bf16[16,32,128]{2,1,0:T(8,128)(2,1)}), bf16[16,32,128]{2,1,0:T(8,128)(2,1)S(1)}, u32[]{:S(2)}, u32[]{:S(2)}) async-start(bf16[16,32,128]{2,1,0:T(8,128)(2,1)} %sum.1), calls=%async_computation.9 | async-start | bytes 262144 | tf_op jit(solution)/shard_map/all_to_all | solution.py:433
  184.4 0.1 reshape.24
  184.4 0.1 reduce
  184.6 11.7 %all-to-all-done.9.y_ref = bf16[16,32,128]{2,1,0:T(8,128)(2,1)S(1)} async-done(((bf16[16,32,128]{2,1,0:T(8,128)(2,1)}), bf16[16,32,128]{2,1,0:T(8,128)(2,1)S(1)}, u32[]{:S(2)}, u32[]{:S(2)}) %all-to-all-start.9) | async-done | bytes 131104 | tf_op jit(solution)/shard_map/all_to_all | solution.py:433
  196.3 0.9 weigh.1
  197.2 19.5 %all-to-all-start.10 = ((bf16[8,32,128]{2,1,0:T(8,128)(2,1)}), bf16[8,32,128]{2,1,0:T(8,128)(2,1)S(1)}, u32[]{:S(2)}, u32[]{:S(2)}) async-start(bf16[8,32,128]{2,1,0:T(8,128)(2,1)} %weigh.1), calls=%async_computation.10 | async-start | bytes 131072 | tf_op jit(solution)/shard_map/all_to_all | solution.py:444
  216.7 4.9 %all-to-all-done.10.y_ref = bf16[8,32,128]{2,1,0:T(8,128)(2,1)S(1)} async-done(((bf16[8,32,128]{2,1,0:T(8,128)(2,1)}), bf16[8,32,128]{2,1,0:T(8,128)(2,1)S(1)}, u32[]{:S(2)}, u32[]{:S(2)}) %all-to-all-start.10) | async-done | bytes 65568 | tf_op jit(solution)/shard_map/all_to_all | solution.py:444
  221.5 1.0 add.6
  (24 shorter events, 0.1 us)
Async XLA Ops:
  0.0 29.2 %copy-start = (bf16[1,144,6144]{2,1,0:T(8,128)(2,1)S(1)}, bf16[1,144,6144]{2,1,0:T(8,128)(2,1)}, u32[]{:S(2)}) copy-start(bf16[1,144,6144]{2,1,0:T(8,128)(2,1)} %param.12) | copy-start | bytes 5308420
  12.1 26.6 %all-to-all-start.1 = ((bf16[16,16,128]{2,1,0:T(8,128)(2,1)}), bf16[16,16,128]{2,1,0:T(8,128)(2,1)S(1)}, u32[]{:S(2)}, u32[]{:S(2)}) async-start(bf16[16,16,128]{2,1,0:T(8,128)(2,1)} %total.1), calls=%async_computation.1 | async-start | bytes 131072 | tf_op jit(solution)/shard_map/all_to_all | solution.py:319
  29.2 36.6 %copy-start.2 = (bf16[256,768]{1,0:T(8,128)(2,1)S(1)}, bf16[256,768]{1,0:T(8,128)(2,1)}, u32[]{:S(2)}) copy-start(bf16[256,768]{1,0:T(8,128)(2,1)} %q_ref.1) | copy-start | bytes 1179652
  30.5 30.4 %copy-start.8 = (s32[1,8,5]{1,0,2:T(1,128)S(1)}, s32[1,8,5]{1,0,2:T(1,128)}, u32[]{:S(2)}) copy-start(s32[1,8,5]{1,0,2:T(1,128)} %param.10) | copy-start | bytes 484
  39.4 15.1 %all-to-all-start.2 = ((bf16[16,16,128]{2,1,0:T(8,128)(2,1)}), bf16[16,16,128]{2,1,0:T(8,128)(2,1)S(1)}, u32[]{:S(2)}, u32[]{:S(2)}) async-start(bf16[16,16,128]{2,1,0:T(8,128)(2,1)} %prefix.1), calls=%async_computation.2 | async-start | bytes 131072 | tf_op jit(solution)/shard_map/all_to_all | solution.py:338
  42.9 1.5 copy-start.1
  46.4 21.2 %copy-start.9 = (bf16[2,96,1152]{2,1,0:T(8,128)(2,1)S(1)}, bf16[2,96,1152]{2,1,0:T(8,128)(2,1)}, u32[]{:S(2)}) copy-start(bf16[2,96,1152]{2,1,0:T(8,128)(2,1)} %get-tuple-element.59) | copy-start | bytes 1327108
  55.2 10.6 %collective-permute-start = (bf16[2,96,1152]{2,1,0:T(8,128)(2,1)}, bf16[2,96,1152]{2,1,0:T(8,128)(2,1)S(1)}, u32[]{:S(2)}, u32[]{:S(2)}) collective-permute-start(bf16[2,96,1152]{2,1,0:T(8,128)(2,1)} %get-tuple-element.52), channel_id=1, source_target_pairs={{0,32},{32,0},{1,33},{33,1},{2,34},{34,2},{3,35},{35,3},{4,36},{36... | collective-permute-start | bytes 1327112 | tf_op jit(solution)/shard_map/ppermute | solution.py:362
  57.6 8.2 %all-to-all-start.3 = ((bf16[4,144,128]{2,1,0:T(8,128)(2,1)}), bf16[4,144,128]{2,1,0:T(8,128)(2,1)S(1)}, u32[]{:S(2)}, u32[]{:S(2)}) async-start(bf16[4,144,128]{2,1,0:T(8,128)(2,1)} %spread.1), calls=%async_computation.3 | async-start | bytes 294912 | tf_op jit(solution)/shard_map/all_to_all | solution.py:361
  67.6 23.2 %collective-permute-start.1 = (bf16[2,96,1152]{2,1,0:T(8,128)(2,1)S(1)}, bf16[2,96,1152]{2,1,0:T(8,128)(2,1)S(1)}, u32[]{:S(2)}, u32[]{:S(2)}) collective-permute-start(bf16[2,96,1152]{2,1,0:T(8,128)(2,1)S(1)} %copy-done.9), channel_id=1, source_target_pairs={{0,32},{32,0},{1,33},{33,1},{2,34},{34,2},{3,35},{35,3},{4,36},{36... | collective-permute-start | bytes 1327112 | tf_op jit(solution)/shard_map/ppermute | solution.py:380
  70.4 20.4 %all-to-all-start.4 = ((bf16[32,32,128]{2,1,0:T(8,128)(2,1)}), bf16[32,32,128]{2,1,0:T(8,128)(2,1)S(1)}, u32[]{:S(2)}, u32[]{:S(2)}) async-start(bf16[32,32,128]{2,1,0:T(8,128)(2,1)} %get-tuple-element.58), calls=%async_computation.4 | async-start | bytes 524288 | tf_op jit(solution)/shard_map/all_to_all | solution.py:381
  90.8 0.7 copy-start.4
  91.6 31.9 %all-to-all-start.5 = ((bf16[4,144,1536]{2,1,0:T(8,128)(2,1)}), bf16[4,144,1536]{2,1,0:T(8,128)(2,1)S(1)}, u32[]{:S(2)}, u32[]{:S(2)}) async-start(bf16[4,144,1536]{2,1,0:T(8,128)(2,1)} %cut_up.1), calls=%async_computation.5 | async-start | bytes 3538944 | tf_op jit(solution)/shard_map/all_to_all | solution.py:393
  125.5 9.9 %all-to-all-start.6 = ((bf16[4,144,384]{2,1,0:T(8,128)(2,1)}), bf16[4,144,384]{2,1,0:T(8,128)(2,1)S(1)}, u32[]{:S(2)}, u32[]{:S(2)}) async-start(bf16[4,144,384]{2,1,0:T(8,128)(2,1)} %bitcast.8), calls=%async_computation.6 | async-start | bytes 884736 | tf_op jit(solution)/shard_map/all_to_all | solution.py:404
  129.0 1.2 copy-start.3
  130.1 1.0 copy-start.5
  135.5 30.1 %all-to-all-start.7 = ((bf16[4,2,96,1152]{3,2,1,0:T(8,128)(2,1)}), bf16[4,2,96,1152]{3,2,1,0:T(8,128)(2,1)S(1)}, u32[]{:S(2)}, u32[]{:S(2)}) async-start(bf16[4,2,96,1152]{3,2,1,0:T(8,128)(2,1)} %join.1), calls=%async_computation.7 | async-start | bytes 3538944 | tf_op jit(solution)/shard_map/all_to_all | solution.py:418
  167.2 17.2 %copy-start.7 = (bf16[6144,1]{0,1:T(2,128)(2,1)S(1)}, bf16[6144,1]{0,1:T(2,128)(2,1)}, u32[]{:S(2)}) copy-start(bf16[6144,1]{0,1:T(2,128)(2,1)} %param.11) | copy-start | bytes 36868
  167.2 54.3 %copy-start.6 = (bf16[256,768]{1,0:T(8,128)(2,1)S(1)}, bf16[256,768]{1,0:T(8,128)(2,1)}, u32[]{:S(2)}) copy-start(bf16[256,768]{1,0:T(8,128)(2,1)} %get-tuple-element.55.attn_ref) | copy-start | bytes 1179652
  179.3 17.0 %all-to-all-start.9 = ((bf16[16,32,128]{2,1,0:T(8,128)(2,1)}), bf16[16,32,128]{2,1,0:T(8,128)(2,1)S(1)}, u32[]{:S(2)}, u32[]{:S(2)}) async-start(bf16[16,32,128]{2,1,0:T(8,128)(2,1)} %sum.1), calls=%async_computation.9 | async-start | bytes 262144 | tf_op jit(solution)/shard_map/all_to_all | solution.py:433
  197.2 24.4 %all-to-all-start.10 = ((bf16[8,32,128]{2,1,0:T(8,128)(2,1)}), bf16[8,32,128]{2,1,0:T(8,128)(2,1)S(1)}, u32[]{:S(2)}, u32[]{:S(2)}) async-start(bf16[8,32,128]{2,1,0:T(8,128)(2,1)} %weigh.1), calls=%async_computation.10 | async-start | bytes 131072 | tf_op jit(solution)/shard_map/all_to_all | solution.py:444

commit v12 on v11

--- a/solution.py
+++ b/solution.py
@@ -63,27 +63,18 @@
     out_ref[...] = rows[...].astype(BF16)
 
 
-def total_kernel(in_ref, out_ref, rows):
+def total_kernel(in_ref, out_ref):
     total = in_ref[0].astype(F32)
     for y in range(1, 4):
         total = total + in_ref[y].astype(F32)
-    rows[0:144] = total
-    rows[144:152] = jnp.zeros((8, LANES), F32)
+    out_ref[...] = total.astype(BF16)
+
+
+def spread_kernel(place_ref, all_ref, in_ref, out_ref):
+    total = jnp.zeros((144, LANES), F32)
     for z in range(16):
-        out_ref[z] = rows[z * 9 : z * 9 + 16].astype(BF16)
-
-
-def prefix_kernel(in_ref, out_ref):
-    total = jnp.zeros((16, LANES), F32)
-    for z in range(16):
-        out_ref[z] = total.astype(BF16)
-        total = total + in_ref[z].astype(F32)
-
-
-def spread_kernel(base_ref, in_ref, out_ref, rows):
-    for z in range(16):
-        rows[z * 9 : z * 9 + 9] = base_ref[z].astype(F32)[0:9]
-    total = rows[...]
+        row = all_ref[z * 144 : z * 144 + 144].astype(F32)
+        total = total + jnp.where(z < place_ref[0], row, 0.0)
     for y in range(4):
         out_ref[y] = total.astype(BF16)
         total = total + in_ref[y].astype(F32)
@@ -307,35 +298,8 @@
         scratch=[pltpu.VMEM((width, width), F32), pltpu.VMEM((4, 144, LANES), F32)],
         name="state",
     )
+    w_down, state = lax.optimization_barrier((w_down, state))
     quarters = lax.all_to_all(state, "y", 0, 0, tiled=True)
-    quarters, queries, w_up, w_down = lax.optimization_barrier((quarters, queries, w_up, w_down))
-    totals = call(
-        total_kernel,
-        shape((16, 16, LANES)),
-        quarters,
-        scratch=[pltpu.VMEM((152, LANES), F32)],
-        name="total",
-    )
-    totals = lax.all_to_all(totals, ("r", "l"), 0, 0, tiled=True)
-    inner = call(
-        inner_kernel,
-        shape((length, width), F32),
-        in_hbm(queries),
-        in_hbm(keys),
-        in_hbm(values),
-        name="inner",
-    )
-    up_cut = call(
-        cut_up_kernel,
-        shape((4, units, quarter)),
-        w_up[0],
-        scratch=[pltpu.SemaphoreType.DMA((4,))],
-        spaces=([HBM], HBM),
-        name="cut_up",
-    )
-    totals, inner, up_cut, w_down = lax.optimization_barrier((totals, inner, up_cut, w_down))
-    bases = call(prefix_kernel, shape((16, 16, LANES)), totals, name="prefix")
-    bases = lax.all_to_all(bases, ("r", "l"), 0, 0, tiled=True)
     pair = lax.axis_index("l").astype(jnp.int32).reshape(1)
     down_keep, down_one, down_two = call(
         cut_down_kernel,
@@ -346,21 +310,43 @@
         spaces=([pltpu.SMEM, pltpu.VMEM], [HBM] * 3),
         name="cut_down",
     )
-    bases, down_keep, down_one, down_two = lax.optimization_barrier(
-        (bases, down_keep, down_one, down_two)
-    )
+    quarters, down_keep, down_one, down_two = lax.optimization_barrier(
+        (quarters, down_keep, down_one, down_two)
+    )
+    totals = call(total_kernel, shape((144, LANES)), quarters, name="total")
+    totals = lax.all_gather(totals, ("r", "l"), axis=0, tiled=True)
+    height = (lax.axis_index("r") * 2 + lax.axis_index("l")).astype(jnp.int32).reshape(1)
     before = call(
         spread_kernel,
         shape((4, 144, LANES)),
-        bases,
+        height,
+        totals,
         quarters,
-        scratch=[pltpu.VMEM((144, LANES), F32)],
+        spaces=([pltpu.SMEM, pltpu.VMEM, pltpu.VMEM], pltpu.VMEM),
         name="spread",
     )
-    before, down_one = lax.optimization_barrier((before, down_one))
+    before, down_one, queries, w_up = lax.optimization_barrier((before, down_one, queries, w_up))
     before = lax.all_to_all(before, "y", 0, 0, tiled=True)
     down_one = lax.ppermute(down_one, "l", [(0, 1), (1, 0)])
-    before, down_one, down_two = lax.optimization_barrier((before, down_one, down_two))
+    inner = call(
+        inner_kernel,
+        shape((length, width), F32),
+        in_hbm(queries),
+        in_hbm(keys),
+        in_hbm(values),
+        name="inner",
+    )
+    up_cut = call(
+        cut_up_kernel,
+        shape((4, units, quarter)),
+        w_up[0],
+        scratch=[pltpu.SemaphoreType.DMA((4,))],
+        spaces=([HBM], HBM),
+        name="cut_up",
+    )
+    before, down_one, down_two, inner, up_cut = lax.optimization_barrier(
+        (before, down_one, down_two, inner, up_cut)
+    )
     attn, pay = call(
         attn_kernel,
         (pltpu.HBM((length, width), BF16), shape((32, SLOTS, LANES))),

time: 224 us -> 220 us (0.982)
  blocking collectives: 75.9 us -> 96.7 us
  waiting for transfers between devices: 49.4 us -> 30.5 us
  starting transfers between devices: 73.6 us -> 67.1 us
    all_gather x0 -> x1, blocking collectives: none -> 32.5 us  [body(): totals = lax.all_gather(totals, ('r', 'l'), axis=0, tiled=True)]
    all_to_all x2 -> x1, waiting for transfers between devices: 16.2 us -> 1.37 us  [body(): quarters = lax.all_to_all(state, 'y', 0, 0, tiled=True)]
    all_to_all x2 -> x1, starting transfers between devices: 18.4 us -> 5.01 us  [body(): quarters = lax.all_to_all(state, 'y', 0, 0, tiled=True)]
    all_to_all x1 -> x0, blocking collectives: 9.73 us -> none  [body(): quarters = lax.all_to_all(state, 'y', 0, 0, tiled=True)]
    all_to_all x1, starting transfers between devices: 11.4 us -> 15.8 us  [body(): whole_rows = lax.all_to_all(pay, ('y', 'p'), 0, 0, tiled=True)]
    all_to_all x1, waiting for transfers between devices: 4.79 us -> 0.7 us  [body(): before = lax.all_to_all(before, 'y', 0, 0, tiled=True)]
    pallas_call x16 -> x15, Pallas kernels: 18.7 us -> 18.1 us  [call(): pl.pallas_call(kernel, out_shape=out, scratch_shapes=list(scratch), compi...]
  transfers between devices with their start and end apart: 11 -> 10, of which waited for: 7 -> 6; matrix products, arithmetic and copies ran while one was open for 0% -> 0% of each run, Pallas kernels for 3% -> 3%
where the time goes in v12:
time: 220 us; the launch traced here: 219 us
  blocking collectives  96.7 us (44%)
  starting transfers between devices  67.1 us (30%)
  waiting for transfers between devices  30.5 us (14%)
  Pallas kernels  18.1 us (8%)
  local copies, waits for them, and re-layouts  5.98 us (3%)
    all_gather x1, blocking collectives, body(): totals = lax.all_gather(totals, ('r', 'l'), axis=0, tiled=True)  32.5 us
    all_gather x1, blocking collectives, body(): arrived = lax.all_gather(near_rows, ('r', 'l'), axis=0, tiled=True)  26.5 us
    all_gather x1, blocking collectives, body(): act = lax.all_gather(act, 'r', axis=0, tiled=True)  26.2 us
    all_to_all x1, starting transfers between devices, body(): weighted = lax.all_to_all(weighted, 'p', 0, 0, tiled=True)  19.5 us
    pallas_call x15, Pallas kernels, call(): pl.pallas_call(kernel, out_shape=out, scratch_shapes=list(scratch), compi...  18.1 us
    all_to_all x1, starting transfers between devices, body(): whole_rows = lax.all_to_all(pay, ('y', 'p'), 0, 0, tiled=True)  15.8 us
    all_to_all x1, waiting for transfers between devices, body(): back = lax.all_to_all(back, ('r', 'l'), 0, 0, tiled=True)  11.7 us
    all_to_all x1, blocking collectives, body(): back = lax.all_to_all(out, 'y', 0, 0, tiled=True)  11.5 us
  transfers between devices with their start and end apart: 10, of which 6 were waited for; matrix products, arithmetic and copies ran while one was open for 0% of the time, Pallas kernels for 3%

profile of v12, /device:TPU:1, one launch (start us, length us, event | category | flops | bytes accessed | tf_op | source)
XLA Modules:
  0.0 218.7 jit_solution(16559691572644308275)
XLA Ops:
  0.0 2.3 %state.1 = bf16[4,144,128]{2,1,0:T(8,128)(2,1)} custom-call(bf16[256,768]{1,0:T(8,128)(2,1)} %k_ref.3, bf16[256,768]{1,0:T(8,128)(2,1)} %v_ref.3), custom_call_target="tpu_custom_call" | custom-call | tf_op jit(solution)/shard_map/state/pallas_call | solution.py:29
  2.3 5.0 %all-to-all-start = ((bf16[4,144,128]{2,1,0:T(8,128)(2,1)}), bf16[4,144,128]{2,1,0:T(8,128)(2,1)S(1)}, u32[]{:S(2)}, u32[]{:S(2)}) async-start(bf16[4,144,128]{2,1,0:T(8,128)(2,1)} %state.1), calls=%async_computation | async-start | bytes 294912 | tf_op jit(solution)/shard_map/all_to_all | solution.py:302
  7.3 1.5 copy-done.1
  8.8 2.1 cut_down.1
  10.8 1.4 all-to-all-done.in_ref
  12.2 0.0 copy-start
  12.2 32.5 %all_gather.9.all_ref = bf16[2304,128]{1,0:T(8,128)(2,1)S(1)} all-gather(bf16[144,128]{1,0:T(8,128)(2,1)S(1)} %total.1), channel_id=1, replica_groups=mesh['r'=8,'l'=2,'y'=4,'p'=8] {'r','l'}, dimensions={0}, use_global_device_ids=true | all-gather | bytes 626688 | tf_op jit(solution)/shard_map/all_gather | solution.py:317
  44.8 0.8 spread.1
  45.6 1.9 collective-permute-start
  47.5 3.3 %all-to-all-start.1 = ((bf16[4,144,128]{2,1,0:T(8,128)(2,1)}), bf16[4,144,128]{2,1,0:T(8,128)(2,1)S(1)}, u32[]{:S(2)}, u32[]{:S(2)}) async-start(bf16[4,144,128]{2,1,0:T(8,128)(2,1)} %spread.1), calls=%async_computation.1 | async-start | bytes 294912 | tf_op jit(solution)/shard_map/all_to_all | solution.py:329
  50.9 0.7 broadcast_in_dim_reshape.4.sel_ref
  51.5 2.2 inner.1.inner_ref
  53.7 0.0 copy-start.2
  53.7 1.3 cut_up.1
  55.0 0.7 all-to-all-done.1.p_ref
  55.7 0.0 collective-permute-done.one_ref
  55.7 0.7 copy-done.7
  56.5 1.8 attn.1
  58.2 3.4 %collective-permute-start.1 = (bf16[2,96,1152]{2,1,0:T(8,128)(2,1)}, bf16[2,96,1152]{2,1,0:T(8,128)(2,1)S(1)}, u32[]{:S(2)}, u32[]{:S(2)}) collective-permute-start(bf16[2,96,1152]{2,1,0:T(8,128)(2,1)} %get-tuple-element.55), channel_id=1, source_target_pairs={{0,32},{32,0},{1,33},{33,1},{2,34},{34,2},{3,35},{35,3},{4,36},{36... | collective-permute-start | bytes 1327112 | tf_op jit(solution)/shard_map/ppermute | solution.py:366
  61.6 15.8 %all-to-all-start.2 = ((bf16[32,32,128]{2,1,0:T(8,128)(2,1)}), bf16[32,32,128]{2,1,0:T(8,128)(2,1)S(1)}, u32[]{:S(2)}, u32[]{:S(2)}) async-start(bf16[32,32,128]{2,1,0:T(8,128)(2,1)} %get-tuple-element.54), calls=%async_computation.2 | async-start | bytes 524288 | tf_op jit(solution)/shard_map/all_to_all | solution.py:367
  77.4 8.9 %all-to-all-done.2.row_ref = bf16[32,32,128]{2,1,0:T(8,128)(2,1)S(1)} async-done(((bf16[32,32,128]{2,1,0:T(8,128)(2,1)}), bf16[32,32,128]{2,1,0:T(8,128)(2,1)S(1)}, u32[]{:S(2)}, u32[]{:S(2)}) %all-to-all-start.2) | async-done | bytes 262176 | tf_op jit(solution)/shard_map/all_to_all | solution.py:367
  86.2 0.0 collective-permute-done.1.two_ref
  86.3 0.8 copy-done.4
  87.0 3.6 %all-to-all-start.3 = ((bf16[4,144,1536]{2,1,0:T(8,128)(2,1)}), bf16[4,144,1536]{2,1,0:T(8,128)(2,1)S(1)}, u32[]{:S(2)}, u32[]{:S(2)}) async-start(bf16[4,144,1536]{2,1,0:T(8,128)(2,1)} %cut_up.1), calls=%async_computation.3 | async-start | bytes 3538944 | tf_op jit(solution)/shard_map/all_to_all | solution.py:379
  90.6 26.5 %all_gather.10.x_ref = bf16[3840,128]{1,0:T(8,128)(2,1)S(1)} all-gather(bf16[240,128]{1,0:T(8,128)(2,1)S(1)} %near.1), channel_id=1, replica_groups=mesh['r'=8,'l'=2,'y'=4,'p'=8] {'r','l'}, dimensions={0}, use_global_device_ids=true | all-gather | bytes 1044480 | tf_op jit(solution)/shard_map/all_gather | solution.py:380
  117.1 0.0 all-to-all-done.3
  117.1 2.1 up.1
  119.2 3.9 %all-to-all-start.4 = ((bf16[4,144,384]{2,1,0:T(8,128)(2,1)}), bf16[4,144,384]{2,1,0:T(8,128)(2,1)S(1)}, u32[]{:S(2)}, u32[]{:S(2)}) async-start(bf16[4,144,384]{2,1,0:T(8,128)(2,1)} %bitcast.9), calls=%async_computation.4 | async-start | bytes 884736 | tf_op jit(solution)/shard_map/all_to_all | solution.py:390
  123.1 1.2 copy-done.3
  124.2 1.0 copy-done.5
  125.3 1.4 join.1
  126.6 2.9 %all-to-all-done.4.in_ref = bf16[4,144,384]{2,1,0:T(8,128)(2,1)S(1)} async-done(((bf16[4,144,384]{2,1,0:T(8,128)(2,1)}), bf16[4,144,384]{2,1,0:T(8,128)(2,1)S(1)}, u32[]{:S(2)}, u32[]{:S(2)}) %all-to-all-start.4) | async-done | bytes 442400 | tf_op jit(solution)/shard_map/all_to_all | solution.py:390
  129.6 0.1 act.1
  129.7 3.6 %all-to-all-start.5 = ((bf16[4,2,96,1152]{3,2,1,0:T(8,128)(2,1)}), bf16[4,2,96,1152]{3,2,1,0:T(8,128)(2,1)S(1)}, u32[]{:S(2)}, u32[]{:S(2)}) async-start(bf16[4,2,96,1152]{3,2,1,0:T(8,128)(2,1)} %join.1), calls=%async_computation.5 | async-start | bytes 3538944 | tf_op jit(solution)/shard_map/all_to_all | solution.py:404
  133.3 26.2 %all_gather.11.h_ref = bf16[1152,384]{1,0:T(8,128)(2,1)S(1)} all-gather(bf16[144,384]{1,0:T(8,128)(2,1)S(1)} %act.1), channel_id=1, replica_groups=mesh['r'=8,'l'=2,'y'=4,'p'=8] {'r'}, dimensions={0}, use_global_device_ids=true | all-gather | bytes 995328 | tf_op jit(solution)/shard_map/all_gather | solution.py:405
  159.5 1.5 down.1
  161.0 0.0 copy-start.8
  161.0 0.0 copy-start.6
  161.0 11.5 %all_to_all.45.in_ref = bf16[64,32,128]{2,1,0:T(8,128)(2,1)S(1)} all-to-all(bf16[64,32,128]{2,1,0:T(8,128)(2,1)S(1)} %down.1), channel_id=1, replica_groups=mesh['r'=8,'l'=2,'y'=4,'p'=8] {'y'}, dimensions={0} | all-to-all | bytes 1048576 | tf_op jit(solution)/shard_map/all_to_all | solution.py:417
  172.6 0.7 sum.1
  173.3 7.2 %all-to-all-start.7 = ((bf16[16,32,128]{2,1,0:T(8,128)(2,1)}), bf16[16,32,128]{2,1,0:T(8,128)(2,1)S(1)}, u32[]{:S(2)}, u32[]{:S(2)}) async-start(bf16[16,32,128]{2,1,0:T(8,128)(2,1)} %sum.1), calls=%async_computation.7 | async-start | bytes 262144 | tf_op jit(solution)/shard_map/all_to_all | solution.py:419
  180.5 0.1 reshape.28
  180.6 0.1 reduce
  180.7 11.7 %all-to-all-done.7.y_ref = bf16[16,32,128]{2,1,0:T(8,128)(2,1)S(1)} async-done(((bf16[16,32,128]{2,1,0:T(8,128)(2,1)}), bf16[16,32,128]{2,1,0:T(8,128)(2,1)S(1)}, u32[]{:S(2)}, u32[]{:S(2)}) %all-to-all-start.7) | async-done | bytes 131104 | tf_op jit(solution)/shard_map/all_to_all | solution.py:419
  192.5 0.9 weigh.1
  193.3 19.5 %all-to-all-start.8 = ((bf16[8,32,128]{2,1,0:T(8,128)(2,1)}), bf16[8,32,128]{2,1,0:T(8,128)(2,1)S(1)}, u32[]{:S(2)}, u32[]{:S(2)}) async-start(bf16[8,32,128]{2,1,0:T(8,128)(2,1)} %weigh.1), calls=%async_computation.8 | async-start | bytes 131072 | tf_op jit(solution)/shard_map/all_to_all | solution.py:430
  212.8 4.9 %all-to-all-done.8.y_ref = bf16[8,32,128]{2,1,0:T(8,128)(2,1)S(1)} async-done(((bf16[8,32,128]{2,1,0:T(8,128)(2,1)}), bf16[8,32,128]{2,1,0:T(8,128)(2,1)S(1)}, u32[]{:S(2)}, u32[]{:S(2)}) %all-to-all-start.8) | async-done | bytes 65568 | tf_op jit(solution)/shard_map/all_to_all | solution.py:430
  217.7 1.0 add.10
  (21 shorter events, 0.1 us)
Async XLA Ops:
  2.3 9.9 %all-to-all-start = ((bf16[4,144,128]{2,1,0:T(8,128)(2,1)}), bf16[4,144,128]{2,1,0:T(8,128)(2,1)S(1)}, u32[]{:S(2)}, u32[]{:S(2)}) async-start(bf16[4,144,128]{2,1,0:T(8,128)(2,1)} %state.1), calls=%async_computation | async-start | bytes 294912 | tf_op jit(solution)/shard_map/all_to_all | solution.py:302
  7.3 1.5 copy-start.1
  8.8 42.1 %copy-start.9 = (s32[1,8,5]{1,0,2:T(1,128)S(1)}, s32[1,8,5]{1,0,2:T(1,128)}, u32[]{:S(2)}) copy-start(s32[1,8,5]{1,0,2:T(1,128)} %param.10) | copy-start | bytes 484
  12.2 41.5 %copy-start = (bf16[1,144,6144]{2,1,0:T(8,128)(2,1)S(1)}, bf16[1,144,6144]{2,1,0:T(8,128)(2,1)}, u32[]{:S(2)}) copy-start(bf16[1,144,6144]{2,1,0:T(8,128)(2,1)} %param.12) | copy-start | bytes 5308420
  45.6 10.2 %collective-permute-start = (bf16[2,96,1152]{2,1,0:T(8,128)(2,1)}, bf16[2,96,1152]{2,1,0:T(8,128)(2,1)S(1)}, u32[]{:S(2)}, u32[]{:S(2)}) collective-permute-start(bf16[2,96,1152]{2,1,0:T(8,128)(2,1)} %get-tuple-element.46), channel_id=1, source_target_pairs={{0,32},{32,0},{1,33},{33,1},{2,34},{34,2},{3,35},{35,3},{4,36},{36... | collective-permute-start | bytes 1327112 | tf_op jit(solution)/shard_map/ppermute | solution.py:330
  47.5 8.2 %all-to-all-start.1 = ((bf16[4,144,128]{2,1,0:T(8,128)(2,1)}), bf16[4,144,128]{2,1,0:T(8,128)(2,1)S(1)}, u32[]{:S(2)}, u32[]{:S(2)}) async-start(bf16[4,144,128]{2,1,0:T(8,128)(2,1)} %spread.1), calls=%async_computation.1 | async-start | bytes 294912 | tf_op jit(solution)/shard_map/all_to_all | solution.py:329
  53.7 2.0 copy-start.2
  55.7 0.7 copy-start.7
  58.2 28.0 %collective-permute-start.1 = (bf16[2,96,1152]{2,1,0:T(8,128)(2,1)}, bf16[2,96,1152]{2,1,0:T(8,128)(2,1)S(1)}, u32[]{:S(2)}, u32[]{:S(2)}) collective-permute-start(bf16[2,96,1152]{2,1,0:T(8,128)(2,1)} %get-tuple-element.55), channel_id=1, source_target_pairs={{0,32},{32,0},{1,33},{33,1},{2,34},{34,2},{3,35},{35,3},{4,36},{36... | collective-permute-start | bytes 1327112 | tf_op jit(solution)/shard_map/ppermute | solution.py:366
  61.6 24.7 %all-to-all-start.2 = ((bf16[32,32,128]{2,1,0:T(8,128)(2,1)}), bf16[32,32,128]{2,1,0:T(8,128)(2,1)S(1)}, u32[]{:S(2)}, u32[]{:S(2)}) async-start(bf16[32,32,128]{2,1,0:T(8,128)(2,1)} %get-tuple-element.54), calls=%async_computation.2 | async-start | bytes 524288 | tf_op jit(solution)/shard_map/all_to_all | solution.py:367
  86.3 0.8 copy-start.4
  87.0 30.1 %all-to-all-start.3 = ((bf16[4,144,1536]{2,1,0:T(8,128)(2,1)}), bf16[4,144,1536]{2,1,0:T(8,128)(2,1)S(1)}, u32[]{:S(2)}, u32[]{:S(2)}) async-start(bf16[4,144,1536]{2,1,0:T(8,128)(2,1)} %cut_up.1), calls=%async_computation.3 | async-start | bytes 3538944 | tf_op jit(solution)/shard_map/all_to_all | solution.py:379
  119.2 10.4 %all-to-all-start.4 = ((bf16[4,144,384]{2,1,0:T(8,128)(2,1)}), bf16[4,144,384]{2,1,0:T(8,128)(2,1)S(1)}, u32[]{:S(2)}, u32[]{:S(2)}) async-start(bf16[4,144,384]{2,1,0:T(8,128)(2,1)} %bitcast.9), calls=%async_computation.4 | async-start | bytes 884736 | tf_op jit(solution)/shard_map/all_to_all | solution.py:390
  123.1 1.2 copy-start.3
  124.2 1.0 copy-start.5
  129.7 29.8 %all-to-all-start.5 = ((bf16[4,2,96,1152]{3,2,1,0:T(8,128)(2,1)}), bf16[4,2,96,1152]{3,2,1,0:T(8,128)(2,1)S(1)}, u32[]{:S(2)}, u32[]{:S(2)}) async-start(bf16[4,2,96,1152]{3,2,1,0:T(8,128)(2,1)} %join.1), calls=%async_computation.5 | async-start | bytes 3538944 | tf_op jit(solution)/shard_map/all_to_all | solution.py:404
  161.0 19.6 %copy-start.8 = (bf16[6144,1]{0,1:T(2,128)(2,1)S(1)}, bf16[6144,1]{0,1:T(2,128)(2,1)}, u32[]{:S(2)}) copy-start(bf16[6144,1]{0,1:T(2,128)(2,1)} %param.11) | copy-start | bytes 36868
  161.0 56.7 %copy-start.6 = (bf16[256,768]{1,0:T(8,128)(2,1)S(1)}, bf16[256,768]{1,0:T(8,128)(2,1)}, u32[]{:S(2)}) copy-start(bf16[256,768]{1,0:T(8,128)(2,1)} %get-tuple-element.51.attn_ref) | copy-start | bytes 1179652
  173.3 19.2 %all-to-all-start.7 = ((bf16[16,32,128]{2,1,0:T(8,128)(2,1)}), bf16[16,32,128]{2,1,0:T(8,128)(2,1)S(1)}, u32[]{:S(2)}, u32[]{:S(2)}) async-start(bf16[16,32,128]{2,1,0:T(8,128)(2,1)} %sum.1), calls=%async_computation.7 | async-start | bytes 262144 | tf_op jit(solution)/shard_map/all_to_all | solution.py:419
  193.3 24.3 %all-to-all-start.8 = ((bf16[8,32,128]{2,1,0:T(8,128)(2,1)}), bf16[8,32,128]{2,1,0:T(8,128)(2,1)S(1)}, u32[]{:S(2)}, u32[]{:S(2)}) async-start(bf16[8,32,128]{2,1,0:T(8,128)(2,1)} %weigh.1), calls=%async_computation.8 | async-start | bytes 131072 | tf_op jit(solution)/shard_map/all_to_all | solution.py:430
